TPU v7x, 32 devices: a whole 2x2x4 slice. The times are simulated.
32 devices in a mesh: grp: 2 (over y), gx: 4 (over z), gy: 2 (over x), gz: 2 (over core).
Axes of the slice: x: 2, y: 2, z: 4, core: 2. Of those that a mesh axis runs over, the one named last changes fastest.
Arguments:
- snapshot: bfloat16 [2048, 4, 16, 1024], P(('grp', 'gx'), None, 'gz', 'gy'), parts along dimension 0, may hold values from -16 to 16
- x_basis: bfloat16 [2048, 128], P('grp'), parts along dimension 0, may hold values from -0.1875 to 0.1875
- y_basis: bfloat16 [2048, 128], P('grp'), parts along dimension 0, may hold values from -0.1875 to 0.1875
Outputs:
- gram_out: float32 [2048, 1024], P(('grp', 'gx'), ('gy', 'gz')), parts along dimension 0
- core_out: float32 [256, 4, 16, 128], P(('grp', 'gx', 'gy'), None, 'gz'), parts along dimension 0
There are 2 independent parts, one for each index of `grp`. A program takes and returns all parts, laid end to end along the dimension named above; each array names one. Nothing has to cross between parts.
All inputs are finite; a program needn't handle non-finite values.
Results may differ from a plain program's by a relative error of at most 0.0029.
Values may be sent and summed in bfloat16 or wider, within the bound.
No kernel may reach another device: no remote copies, remote signals or barrier semaphores. Data moves between devices by JAX's collectives and lax.ppermute only.
A program may use at most 128 MiB of HBM per device.

v0:
```python
import jax
import jax.numpy as jnp
from jax import lax
from jax.sharding import PartitionSpec as P


def on_device(snapshot, x_basis, y_basis):
    rows_local = snapshot.shape[0]
    columns = snapshot.shape[1] * snapshot.shape[2] * snapshot.shape[3]
    unfolded = snapshot.reshape(rows_local, columns)
    rank_count = x_basis.shape[1]
    across = lax.axis_size("gx")
    rank_rows = rank_count // across
    groups = lax.axis_size("gy") * lax.axis_size("gz")
    inverse = 1.0 / (columns * groups)
    basis_cols = lax.dynamic_slice_in_dim(x_basis, lax.axis_index("gx") * rank_rows, rank_rows, 1)
    shard_rows = lax.all_gather(unfolded, "gx", axis=0, tiled=True)
    gram_block = lax.dot_general(
        unfolded, shard_rows, (((1,), (1,)), ((), ())), preferred_element_type=jnp.float32
    )
    gram_rows = gram_block
    partial_value = lax.dot_general(
        basis_cols, shard_rows, (((0,), (0,)), ((), ())), preferred_element_type=jnp.float32
    )
    gram_rows, partial_value = (gram_rows, partial_value)
    gram_out = lax.psum_scatter(gram_rows * inverse, ("gy", "gz"), scatter_dimension=1, tiled=True)
    own_rows = partial_value.astype(jnp.bfloat16)
    shaped = own_rows.reshape(rank_rows, snapshot.shape[1], snapshot.shape[2], snapshot.shape[3])
    along_y = lax.all_to_all(shaped, "gy", split_axis=0, concat_axis=3, tiled=True)
    core_flat = jnp.dot(
        along_y.reshape(-1, along_y.shape[3]), y_basis, preferred_element_type=jnp.float32
    )
    core_block = core_flat.reshape(
        along_y.shape[0], along_y.shape[1], along_y.shape[2], y_basis.shape[1]
    )
    return (gram_out, core_block)


def solution(mesh):
    in_specs = (P(("grp", "gx"), None, "gz", "gy"), P("grp", None), P("grp", None))
    out_specs = (P(("grp", "gx"), ("gy", "gz")), P(("grp", "gx", "gy"), None, "gz", None))
    return jax.shard_map(
        on_device, mesh=mesh, in_specs=in_specs, out_specs=out_specs, check_vma=False
    )
```

profile of v0, /device:TPU:0, one launch (start us, length us, event | category | flops | bytes accessed | tf_op | source)
XLA Modules:
  0.0 646.1 jit_solution(14155558887606311559)
XLA Ops:
  7.2 0.0 copy-start
  7.2 0.0 all-gather.2.cloned.1.call-start
  7.2 15.4 %copy.7 = bf16[32,8,32,512]{3,1,2,0:T(8,128)(2,1)} copy(bf16[32,8,32,512]{3,2,1,0:T(8,128)(2,1)} %bitcast.21) | data formatting | bytes 16777216
  22.6 0.0 all-gather.2.cloned.1.call-update
  22.6 0.2 reduce-scatter.2.cloned.1.call-start
  22.9 564.0 %all-gather.2.cloned.1.call-done = bf16[1024,16384]{1,0:T(8,128)(2,1)} async-done(((bf16[256,16384]{1,0:T(8,128)(2,1)}), bf16[1024,16384]{1,0:T(8,128)(2,1)}) %all-gather.2.cloned.1.call-update) | async-done | bytes 33554448 | tf_op jit(solution)/shard_map/all_gather | solution.py:17
  586.9 17.6 %convolution_multiply_fusion = f32[256,1024]{1,0:T(8,128)} fusion(bf16[256,16384]{1,0:T(8,128)(2,1)} %bitcast.20, bf16[1024,16384]{1,0:T(8,128)(2,1)} %all-gather.2.cloned.1.call-done), kind=kOutput, calls=%fused_computation.1 | convolution fusion | flops 8590196736 | bytes 42991616 | tf_op jit(solution)/shard_map/dot_general | solution.py:18
  604.5 0.0 copy-start.1
  604.5 0.0 reduce-scatter.2.cloned.1.call-update
  604.5 0.0 copy-done
  604.5 14.4 %convolution_convert_fusion = bf16[32,16384]{1,0:T(8,128)(2,1)S(1)} fusion(bf16[1024,16384]{1,0:T(8,128)(2,1)} %all-gather.2.cloned.1.call-done, bf16[1024,128]{1,0:T(8,128)(2,1)S(1)} %copy-done, s32[]{:T(128)S(6)} %select_n.3), kind=kOutput, calls=%fused_computation | convolution fusion | flops 1074266112 | bytes 34865156 | tf_op jit(solution)/shard_map/dot_general | solution.py:22
  618.9 0.3 copy.8
  619.2 18.8 %all_to_all.15 = bf16[32,4,8,512]{3,2,1,0:T(8,128)(2,1)S(1)} all-to-all(bf16[32,4,8,512]{3,2,1,0:T(8,128)(2,1)S(1)} %bitcast.23), channel_id=1, replica_groups=mesh['grp'=2,'gx'=4,'gy'=2,'gz'=2] {'gy'}, dimensions={0} | all-to-all | bytes 2097152 | tf_op jit(solution)/shard_map/all_to_all | solution.py:29
  638.0 0.1 copy.5
  638.1 0.0 copy-done.1
  638.1 1.1 fusion
  639.2 0.0 reduce-scatter.2.cloned.1.call-done
Async XLA Ops:
  7.2 597.3 %copy-start = (bf16[1024,128]{1,0:T(8,128)(2,1)S(1)}, bf16[1024,128]{1,0:T(8,128)(2,1)}, u32[]{:S(2)}) copy-start(bf16[1024,128]{1,0:T(8,128)(2,1)} %param.4) | copy-start | bytes 786436
  7.2 579.7 %all-gather.2.cloned.1.call-start = ((), (), s32[]{:S(2)}) async-start(), calls=%async_computation.2 | async-start | bytes 41943040 | tf_op jit(solution)/shard_map/all_gather | solution.py:17
  22.6 616.6 %reduce-scatter.2.cloned.1.call-start = ((), (), s32[]{:S(2)}) async-start(), calls=%async_computation.3 | async-start | bytes 1310720 | tf_op jit(solution)/shard_map/reduce_scatter | solution.py:26
  604.5 33.6 %copy-start.1 = (bf16[1024,128]{1,0:T(8,128)(2,1)S(1)}, bf16[1024,128]{1,0:T(8,128)(2,1)}, u32[]{:S(2)}) copy-start(bf16[1024,128]{1,0:T(8,128)(2,1)} %param.5) | copy-start | bytes 786436
Sparse Core Ops, SparseCore 0:
  22.7 564.0 all-gather.1
  604.6 25.1 reduce-scatter.1
where the time goes:
time: 646 us
  waiting for transfers between devices  564 us (87%)
  matrix products  33.1 us (5%)
  blocking collectives  18.8 us (3%)
  local copies, waits for them, and re-layouts  15.8 us (2%)
  between operations  14.1 us (2%)
    all_gather x1, waiting for transfers between devices, on_device(): shard_rows = lax.all_gather(unfolded, 'gx', axis=0, tiled=True)  564 us
    all_to_all x1, blocking collectives, on_device(): lax.all_to_all(shaped, 'gy', split_axis=0, concat_axis=3, tiled=True)  18.8 us
    dot_general x1, matrix products, on_device(): lax.dot_general(unfolded, shard_rows, (((1,), (1,)), ((), ())), preferred...  17.6 us
    unnamed x6, local copies, waits for them, and re-layouts  15.7 us
    dot_general x1, matrix products, on_device(): lax.dot_general(basis_cols, shard_rows, (((0,), (0,)), ((), ())), preferr...  14.4 us
  transfers between devices with their start and end apart: 2, of which 1 were waited for; matrix products, arithmetic and copies ran while one was open for 2% of the time, Pallas kernels for 0%

commit v1 on v0

v1 whole, which is shorter than its diff:
```python
import jax
import jax.numpy as jnp
from jax import lax
from jax.sharding import PartitionSpec as P

F32 = jnp.float32
BF16 = jnp.bfloat16
NEAR = [(0, 1), (3, 2)]
CROSS = [(1, 2), (2, 1)]
FAR = [(0, 2), (3, 1)]
NEAR_BACK = [(1, 0), (2, 3)]
FAR_BACK = [(1, 3), (2, 0)]
SWAP = [(0, 1), (1, 0)]


def gathered(snapshot, x_basis, y_basis):
    rows_local = snapshot.shape[0]
    columns = snapshot.shape[1] * snapshot.shape[2] * snapshot.shape[3]
    unfolded = snapshot.reshape(rows_local, columns)
    rank_count = x_basis.shape[1]
    rank_rows = rank_count // lax.axis_size("gx")
    inverse = 1.0 / (columns * lax.axis_size("gy") * lax.axis_size("gz"))
    basis_cols = lax.dynamic_slice_in_dim(x_basis, lax.axis_index("gx") * rank_rows, rank_rows, 1)
    shard_rows = lax.all_gather(unfolded, "gx", axis=0, tiled=True)
    gram_rows = nt(unfolded, shard_rows)
    own_rows = tn(basis_cols, shard_rows).astype(BF16)
    gram_out = lax.psum_scatter(gram_rows * inverse, ("gy", "gz"), scatter_dimension=1, tiled=True)
    shaped = own_rows.reshape(rank_rows, *snapshot.shape[1:])
    along_y = lax.all_to_all(shaped, "gy", split_axis=0, concat_axis=3, tiled=True)
    core_flat = jnp.dot(along_y.reshape(-1, along_y.shape[3]), y_basis, preferred_element_type=F32)
    return gram_out, core_flat.reshape(*along_y.shape[:3], y_basis.shape[1])


def nt(a, b):
    return lax.dot_general(a, b, (((1,), (1,)), ((), ())), preferred_element_type=F32)


def tn(a, b):
    return lax.dot_general(a, b, (((0,), (0,)), ((), ())), preferred_element_type=F32)


def meeting(snapshot, x_basis, y_basis):
    rows, ncomp, nz, ny = snapshot.shape
    rank = x_basis.shape[1]
    gx, gy, gz = lax.axis_index("gx"), lax.axis_index("gy"), lax.axis_index("gz")
    side = gx // 2
    inner = (gx == 1) | (gx == 2)
    half = ncomp // 2
    width = nz * ny
    inverse = 1.0 / (ncomp * width * lax.axis_size("gy") * lax.axis_size("gz"))

    def take(start):
        return lax.dynamic_slice_in_dim(snapshot, start, 1, 1).reshape(rows, nz, ny)

    own_raw = [take((1 - side) * half + h) for h in range(half)]
    oth_raw = [take(side * half + h) for h in range(half)]
    near_raw, cross_raw = [], []
    for h in range(half):
        near_raw.append(lax.ppermute(own_raw[h], "gx", NEAR))
        cross_raw.append(lax.ppermute(oth_raw[h], "gx", CROSS))

    def flat(a):
        return a.reshape(rows, width)

    oth = [flat(a) for a in oth_raw]
    own = [flat(a) for a in own_raw]
    cuts = [(0, 0, 8), (1, 0, 6), (1, 6, 8)]
    far = []
    for h, lo, hi in cuts:
        far.append(lax.ppermute(oth[h][:, lo * ny : hi * ny], "gx", FAR))
    near = [flat(a) for a in near_raw]
    cross = [flat(a) for a in cross_raw]

    n_at = jnp.where(side == 0, 0, 3)
    c_at = jnp.where(side == 0, 2, 1)
    f_at = jnp.where(side == 0, 3, 0)

    def basis(at):
        return lax.dynamic_slice_in_dim(x_basis, at * rows, rows, 0)

    b_n, b_s, b_c, b_f = basis(n_at), basis(gx), basis(c_at), basis(f_at)

    def total(f, *lists):
        return sum(f(*items) for items in zip(*lists))

    diag = total(lambda a: nt(a, a), own) + total(lambda a: nt(a, a), oth)
    ns = total(nt, near, own)
    sn = total(nt, own, near)
    nc_ = total(nt, near, cross)
    cn = total(nt, cross, near)
    sc = total(nt, own, cross)
    cs = total(nt, cross, own)
    zero = jnp.zeros_like(diag)
    row_n = [zero, ns, nc_, zero]
    row_s = [sn + jnp.where(inner, zero, diag), jnp.where(inner, diag, zero), sc, zero]
    row_c = [cn, cs, zero, zero]

    def placed(blocks):
        return jnp.concatenate(
            [jnp.where(side == 0, blocks[k], blocks[3 - k]) for k in range(4)], 1
        )

    early = jnp.concatenate([placed(row_n), placed(row_s), placed(row_c)], 0)
    early = lax.psum_scatter(early, ("gy", "gz"), scatter_dimension=1, tiled=True)
    gram = (
        early[rows : 2 * rows]
        + lax.ppermute(early[:rows], "gx", NEAR_BACK)
        + lax.ppermute(early[2 * rows :], "gx", CROSS)
    )

    part = [
        tn(b_n, near[h]) + tn(b_s, own[h]) + tn(b_c, cross[h]) for h in range(half)
    ]
    y_own = lax.dynamic_slice_in_dim(y_basis, gy * ny, ny, 0)
    own_out, oth_out = [], []
    fs, fc, fn = zero, zero, zero
    for (h, lo, hi), f in zip(cuts, far):
        span = slice(lo * ny, hi * ny)
        fn = fn + nt(f, near[h][:, span])
        fs = fs + nt(f, own[h][:, span])
        fc = fc + nt(f, cross[h][:, span])
        projected = (part[h][:, span] + tn(b_f, f)).astype(BF16)
        cz = hi - lo
        core = jnp.dot(projected.reshape(rank * cz, ny), y_own, preferred_element_type=F32)
        core = core.reshape(4, 2, rank // 8, cz, -1)
        keep = lax.dynamic_index_in_dim(core, gy, 1, False)
        give = lax.dynamic_index_in_dim(core, 1 - gy, 1, False)
        summed = keep + lax.ppermute(give, "gy", SWAP)

        def block(at):
            return lax.dynamic_index_in_dim(summed, at, 0, False)

        own_out.append(
            lax.ppermute(block(n_at), "gx", NEAR_BACK)
            + jnp.where(inner, block(gx), 0.0)
        )
        oth_out.append(
            lax.ppermute(block(c_at), "gx", CROSS) + lax.ppermute(block(f_at), "gx", FAR_BACK)
        )
    late = placed([fn, fs, fc, zero]).reshape(rows, 2, 2, rows)
    mine = lax.dynamic_index_in_dim(late, gz, 2, False)
    give = lax.dynamic_index_in_dim(late, 1 - gz, 2, False)
    late = mine + lax.ppermute(give, "gz", SWAP)
    mine = lax.dynamic_index_in_dim(late, gy, 1, False)
    give = lax.dynamic_index_in_dim(late, 1 - gy, 1, False)
    late = mine + lax.ppermute(give, "gy", SWAP)
    turn = [(4 + l, 4 * l + 3) for l in (0, 1, 2)] + [(8 + l, 4 * l) for l in (1, 2, 3)]
    gram = (
        gram
        + lax.ppermute(late, "gx", FAR_BACK)
        + lax.ppermute(late, ("gx", "gy", "gz"), turn).T
    )
    own_half = jnp.concatenate(own_out, 1)
    oth_half = jnp.concatenate(oth_out, 1)
    low = jnp.where(side == 0, oth_half, own_half)
    high = jnp.where(side == 0, own_half, oth_half)
    core_out = jnp.concatenate([low, high], 1).reshape(rank // 8, ncomp, nz, -1)
    return gram * inverse, core_out


def solution(mesh):
    in_specs = (P(("grp", "gx"), None, "gz", "gy"), P("grp", None), P("grp", None))
    out_specs = (P(("grp", "gx"), ("gy", "gz")), P(("grp", "gx", "gy"), None, "gz", None))
    sizes = (mesh.shape["gx"], mesh.shape["gy"], mesh.shape["gz"])
    body = meeting if sizes == (4, 2, 2) else gathered
    return jax.shard_map(body, mesh=mesh, in_specs=in_specs, out_specs=out_specs, check_vma=False)
```

time: 646 us -> 306 us (0.47)
  waiting for transfers between devices: 564 us -> 107 us
  starting transfers between devices: 0.26 us -> 43.6 us
  local copies, waits for them, and re-layouts: 15.8 us -> 55.6 us
  matrix products: 33.1 us -> 69.8 us
  blocking collectives: 18.8 us -> 0 us
  other arithmetic: 0 us -> 9.24 us
    all_gather x1 -> x0, waiting for transfers between devices: 564 us -> none  [on_device(): shard_rows = lax.all_gather(unfolded, 'gx', axis=0, tiled=True)]
    ppermute x0 -> x25, waiting for transfers between devices: none -> 107 us  [the longest x2 37.2 us: meeting(): near_raw.append(lax.ppermute(own_raw[h], 'gx', NEAR))]
    ppermute x0 -> x25, starting transfers between devices: none -> 43.5 us  [the longest x3 15.1 us: meeting(): far.append(lax.ppermute(oth[h][:, lo * ny:hi * ny], 'gx', FAR))]
    dot_general x3 -> x37, matrix products: 33.1 us -> 69.8 us  [the longest x25 50.3 us: nt(): lax.dot_general(a, b, (((1,), (1,)), ((), ())), preferred_element_type=F32)]
    all_to_all x1 -> x0, blocking collectives: 18.8 us -> none  [on_device(): lax.all_to_all(shaped, 'gy', split_axis=0, concat_axis=3, tiled=True)]
    ppermute x0 -> x5, local copies, waits for them, and re-layouts: none -> 15.8 us  [the longest x2 7.85 us: meeting(): cross_raw.append(lax.ppermute(oth_raw[h], 'gx', CROSS))]
    dynamic_slice x0 -> x8, local copies, waits for them, and re-layouts: none -> 12.7 us  [the longest x5 12.2 us: take(): return lax.dynamic_slice_in_dim(snapshot, start, 1, 1).reshape(rows, nz, ny)]
    unnamed x6 -> x72, local copies, waits for them, and re-layouts: 15.7 us -> 17.3 us
  transfers between devices with their start and end apart: 2 -> 26, of which waited for: 1 -> 10; matrix products, arithmetic and copies ran while one was open for 2% -> 40% of each run, Pallas kernels for 0% -> 0%
where the time goes in v1:
time: 306 us; the launch traced here: 300 us
  waiting for transfers between devices  107 us (35%)
  matrix products  69.8 us (23%)
  local copies, waits for them, and re-layouts  55.6 us (18%)
  starting transfers between devices  43.6 us (14%)
  between operations  15.2 us (5%)
  other arithmetic  9.24 us (3%)
    dot_general x25, matrix products, nt(): lax.dot_general(a, b, (((1,), (1,)), ((), ())), preferred_element_type=F32)  50.3 us
    ppermute x2, waiting for transfers between devices, meeting(): near_raw.append(lax.ppermute(own_raw[h], 'gx', NEAR))  37.2 us
    ppermute x3, waiting for transfers between devices, meeting(): lax.ppermute(block(n_at), 'gx', NEAR_BACK)  31.3 us
    ppermute x3, waiting for transfers between devices, meeting(): far.append(lax.ppermute(oth[h][:, lo * ny:hi * ny], 'gx', FAR))  18.2 us
    unnamed x72, local copies, waits for them, and re-layouts  17.3 us
    dot_general x9, matrix products, tn(): lax.dot_general(a, b, (((0,), (0,)), ((), ())), preferred_element_type=F32)  16.2 us
    ppermute x3, starting transfers between devices, meeting(): far.append(lax.ppermute(oth[h][:, lo * ny:hi * ny], 'gx', FAR))  15.1 us
    dynamic_slice x5, local copies, waits for them, and re-layouts, take(): return lax.dynamic_slice_in_dim(snapshot, start, 1, 1).reshape(rows, nz, ny)  12.2 us
  transfers between devices with their start and end apart: 26, of which 10 were waited for; matrix products, arithmetic and copies ran while one was open for 40% of the time, Pallas kernels for 0%

profile of v1, /device:TPU:0, one launch (start us, length us, event | category | flops | bytes accessed | tf_op | source)
XLA Modules:
  0.0 300.5 jit_solution(9708820785641870355)
XLA Ops:
  7.3 4.1 %constant_dynamic-slice_fusion.5 = (bf16[256,1,8,512]{3,2,1,0:T(8,128)(2,1)S(1)}, bf16[256,1,8,512]{3,2,1,0:T(8,128)(2,1)S(1)}, bf16[256,1,8,512]{3,2,1,0:T(8,128)(2,1)S(1)}, bf16[256,1,8,512]{3,2,1,0:T(8,128)(2,1)S(1)}) fusion(bf16[256,4,8,512]{3,2,1,0:T(8,128)(2,1)} %param.3, s32[]{:T(128)S(6)} %select_n.210, s32[]{:T(128)S(6)} %select_n.211, ...), kind=kLoop, calls=%fused_computation.141 | loop fusion | bytes 16777232 | tf_op jit(solution)/shard_map/dynamic_slice | solution.py:53
  13.6 6.0 %collective-permute-start.8 = (bf16[256,1024]{1,0:T(8,128)(2,1)}, bf16[256,1024]{1,0:T(8,128)(2,1)S(1)}, u32[]{:S(2)}, u32[]{:S(2)}) collective-permute-start(bf16[256,1024]{1,0:T(8,128)(2,1)} %slice.57), channel_id=1, source_target_pairs={{0,8},{12,4},{1,9},{13,5},{2,10},{14,6},{3,11},{15,7},{16,24},{28,... | collective-permute-start | bytes 1572872 | tf_op jit(solution)/shard_map/ppermute | solution.py:70
  33.5 2.8 collective-permute-start.1
  40.9 4.0 %copy.52 = bf16[32,8,8,512]{3,1,2,0:T(8,128)(2,1)} copy(bf16[32,8,8,512]{3,2,1,0:T(8,128)(2,1)} %bitcast.196) | data formatting | bytes 4194304
  51.6 4.6 %fusion.18 = f32[256,256]{0,1:T(8,128)S(1)} fusion(f32[256,256]{0,1:T(8,128)S(1)} %convolution_bitcast_fusion.2, bf16[256,1,8,512]{3,2,1,0:T(8,128)(2,1)} %copy-done.16), kind=kOutput, calls=%fused_computation.41 | convolution fusion | flops 536936448 | bytes 2621440 | tf_op jit(solution)/shard_map/dot_general | solution.py:35
  66.0 6.7 %collective-permute-start.6 = (bf16[256,4096]{1,0:T(8,128)(2,1)}, bf16[256,4096]{1,0:T(8,128)(2,1)}, u32[]{:S(2)}, u32[]{:S(2)}) collective-permute-start(bf16[256,4096]{1,0:T(8,128)(2,1)} %bitcast.52), channel_id=1, source_target_pairs={{0,8},{12,4},{1,9},{13,5},{2,10},{14,6},{3,11},{15,7},{16,24},{28,... | collective-permute-start | bytes 6291464 | tf_op jit(solution)/shard_map/ppermute | solution.py:70
  75.3 3.9 %copy.38 = bf16[256,8,512]{0,2,1:T(8,128)(2,1)} copy(bf16[256,8,512]{2,0,1:T(8,128)(2,1)} %collective-permute-done.3) | data formatting | bytes 4194304 | tf_op jit(solution)/shard_map/ppermute | solution.py:60
  79.3 31.6 %collective-permute-done.1 = bf16[256,8,512]{2,0,1:T(8,128)(2,1)} collective-permute-done((bf16[256,8,512]{2,0,1:T(8,128)(2,1)}, bf16[256,8,512]{2,0,1:T(8,128)(2,1)}, u32[]{:S(2)}, u32[]{:S(2)}) %collective-permute-start.1) | collective-permute-done | bytes 2097184 | tf_op jit(solution)/shard_map/ppermute | solution.py:59
  110.9 3.9 %copy.34 = bf16[256,8,512]{0,2,1:T(8,128)(2,1)} copy(bf16[256,8,512]{2,0,1:T(8,128)(2,1)} %collective-permute-done.1) | data formatting | bytes 4194304 | tf_op jit(solution)/shard_map/ppermute | solution.py:59
  126.1 3.7 %convolution_bitcast_fusion = f32[256,256]{0,1:T(8,128)} fusion(bf16[256,8,512]{2,0,1:T(8,128)(2,1)} %collective-permute-done.3, bf16[256,8,512]{2,0,1:T(8,128)(2,1)} %collective-permute-done.1), kind=kOutput, calls=%fused_computation.27 | convolution fusion | flops 536870912 | bytes 4456448 | tf_op jit(solution)/shard_map/dot_general | solution.py:35
  132.5 2.7 dot_general.152
  135.3 3.9 %copy.37 = bf16[256,8,512]{0,2,1:T(8,128)(2,1)} copy(bf16[256,8,512]{2,0,1:T(8,128)(2,1)} %collective-permute-done.2) | data formatting | bytes 4194304 | tf_op jit(solution)/shard_map/ppermute | solution.py:60
  139.2 3.8 %convolution_bitcast_fusion.6 = f32[256,256]{0,1:T(8,128)} fusion(bf16[256,8,512]{2,0,1:T(8,128)(2,1)} %collective-permute-done.1, bf16[256,8,512]{2,0,1:T(8,128)(2,1)} %collective-permute-done.3), kind=kOutput, calls=%fused_computation.36 | convolution fusion | flops 536870912 | bytes 4456448 | tf_op jit(solution)/shard_map/dot_general | solution.py:35
  150.3 5.6 %collective-permute-done = bf16[256,8,512]{2,0,1:T(8,128)(2,1)} collective-permute-done((bf16[256,8,512]{2,0,1:T(8,128)(2,1)}, bf16[256,8,512]{2,0,1:T(8,128)(2,1)}, u32[]{:S(2)}, u32[]{:S(2)}) %collective-permute-start) | collective-permute-done | bytes 2097184 | tf_op jit(solution)/shard_map/ppermute | solution.py:59
  155.8 3.9 %copy.32 = bf16[256,8,512]{0,2,1:T(8,128)(2,1)} copy(bf16[256,8,512]{2,0,1:T(8,128)(2,1)} %collective-permute-done) | data formatting | bytes 4194304 | tf_op jit(solution)/shard_map/ppermute | solution.py:59
  159.7 3.0 fusion.15
  162.8 3.1 %broadcast_select_fusion.5 = (f32[256,256]{0,1:T(8,128)S(1)}, f32[256,256]{0,1:T(8,128)S(1)}) fusion(pred[]{:T(512)S(6)} %eq.6, f32[256,256]{0,1:T(8,128)S(1)} %copy-done.28, bf16[256,8,512]{2,0,1:T(8,128)(2,1)} %collective-permute-done.2, bf16[256,8,512]{2,0,1:T(8,128)(2,1)} %collective-permute-done), kind=kOutput, calls=%fused_computation.82 | convolution fusion | flops 537067520 | bytes 4980737 | tf_op jit(solution)/shard_map/dot_general | solution.py:35
  170.0 5.3 %maximum_maximum_fusion = f32[768,1024]{0,1:T(8,128)} fusion(f32[256,256]{0,1:T(8,128)S(1)} %get-tuple-element.30, f32[256,256]{0,1:T(8,128)S(1)} %copy-done.25, f32[256,256]{0,1:T(8,128)S(1)} %copy-done.24, f32[256,256]{0,1:T(8,128)S(1)} %get-tuple-element.29, f32[256,256]{0,1:T(8,128)S(1)} %get-tuple-element.28, f32[256,256]{0,1:T(8,128)S(1)} %copy-done.27, ...), kind=kLoop, calls=%fused_computation.6 | loop fusion | flops 8650752 | bytes 6029312 | tf_op jit(solution)/shard_map/concatenate | solution.py:103
  181.6 18.0 %collective-permute-done.6 = bf16[256,4096]{1,0:T(8,128)(2,1)} collective-permute-done((bf16[256,4096]{1,0:T(8,128)(2,1)}, bf16[256,4096]{1,0:T(8,128)(2,1)}, u32[]{:S(2)}, u32[]{:S(2)}) %collective-permute-start.6) | collective-permute-done | bytes 2097184 | tf_op jit(solution)/shard_map/ppermute | solution.py:70
  226.3 28.5 %collective-permute-done.24 = f32[16,2,128]{2,0,1:T(8,128)S(1)} collective-permute-done((f32[16,2,128]{2,0,1:T(8,128)S(1)}, f32[16,2,128]{2,0,1:T(8,128)S(1)}, u32[]{:S(2)}, u32[]{:S(2)}) %collective-permute-start.24) | collective-permute-done | bytes 16416 | tf_op jit(solution)/shard_map/ppermute | solution.py:134
  258.1 2.8 collective-permute-done.23
  267.3 3.1 %collective-permute-done.10 = f32[256,256]{1,0:T(8,128)S(1)} collective-permute-done((f32[256,256]{1,0:T(8,128)S(1)}, f32[256,256]{1,0:T(8,128)S(1)}, u32[]{:S(2)}, u32[]{:S(2)}) %collective-permute-start.10) | collective-permute-done | bytes 262176 | tf_op jit(solution)/shard_map/ppermute | solution.py:146
  276.4 7.3 %collective-permute-done.11 = f32[256,256]{1,0:T(8,128)S(1)} collective-permute-done((f32[256,256]{1,0:T(8,128)S(1)}, f32[256,256]{1,0:T(8,128)S(1)}, u32[]{:S(2)}, u32[]{:S(2)}) %collective-permute-start.11) | collective-permute-done | bytes 262176 | tf_op jit(solution)/shard_map/ppermute | solution.py:150
  283.8 7.8 %collective-permute-done.4 = f32[256,256]{0,1:T(8,128)S(1)} collective-permute-done((f32[256,256]{0,1:T(8,128)S(1)}, f32[256,256]{0,1:T(8,128)S(1)}, u32[]{:S(2)}, u32[]{:S(2)}) %collective-permute-start.4) | collective-permute-done | bytes 262176 | tf_op jit(solution)/shard_map/ppermute | solution.py:107
  (184 shorter events, 115.2 us)
Async XLA Ops:
  7.2 265.3 %reduce-scatter.2.cloned.1.call-start = ((), (), s32[]{:S(2)}) async-start(), calls=%async_computation.1 | async-start | bytes 3932160 | tf_op jit(solution)/shard_map/reduce_scatter | solution.py:104
  13.6 49.2 %collective-permute-start.8 = (bf16[256,1024]{1,0:T(8,128)(2,1)}, bf16[256,1024]{1,0:T(8,128)(2,1)S(1)}, u32[]{:S(2)}, u32[]{:S(2)}) collective-permute-start(bf16[256,1024]{1,0:T(8,128)(2,1)} %slice.57), channel_id=1, source_target_pairs={{0,8},{12,4},{1,9},{13,5},{2,10},{14,6},{3,11},{15,7},{16,24},{28,... | collective-permute-start | bytes 1572872 | tf_op jit(solution)/shard_map/ppermute | solution.py:70
  20.9 45.1 %collective-permute-start.7 = (bf16[256,3072]{1,0:T(8,128)(2,1)}, bf16[256,3072]{1,0:T(8,128)(2,1)}, u32[]{:S(2)}, u32[]{:S(2)}) collective-permute-start(bf16[256,3072]{1,0:T(8,128)(2,1)} %slice.55), channel_id=1, source_target_pairs={{0,8},{12,4},{1,9},{13,5},{2,10},{14,6},{3,11},{15,7},{16,24},{28,... | collective-permute-start | bytes 4718600 | tf_op jit(solution)/shard_map/ppermute | solution.py:70
  25.4 109.9 %collective-permute-start.2 = (bf16[256,8,512]{2,0,1:T(8,128)(2,1)}, bf16[256,8,512]{2,0,1:T(8,128)(2,1)}, u32[]{:S(2)}, u32[]{:S(2)}) collective-permute-start(bf16[256,8,512]{2,0,1:T(8,128)(2,1)} %bitcast.161), channel_id=1, source_target_pairs={{4,8},{8,4},{5,9},{9,5},{6,10},{10,6},{7,11},{11,7},{20,24},{24,20... | collective-permute-start | bytes 6291464 | tf_op jit(solution)/shard_map/ppermute | solution.py:60
  29.5 45.9 %collective-permute-start.3 = (bf16[256,8,512]{2,0,1:T(8,128)(2,1)}, bf16[256,8,512]{2,0,1:T(8,128)(2,1)}, u32[]{:S(2)}, u32[]{:S(2)}) collective-permute-start(bf16[256,8,512]{2,0,1:T(8,128)(2,1)} %bitcast.160), channel_id=1, source_target_pairs={{4,8},{8,4},{5,9},{9,5},{6,10},{10,6},{7,11},{11,7},{20,24},{24,20... | collective-permute-start | bytes 6291464 | tf_op jit(solution)/shard_map/ppermute | solution.py:60
  33.5 77.4 %collective-permute-start.1 = (bf16[256,8,512]{2,0,1:T(8,128)(2,1)}, bf16[256,8,512]{2,0,1:T(8,128)(2,1)}, u32[]{:S(2)}, u32[]{:S(2)}) collective-permute-start(bf16[256,8,512]{2,0,1:T(8,128)(2,1)} %bitcast.162), channel_id=1, source_target_pairs={{0,4},{12,8},{1,5},{13,9},{2,6},{14,10},{3,7},{15,11},{16,20},{28,... | collective-permute-start | bytes 6291464 | tf_op jit(solution)/shard_map/ppermute | solution.py:59
  62.8 93.0 %collective-permute-start = (bf16[256,8,512]{2,0,1:T(8,128)(2,1)}, bf16[256,8,512]{2,0,1:T(8,128)(2,1)}, u32[]{:S(2)}, u32[]{:S(2)}) collective-permute-start(bf16[256,8,512]{2,0,1:T(8,128)(2,1)} %bitcast.163), channel_id=1, source_target_pairs={{0,4},{12,8},{1,5},{13,9},{2,6},{14,10},{3,7},{15,11},{16,20},{28,... | collective-permute-start | bytes 6291464 | tf_op jit(solution)/shard_map/ppermute | solution.py:59
  66.0 133.7 %collective-permute-start.6 = (bf16[256,4096]{1,0:T(8,128)(2,1)}, bf16[256,4096]{1,0:T(8,128)(2,1)}, u32[]{:S(2)}, u32[]{:S(2)}) collective-permute-start(bf16[256,4096]{1,0:T(8,128)(2,1)} %bitcast.52), channel_id=1, source_target_pairs={{0,8},{12,4},{1,9},{13,5},{2,10},{14,6},{3,11},{15,7},{16,24},{28,... | collective-permute-start | bytes 6291464 | tf_op jit(solution)/shard_map/ppermute | solution.py:70
  124.6 96.5 %collective-permute-start.19 = (f32[4,16,2,128]{3,1,2,0:T(8,128)}, f32[4,16,2,128]{3,1,2,0:T(8,128)}, u32[]{:S(2)}, u32[]{:S(2)}) collective-permute-start(f32[4,16,2,128]{3,1,2,0:T(8,128)} %dynamic-slice_bitcast_fusion.4), channel_id=1, source_target_pairs={{0,2},{2,0},{1,3},{3,1},{4,6},{6,4},{5,7},{7,5},{8,10},{10,8},{9,1... | collective-permute-start | bytes 196616 | tf_op jit(solution)/shard_map/ppermute | solution.py:128
  177.7 46.9 %collective-permute-start.16 = (f32[4,16,6,128]{3,1,2,0:T(8,128)}, f32[4,16,6,128]{3,1,2,0:T(8,128)}, u32[]{:S(2)}, u32[]{:S(2)}) collective-permute-start(f32[4,16,6,128]{3,1,2,0:T(8,128)} %dynamic-slice_bitcast_fusion.2), channel_id=1, source_target_pairs={{0,2},{2,0},{1,3},{3,1},{4,6},{6,4},{5,7},{7,5},{8,10},{10,8},{9,1... | collective-permute-start | bytes 589832 | tf_op jit(solution)/shard_map/ppermute | solution.py:128
  219.2 44.7 %collective-permute-start.13 = (f32[4,16,8,128]{3,2,1,0:T(8,128)S(1)}, f32[4,16,8,128]{3,2,1,0:T(8,128)S(1)}, u32[]{:S(2)}, u32[]{:S(2)}) collective-permute-start(f32[4,16,8,128]{3,2,1,0:T(8,128)S(1)} %dynamic-slice_bitcast_fusion), channel_id=1, source_target_pairs={{0,2},{2,0},{1,3},{3,1},{4,6},{6,4},{5,7},{7,5},{8,10},{10,8},{9,1... | collective-permute-start | bytes 786440 | tf_op jit(solution)/shard_map/ppermute | solution.py:128
  221.0 42.1 %collective-permute-start.9 = (f32[256,2,256]{2,0,1:T(8,128)S(1)}, f32[256,2,256]{2,0,1:T(8,128)S(1)}, u32[]{:S(2)}, u32[]{:S(2)}) collective-permute-start(f32[256,2,256]{2,0,1:T(8,128)S(1)} %bitcast.204), channel_id=1, source_target_pairs={{0,1},{1,0},{2,3},{3,2},{4,5},{5,4},{6,7},{7,6},{8,9},{9,8},{10,11... | collective-permute-start | bytes 1572872 | tf_op jit(solution)/shard_map/ppermute | solution.py:143
  222.0 34.1 %collective-permute-start.21 = (f32[16,2,128]{2,0,1:T(8,128)S(1)}, f32[16,2,128]{2,0,1:T(8,128)S(1)}, u32[]{:S(2)}, u32[]{:S(2)}) collective-permute-start(f32[16,2,128]{2,0,1:T(8,128)S(1)} %get-tuple-element.38), channel_id=1, source_target_pairs={{4,12},{8,0},{5,13},{9,1},{6,14},{10,2},{7,15},{11,3},{20,28},{24,... | collective-permute-start | bytes 49160 | tf_op jit(solution)/shard_map/ppermute | solution.py:138
  223.3 31.5 %collective-permute-start.24 = (f32[16,2,128]{2,0,1:T(8,128)S(1)}, f32[16,2,128]{2,0,1:T(8,128)S(1)}, u32[]{:S(2)}, u32[]{:S(2)}) collective-permute-start(f32[16,2,128]{2,0,1:T(8,128)S(1)} %get-tuple-element.39), channel_id=1, source_target_pairs={{4,0},{8,12},{5,1},{9,13},{6,2},{10,14},{7,3},{11,15},{20,16},{24,... | collective-permute-start | bytes 49160 | tf_op jit(solution)/shard_map/ppermute | solution.py:134
  224.6 31.5 %collective-permute-start.20 = (f32[16,2,128]{2,0,1:T(8,128)S(1)}, f32[16,2,128]{2,0,1:T(8,128)S(1)}, u32[]{:S(2)}, u32[]{:S(2)}) collective-permute-start(f32[16,2,128]{2,0,1:T(8,128)S(1)} %get-tuple-element.40), channel_id=1, source_target_pairs={{4,8},{8,4},{5,9},{9,5},{6,10},{10,6},{7,11},{11,7},{20,24},{24,20... | collective-permute-start | bytes 49160 | tf_op jit(solution)/shard_map/ppermute | solution.py:138
  256.2 6.9 %collective-permute-start.18 = (f32[16,6,128]{2,0,1:T(8,128)S(1)}, f32[16,6,128]{2,0,1:T(8,128)S(1)}, u32[]{:S(2)}, u32[]{:S(2)}) collective-permute-start(f32[16,6,128]{2,0,1:T(8,128)S(1)} %get-tuple-element.35), channel_id=1, source_target_pairs={{4,12},{8,0},{5,13},{9,1},{6,14},{10,2},{7,15},{11,3},{20,28},{24,... | collective-permute-start | bytes 147464 | tf_op jit(solution)/shard_map/ppermute | solution.py:138
  263.3 7.2 %collective-permute-start.10 = (f32[256,256]{1,0:T(8,128)S(1)}, f32[256,256]{1,0:T(8,128)S(1)}, u32[]{:S(2)}, u32[]{:S(2)}) collective-permute-start(f32[256,256]{1,0:T(8,128)S(1)} %dynamic-slice_bitcast_fusion.1), channel_id=1, source_target_pairs={{0,2},{2,0},{1,3},{3,1},{4,6},{6,4},{5,7},{7,5},{8,10},{10,8},{9,1... | collective-permute-start | bytes 786440 | tf_op jit(solution)/shard_map/ppermute | solution.py:146
  264.0 9.5 %collective-permute-start.15 = (f32[16,8,128]{2,1,0:T(8,128)S(1)}, f32[16,8,128]{2,1,0:T(8,128)S(1)}, u32[]{:S(2)}, u32[]{:S(2)}) collective-permute-start(f32[16,8,128]{2,1,0:T(8,128)S(1)} %get-tuple-element.24), channel_id=1, source_target_pairs={{4,12},{8,0},{5,13},{9,1},{6,14},{10,2},{7,15},{11,3},{20,28},{24,... | collective-permute-start | bytes 196616 | tf_op jit(solution)/shard_map/ppermute | solution.py:138
  265.3 9.6 %collective-permute-start.22 = (f32[16,8,128]{2,1,0:T(8,128)S(1)}, f32[16,8,128]{2,1,0:T(8,128)S(1)}, u32[]{:S(2)}, u32[]{:S(2)}) collective-permute-start(f32[16,8,128]{2,1,0:T(8,128)S(1)} %get-tuple-element.25), channel_id=1, source_target_pairs={{4,0},{8,12},{5,1},{9,13},{6,2},{10,14},{7,3},{11,15},{20,16},{24,... | collective-permute-start | bytes 196616 | tf_op jit(solution)/shard_map/ppermute | solution.py:134
  266.6 9.0 %collective-permute-start.14 = (f32[16,8,128]{2,1,0:T(8,128)S(1)}, f32[16,8,128]{2,1,0:T(8,128)S(1)}, u32[]{:S(2)}, u32[]{:S(2)}) collective-permute-start(f32[16,8,128]{2,1,0:T(8,128)S(1)} %get-tuple-element.26), channel_id=1, source_target_pairs={{4,8},{8,4},{5,9},{9,5},{6,10},{10,6},{7,11},{11,7},{20,24},{24,20... | collective-permute-start | bytes 196616 | tf_op jit(solution)/shard_map/ppermute | solution.py:138
  270.5 13.3 %collective-permute-start.12 = (f32[256,256]{1,0:T(8,128)S(1)}, f32[256,256]{1,0:T(8,128)S(1)}, u32[]{:S(2)}, u32[]{:S(2)}) collective-permute-start(f32[256,256]{1,0:T(8,128)S(1)} %bitcast_add_fusion.2), channel_id=1, source_target_pairs={{4,3},{5,7},{6,11},{9,4},{10,8},{11,12},{20,19},{21,23},{22,27},{2... | collective-permute-start | bytes 786440 | tf_op jit(solution)/shard_map/ppermute | solution.py:151
  271.1 12.5 %collective-permute-start.11 = (f32[256,256]{1,0:T(8,128)S(1)}, f32[256,256]{1,0:T(8,128)S(1)}, u32[]{:S(2)}, u32[]{:S(2)}) collective-permute-start(f32[256,256]{1,0:T(8,128)S(1)} %bitcast_add_fusion.2), channel_id=1, source_target_pairs={{4,12},{8,0},{5,13},{9,1},{6,14},{10,2},{7,15},{11,3},{20,28},{24,... | collective-permute-start | bytes 786440 | tf_op jit(solution)/shard_map/ppermute | solution.py:150
  273.6 18.0 %collective-permute-start.4 = (f32[256,256]{0,1:T(8,128)S(1)}, f32[256,256]{0,1:T(8,128)S(1)}, u32[]{:S(2)}, u32[]{:S(2)}) collective-permute-start(f32[256,256]{0,1:T(8,128)S(1)} %get-tuple-element.14), channel_id=1, source_target_pairs={{4,0},{8,12},{5,1},{9,13},{6,2},{10,14},{7,3},{11,15},{20,16},{24,... | collective-permute-start | bytes 786440 | tf_op jit(solution)/shard_map/ppermute | solution.py:107
  274.9 16.7 %collective-permute-start.5 = (f32[256,256]{0,1:T(8,128)S(1)}, f32[256,256]{0,1:T(8,128)S(1)}, u32[]{:S(2)}, u32[]{:S(2)}) collective-permute-start(f32[256,256]{0,1:T(8,128)S(1)} %get-tuple-element.15), channel_id=1, source_target_pairs={{4,8},{8,4},{5,9},{9,5},{6,10},{10,6},{7,11},{11,7},{20,24},{24,20... | collective-permute-start | bytes 786440 | tf_op jit(solution)/shard_map/ppermute | solution.py:108
  (35 other events, 242.9 us)
Sparse Core Ops, SparseCore 0:
  175.5 81.3 reduce-scatter.1

commit v2 on v0

v2 whole, which is shorter than its diff:
```python
import functools

import jax
import jax.numpy as jnp
from jax import lax
from jax.experimental import pallas as pl
from jax.experimental.pallas import tpu as pltpu
from jax.sharding import PartitionSpec as P

F32 = jnp.float32
BF16 = jnp.bfloat16
NEAR = [(0, 1), (3, 2)]
CROSS = [(1, 2), (2, 1)]
FAR = [(0, 2), (3, 1)]
NEAR_BACK = [(1, 0), (2, 3)]
FAR_BACK = [(1, 3), (2, 0)]
SWAP = [(0, 1), (1, 0)]
TURN = [(4 + l, 4 * l + 3) for l in (0, 1, 2)] + [(8 + l, 4 * l) for l in (1, 2, 3)]


def nt(a, b):
    return lax.dot_general(a, b, (((1,), (1,)), ((), ())), preferred_element_type=F32)


def tn(a, b):
    return lax.dot_general(a, b, (((0,), (0,)), ((), ())), preferred_element_type=F32)


def nn(a, b):
    return jnp.dot(a, b, preferred_element_type=F32)


def gathered(snapshot, x_basis, y_basis):
    rows_local = snapshot.shape[0]
    columns = snapshot.shape[1] * snapshot.shape[2] * snapshot.shape[3]
    unfolded = snapshot.reshape(rows_local, columns)
    rank_count = x_basis.shape[1]
    rank_rows = rank_count // lax.axis_size("gx")
    inverse = 1.0 / (columns * lax.axis_size("gy") * lax.axis_size("gz"))
    basis_cols = lax.dynamic_slice_in_dim(x_basis, lax.axis_index("gx") * rank_rows, rank_rows, 1)
    shard_rows = lax.all_gather(unfolded, "gx", axis=0, tiled=True)
    gram_rows = nt(unfolded, shard_rows)
    own_rows = tn(basis_cols, shard_rows).astype(BF16)
    gram_out = lax.psum_scatter(gram_rows * inverse, ("gy", "gz"), scatter_dimension=1, tiled=True)
    shaped = own_rows.reshape(rank_rows, *snapshot.shape[1:])
    along_y = lax.all_to_all(shaped, "gy", split_axis=0, concat_axis=3, tiled=True)
    core_flat = nn(along_y.reshape(-1, along_y.shape[3]), y_basis)
    return gram_out, core_flat.reshape(*along_y.shape[:3], y_basis.shape[1])


def pairs_kernel(first, last, at, near, own, cross, other, *rest):
    if not first:
        carried, *rest = rest
    *outs, acc = rest
    step = pl.program_id(0)

    @pl.when(step == 0)
    def _():
        acc[...] = jnp.zeros_like(acc) if first else carried[...]

    n, s, c, o = near[...], own[...], cross[...], other[...]
    acc[0] += nt(n, s)
    acc[1] += nt(n, c)
    acc[2] += nt(s, c)
    acc[3] += nt(s, s) + nt(o, o)

    @pl.when(step == pl.num_programs(0) - 1)
    def _():
        if not last:
            outs[0][...] = acc[...]
            return
        gy, gz, side, inner = at[0], at[1], at[2], at[3]
        size = acc.shape[1]
        zero = jnp.zeros((size, size), F32)
        ns, nc, sc, diag = acc[0], acc[1], acc[2], acc[3]
        mid = jnp.full((size, size), inner, jnp.int32) == 1
        table = [
            [zero, ns, nc, zero],
            [ns.T + jnp.where(mid, 0.0, diag), jnp.where(mid, diag, 0.0), sc, zero],
            [nc.T, sc.T, zero, zero],
        ]
        for k in range(4):
            l = jnp.where(side == 0, k, 3 - k)
            for out, flag in zip(outs, (0, 1)):

                @pl.when(((l & 1) ^ gz) == flag)
                def _(k=k, l=l, out=out):
                    for row in range(3):
                        out[(l >> 1) ^ gy, row * size : (row + 1) * size, :] = table[row][k]


def whole(shape):
    return pl.BlockSpec(shape, lambda j, at: (0,) * len(shape))


def call(name, kernel, at, grid, in_specs, operands, out_shapes, scratch=(), types=None):
    types = types or [F32] * len(out_shapes)
    return pl.pallas_call(
        kernel,
        out_shape=tuple(jax.ShapeDtypeStruct(o, t) for o, t in zip(out_shapes, types)),
        grid_spec=pltpu.PrefetchScalarGridSpec(
            num_scalar_prefetch=1,
            grid=(grid,),
            in_specs=in_specs,
            out_specs=tuple(whole(o) for o in out_shapes),
            scratch_shapes=scratch,
        ),
        cost_estimate=pl.CostEstimate(flops=1, transcendentals=0, bytes_accessed=1),
        compiler_params=pltpu.CompilerParams(vmem_limit_bytes=40 << 20),
        name=name,
    )(at, *operands)


def once(name, kernel, at, operands, out_shapes, types=None):
    specs = [whole(o.shape) for o in operands]
    return call(name, kernel, at, 1, specs, operands, out_shapes, types=types)


def add_split_kernel(at, keep, got, first, second):
    first[...] = keep[0] + got[0]
    second[...] = keep[1] + got[1]


def add_rows_kernel(at, keep, got, *outs):
    size = keep.shape[0] // len(outs)
    for i, out in enumerate(outs):
        out[...] = keep[i * size : (i + 1) * size] + got[i * size : (i + 1) * size]


def add_home_kernel(at, keep, got, *outs):
    for k, out in enumerate(outs):
        out[...] = (keep[k] + got[k]).astype(out.dtype)


def add_late_kernel(at, keep, got, stay, leave):
    stay[...] = keep[0] + got[0]
    leave[...] = (keep[1] + got[1]).astype(leave.dtype)


def part_kernel(at, stay, got, late, turned):
    total = stay[...] + got[...]
    late[...] = total.astype(late.dtype)
    turned[...] = total.T.astype(turned.dtype)


def final_kernel(inverse, at, gram_own, gram_near, gram_cross, late, turned, *rest):
    *groups, gram, core = rest
    side, inner = at[2], at[3]
    gram[...] = (
        (gram_own[...] + gram_near[...] + gram_cross[...])
        + (late[...].astype(F32) + turned[...].astype(F32))
    ) * inverse
    nz = core.shape[2]
    half = core.shape[1] // 2
    mid = jnp.full((core.shape[0], 128), inner, jnp.int32) == 1
    j = 0
    for near, kept, cross, far in (groups[:4], groups[4:]):
        for k in range(near.shape[1] // 128):
            span = slice(k * 128, (k + 1) * 128)
            mine = jnp.where(mid, kept[:, span], near[:, span].astype(F32))
            other = cross[:, span].astype(F32) + far[:, span].astype(F32)
            c, z = divmod(j, nz)
            core[:, half * (1 - side) + c, z, :] = mine
            core[:, half * side + c, z, :] = other
            j += 1


def pairs(at, near, own, cross, other, carried, last, ny):
    rows, width = near.shape
    first = carried is None
    acc_shape = (4, rows, rows)
    return call(
        "pairs",
        functools.partial(pairs_kernel, first, last),
        at,
        width // ny,
        [pl.BlockSpec((rows, ny), lambda j, at: (0, j))] * 4 + ([] if first else [whole(acc_shape)]),
        [near, own, cross, other] + ([] if first else [carried]),
        [(2, 3 * rows, rows)] * 2 if last else [acc_shape],
        [pltpu.VMEM(acc_shape, F32)],
    )


def meet_kernel(first, last, joined, at, far, near, own, cross, basis, y_own, *rest):
    if not first:
        carried, *rest = rest
    if joined:
        old_keep, old_give, *rest = rest
    *outs, core_keep, core_give, acc = rest
    step = pl.program_id(0)
    gy, gz, side = at[0], at[1], at[2]
    base = 0
    if joined:
        base = old_keep.shape[2]

    @pl.when(step == 0)
    def _():
        acc[...] = jnp.zeros_like(acc) if first else carried[...]
        if joined:
            core_keep[:, :, :base] = old_keep[...]
            core_give[:, :, :base] = old_give[...]

    f, n, s, c = far[...], near[...], own[...], cross[...]
    projected = nn(basis[0], n) + nn(basis[1], s) + nn(basis[2], c) + nn(basis[3], f)
    part = nn(projected.astype(BF16), y_own[...])
    acc[0] += nt(f, n)
    acc[1] += nt(f, s)
    acc[2] += nt(f, c)
    few, cols = part.shape[0] // 8, part.shape[1]
    span = pl.ds(pl.multiple_of(base + step * cols, 128), cols)
    for z in range(4):
        k = jnp.where(side == 0, z, 3 - z)
        for out, flag in ((core_keep, gy), (core_give, 1 - gy)):
            for y in range(2):

                @pl.when(flag == y)
                def _(z=z, k=k, y=y, out=out):
                    start = (2 * z + y) * few
                    out[k, :, span] = part[start : start + few]

    @pl.when(step == pl.num_programs(0) - 1)
    def _():
        if not last:
            outs[0][...] = acc[...]
            return
        for k in range(4):
            l = jnp.where(side == 0, k, 3 - k)
            for out, flag in zip(outs, (0, 1)):

                @pl.when(((l & 1) ^ gz) == flag)
                def _(k=k, l=l, out=out):
                    out[(l >> 1) ^ gy] = acc[k] if k < 3 else jnp.zeros_like(acc[0])


def meet(at, far, near, own, cross, lo, basis, y_own, carried, old, last):
    rows, width = far.shape
    ny, s_cols = y_own.shape
    rank = basis.shape[1]
    n = width // ny
    first, joined = carried is None, old is not None
    shifted = pl.BlockSpec((rows, ny), lambda j, at: (0, lo + j))
    acc_shape = (3, rows, rows)
    core_shape = (4, rank // 8, n * s_cols + (old[0].shape[2] if joined else 0))
    return call(
        "meet",
        functools.partial(meet_kernel, first, last, joined),
        at,
        n,
        [pl.BlockSpec((rows, ny), lambda j, at: (0, j)), shifted, shifted, shifted]
        + [whole(basis.shape), whole(y_own.shape)]
        + ([] if first else [whole(acc_shape)])
        + ([whole(o.shape) for o in old] if joined else []),
        [far, near, own, cross, basis, y_own]
        + ([] if first else [carried])
        + (list(old) if joined else []),
        ([(2, rows, rows)] * 2 if last else [acc_shape]) + [core_shape] * 2,
        [pltpu.VMEM(acc_shape, F32)],
    )


def meeting(snapshot, x_basis, y_basis):
    rows, ncomp, nz, ny = snapshot.shape
    rank = x_basis.shape[1]
    gx, gy, gz = lax.axis_index("gx"), lax.axis_index("gy"), lax.axis_index("gz")
    side = gx // 2
    inner = (gx == 1) | (gx == 2)
    half = ncomp // 2
    width = nz * ny
    inverse = 1.0 / (ncomp * width * lax.axis_size("gy") * lax.axis_size("gz"))
    own_at, oth_at = (1 - side) * half, side * half
    at = jnp.stack([gy, gz, side, inner.astype(jnp.int32)])

    tied = lax.optimization_barrier

    def take(source, start):
        return lax.dynamic_slice_in_dim(source, start, 1, 1).reshape(rows, nz, ny)

    def flat(a):
        return a.reshape(rows, width)

    near, cross, own, oth = ([None] * half for _ in range(4))
    oth_raw = take(snapshot, oth_at)
    source, oth_raw = tied((snapshot, oth_raw))
    own_raw = take(source, own_at)
    source, own_raw = tied((source, own_raw))
    oth_late = take(source, oth_at + 1)
    source, oth_late = tied((source, oth_late))
    oth[1], own[1] = flat(oth_late), flat(take(source, own_at + 1))
    cross_raw = lax.ppermute(oth_raw, "gx", CROSS)
    near_raw = lax.ppermute(own_raw, "gx", NEAR)
    cross[1] = lax.ppermute(oth[1], "gx", CROSS)
    near[1] = lax.ppermute(own[1], "gx", NEAR)
    oth_raw, own_raw, oth[1], own[1] = tied((oth_raw, own_raw, oth[1], own[1]))
    oth[0], own[0] = flat(oth_raw), flat(own_raw)

    places = [
        jnp.where(side == 0, 0, 3),
        gx,
        jnp.where(side == 0, 2, 1),
        jnp.where(side == 0, 3, 0),
    ]
    basis = jnp.stack([lax.dynamic_slice_in_dim(x_basis, p * rows, rows, 0).T for p in places])
    y_own = lax.dynamic_slice_in_dim(y_basis, gy * ny, ny, 0)

    cuts = [(0, 0, 8), (1, 0, 3), (1, 3, 7), (1, 7, 8)]

    def send_far(i, *gate):
        data, gate = tied((sends[i], gate))
        return lax.ppermute(data, "gx", FAR), *gate

    def meets(i, far, carried, old, last=False):
        h, lo, _ = cuts[i]
        return meet(at, far, near[h], own[h], cross[h], lo, basis, y_own, carried, old, last)

    def across(core, link):
        keep, give = core
        return once(
            "add_home",
            add_home_kernel,
            at,
            [keep, lax.ppermute(give, "gy", SWAP)],
            [keep.shape[1:]] * 4,
            [link, F32, link, link],
        )

    def send_home(near, kept, cross, far):
        return (
            lax.ppermute(near, "gx", NEAR_BACK),
            kept,
            lax.ppermute(cross, "gx", CROSS),
            lax.ppermute(far, "gx", FAR_BACK),
        )

    sends = [oth[0]] + [oth[1][:, lo * ny : hi * ny] for _, lo, hi in cuts[1:]]
    sends, cross_raw, own[0] = tied((sends, cross_raw, own[0]))
    cross[0] = flat(cross_raw)
    cross[0], near_raw = tied((cross[0], near_raw))
    near[0] = flat(near_raw)
    far0, cross[0], near[0], own[0], basis, y_own = send_far(
        0, cross[0], near[0], own[0], basis, y_own
    )
    (sums,) = pairs(at, near[0], own[0], cross[0], oth[0], None, False, ny)
    sums, cross[1] = tied((sums, cross[1]))

    far1, cross[1], near[1], sums = send_far(1, cross[1], near[1], sums)
    keep, give = pairs(at, near[1], own[1], cross[1], oth[1], sums, True, ny)

    early, leave = once(
        "add_split", add_split_kernel, at, [keep, lax.ppermute(give, "gz", SWAP)], [keep.shape[1:]] * 2
    )
    far2, far0, leave = send_far(2, far0, leave)
    far0, far1 = tied((far0, far1))
    acc, *core = meets(0, far0, None, None)
    gram_near, gram_own, gram_cross = once(
        "add_rows", add_rows_kernel, at, [early, lax.ppermute(leave, "gy", SWAP)], [(rows, rows)] * 3
    )

    far3, far1, gram_own, acc = send_far(3, far1, gram_own, acc)
    acc, *core = meets(1, far1, acc, core)
    gram_near = lax.ppermute(gram_near, "gx", NEAR_BACK)
    gram_cross = lax.ppermute(gram_cross, "gx", CROSS)
    blocks = across(core, F32)
    home = send_home(*blocks)

    far2, blocks = tied((far2, blocks))
    acc, *core = meets(2, far2, acc, None)
    far3, acc, gram_near, gram_cross, home = tied(
        (far3, acc, gram_near, gram_cross, home)
    )
    keep, give, *core = meets(3, far3, acc, core, True)
    stay, leave = once(
        "add_late",
        add_late_kernel,
        at,
        [keep, lax.ppermute(give, "gz", SWAP)],
        [(rows, rows)] * 2,
        [F32, BF16],
    )
    rest = send_home(*across(core, BF16))
    late, turned = once(
        "part",
        part_kernel,
        at,
        [stay, lax.ppermute(leave, "gy", SWAP)],
        [(rows, rows)] * 2,
        [BF16] * 2,
    )
    late = lax.ppermute(late, "gx", FAR_BACK)
    turned = lax.ppermute(turned, ("gx", "gy", "gz"), TURN)
    return once(
        "final",
        functools.partial(final_kernel, inverse),
        at,
        [gram_own, gram_near, gram_cross, late, turned, *home, *rest],
        [(rows, rows), (rank // 8, ncomp, nz, y_basis.shape[1])],
    )


def solution(mesh):
    in_specs = (P(("grp", "gx"), None, "gz", "gy"), P("grp", None), P("grp", None))
    out_specs = (P(("grp", "gx"), ("gy", "gz")), P(("grp", "gx", "gy"), None, "gz", None))
    sizes = (mesh.shape["gx"], mesh.shape["gy"], mesh.shape["gz"])
    body = meeting if sizes == (4, 2, 2) else gathered
    return jax.shard_map(body, mesh=mesh, in_specs=in_specs, out_specs=out_specs, check_vma=False)
```

time: 646 us -> 236 us (0.37)
  waiting for transfers between devices: 564 us -> 102 us
  starting transfers between devices: 0.26 us -> 51.2 us
  Pallas kernels: 0 us -> 42.3 us
  matrix products: 33.1 us -> 0 us
  local copies, waits for them, and re-layouts: 15.8 us -> 38.8 us
  blocking collectives: 18.8 us -> 0 us
  between operations: 14.1 us -> 1.04 us
    all_gather x1 -> x0, waiting for transfers between devices: 564 us -> none  [on_device(): shard_rows = lax.all_gather(unfolded, 'gx', axis=0, tiled=True)]
    ppermute x0 -> x24, waiting for transfers between devices: none -> 102 us  [the longest x4 43.1 us: send_far(): return (lax.ppermute(data, 'gx', FAR), *gate)]
    ppermute x0 -> x24, starting transfers between devices: none -> 51.2 us  [the longest x4 20.9 us: send_far(): return (lax.ppermute(data, 'gx', FAR), *gate)]
    pallas_call x0 -> x13, Pallas kernels: none -> 42.3 us  [call(): pl.pallas_call(kernel, out_shape=tuple((jax.ShapeDtypeStruct(o, t) for o,...]
    dot_general x3 -> x0, matrix products: 33.1 us -> none  [the longest x1 17.6 us: on_device(): lax.dot_general(unfolded, shard_rows, (((1,), (1,)), ((), ())), preferred...]
    all_to_all x1 -> x0, blocking collectives: 18.8 us -> none  [on_device(): lax.all_to_all(shaped, 'gy', split_axis=0, concat_axis=3, tiled=True)]
    unnamed x6 -> x30, local copies, waits for them, and re-layouts: 15.7 us -> 23.8 us
    reshape x0 -> x3, local copies, waits for them, and re-layouts: none -> 7.9 us  [take(): return lax.dynamic_slice_in_dim(source, start, 1, 1).reshape(rows, nz, ny)]
  transfers between devices with their start and end apart: 2 -> 24, of which waited for: 1 -> 11; matrix products, arithmetic and copies ran while one was open for 2% -> 13% of each run, Pallas kernels for 0% -> 16%
where the time goes in v2:
time: 236 us; the launch traced here: 235 us
  waiting for transfers between devices  102 us (43%)
  starting transfers between devices  51.2 us (22%)
  Pallas kernels  42.3 us (18%)
  local copies, waits for them, and re-layouts  38.8 us (16%)
    ppermute x4, waiting for transfers between devices, send_far(): return (lax.ppermute(data, 'gx', FAR), *gate)  43.1 us
    pallas_call x13, Pallas kernels, call(): pl.pallas_call(kernel, out_shape=tuple((jax.ShapeDtypeStruct(o, t) for o,...  42.3 us
    unnamed x30, local copies, waits for them, and re-layouts  23.8 us
    ppermute x1, waiting for transfers between devices, meeting(): near[1] = lax.ppermute(own[1], 'gx', NEAR)  22.9 us
    ppermute x4, starting transfers between devices, send_far(): return (lax.ppermute(data, 'gx', FAR), *gate)  20.9 us
    ppermute x1, waiting for transfers between devices, meeting(): near_raw = lax.ppermute(own_raw, 'gx', NEAR)  16.3 us
    ppermute x2, waiting for transfers between devices, send_home(): lax.ppermute(far, 'gx', FAR_BACK)  8.49 us
    reshape x3, local copies, waits for them, and re-layouts, take(): return lax.dynamic_slice_in_dim(source, start, 1, 1).reshape(rows, nz, ny)  7.9 us
  transfers between devices with their start and end apart: 24, of which 11 were waited for; matrix products, arithmetic and copies ran while one was open for 13% of the time, Pallas kernels for 16%

profile of v2, /device:TPU:0, one launch (start us, length us, event | category | flops | bytes accessed | tf_op | source)
XLA Modules:
  0.0 235.1 jit_solution(8609642147098099155)
XLA Ops:
  0.7 3.1 %dynamic-slice_bitcast_fusion.2 = bf16[256,8,512]{2,1,0:T(8,128)(2,1)} fusion(bf16[256,4,8,512]{3,2,1,0:T(8,128)(2,1)} %param.3, s32[]{:T(128)S(6)} %select_n.43), kind=kLoop, calls=%fused_computation.2 | loop fusion | bytes 4194308 | tf_op jit(solution)/shard_map/reshape | solution.py:276
  5.7 3.1 %dynamic-slice_bitcast_fusion.1 = bf16[256,8,512]{2,1,0:T(8,128)(2,1)} fusion(bf16[256,4,8,512]{3,2,1,0:T(8,128)(2,1)} %param.3, s32[]{:T(128)S(6)} %select_n.44), kind=kLoop, calls=%fused_computation.1 | loop fusion | bytes 4194308 | tf_op jit(solution)/shard_map/reshape | solution.py:276
  8.8 7.8 %collective-permute-start.1 = (bf16[256,8,512]{2,1,0:T(8,128)(2,1)}, bf16[256,8,512]{2,1,0:T(8,128)(2,1)}, u32[]{:S(2)}, u32[]{:S(2)}) collective-permute-start(bf16[256,8,512]{2,1,0:T(8,128)(2,1)} %dynamic-slice_bitcast_fusion.1), channel_id=1, source_target_pairs={{0,4},{12,8},{1,5},{13,9},{2,6},{14,10},{3,7},{15,11},{16,20},{28,... | collective-permute-start | bytes 6291464 | tf_op jit(solution)/shard_map/ppermute | solution.py:290
  33.8 3.9 %copy.16 = bf16[32,8,8,512]{3,1,2,0:T(8,128)(2,1)} copy(bf16[32,8,8,512]{3,2,1,0:T(8,128)(2,1)} %bitcast.26) | data formatting | bytes 4194304
  37.6 3.8 %copy.15 = bf16[32,8,8,512]{3,1,2,0:T(8,128)(2,1)} copy(bf16[32,8,8,512]{3,2,1,0:T(8,128)(2,1)} %bitcast.24) | data formatting | bytes 4194304
  41.5 3.8 %copy.17 = bf16[32,8,8,512]{3,1,2,0:T(8,128)(2,1)} copy(bf16[32,8,8,512]{3,2,1,0:T(8,128)(2,1)} %bitcast.28) | data formatting | bytes 4194304
  45.3 16.3 %collective-permute-done.1 = bf16[256,8,512]{2,1,0:T(8,128)(2,1)} collective-permute-done((bf16[256,8,512]{2,1,0:T(8,128)(2,1)}, bf16[256,8,512]{2,1,0:T(8,128)(2,1)}, u32[]{:S(2)}, u32[]{:S(2)}) %collective-permute-start.1) | collective-permute-done | bytes 2097184 | tf_op jit(solution)/shard_map/ppermute | solution.py:290
  61.6 3.9 %copy.18 = bf16[32,8,8,512]{3,1,2,0:T(8,128)(2,1)} copy(bf16[32,8,8,512]{3,2,1,0:T(8,128)(2,1)} %bitcast.30) | data formatting | bytes 4194304
  65.5 5.6 %collective-permute-start.2 = (bf16[256,4096]{1,0:T(8,128)(2,1)}, bf16[256,4096]{1,0:T(8,128)(2,1)}, u32[]{:S(2)}, u32[]{:S(2)}) collective-permute-start(bf16[256,4096]{1,0:T(8,128)(2,1)} %bitcast.25.other), channel_id=1, source_target_pairs={{0,8},{12,4},{1,9},{13,5},{2,10},{14,6},{3,11},{15,7},{16,24},{28,... | collective-permute-start | bytes 6291464 | tf_op jit(solution)/shard_map/ppermute | solution.py:309
  76.0 7.6 %pairs.2.rest_0_ = f32[4,256,256]{2,1,0:T(8,128)S(1)} custom-call(s32[4]{0:T(128)S(1)} %pad_add_fusion.at, bf16[256,4096]{1,0:T(8,128)(2,1)S(1)} %bitcast.44, bf16[256,4096]{1,0:T(8,128)(2,1)S(1)} %bitcast.40, bf16[256,4096]{1,0:T(8,128)(2,1)S(1)} %bitcast.42, bf16[256,4096]{1,0:T(8,128)(2,1)} %bitcast.25.other), custom_call_target="tpu_custom_call" | custom-call | flops 1 | bytes 1 | tf_op jit(solution)/shard_map/pairs/pallas_call | solution.py:98
  83.6 22.9 %collective-permute-done.4.near = bf16[256,4096]{1,0:T(8,128)(2,1)} collective-permute-done((bf16[256,4096]{1,0:T(8,128)(2,1)S(1)}, bf16[256,4096]{1,0:T(8,128)(2,1)}, u32[]{:S(2)}, u32[]{:S(2)}) %collective-permute-start.4) | collective-permute-done | bytes 2097184 | tf_op jit(solution)/shard_map/ppermute | solution.py:292
  106.5 8.8 %pairs.3 = (f32[2,768,256]{2,1,0:T(8,128)S(1)}, f32[2,768,256]{2,1,0:T(8,128)S(1)}) custom-call(s32[4]{0:T(128)S(1)} %pad_add_fusion.at, bf16[256,4096]{1,0:T(8,128)(2,1)} %collective-permute-done.4.near, bf16[256,4096]{1,0:T(8,128)(2,1)S(1)} %bitcast.36, bf16[256,4096]{1,0:T(8,128)(2,1)} %collective-permute-done.3.cross, bf16[256,4096]{1,0:T(8,128)(2,1)} %bitcast.20.other, ...), custom_call_target="tpu_custom_call" | custom-call | flops 1 | bytes 1 | tf_op jit(solution)/shard_map/pairs/pallas_call | solution.py:98
  115.4 4.7 %collective-permute-start.6 = (bf16[256,1536]{1,0:T(8,128)(2,1)S(1)}, bf16[256,1536]{1,0:T(8,128)(2,1)S(1)}, u32[]{:S(2)}, u32[]{:S(2)}) collective-permute-start(bf16[256,1536]{1,0:T(8,128)(2,1)S(1)} %copy-done.8), channel_id=1, source_target_pairs={{0,8},{12,4},{1,9},{13,5},{2,10},{14,6},{3,11},{15,7},{16,24},{28,... | collective-permute-start | bytes 2359304 | tf_op jit(solution)/shard_map/ppermute | solution.py:309
  120.8 30.7 %collective-permute-done.2.far = bf16[256,4096]{1,0:T(8,128)(2,1)} collective-permute-done((bf16[256,4096]{1,0:T(8,128)(2,1)}, bf16[256,4096]{1,0:T(8,128)(2,1)}, u32[]{:S(2)}, u32[]{:S(2)}) %collective-permute-start.2) | collective-permute-done | bytes 2097184 | tf_op jit(solution)/shard_map/ppermute | solution.py:309
  153.0 5.3 %collective-permute-start.9 = (bf16[256,2048]{1,0:T(8,128)(2,1)S(1)}, bf16[256,2048]{1,0:T(8,128)(2,1)S(1)}, u32[]{:S(2)}, u32[]{:S(2)}) collective-permute-start(bf16[256,2048]{1,0:T(8,128)(2,1)S(1)} %copy-done.7), channel_id=1, source_target_pairs={{0,8},{12,4},{1,9},{13,5},{2,10},{14,6},{3,11},{15,7},{16,24},{28,... | collective-permute-start | bytes 3145736 | tf_op jit(solution)/shard_map/ppermute | solution.py:309
  158.4 9.9 %collective-permute-done.6.far = bf16[256,1536]{1,0:T(8,128)(2,1)S(1)} collective-permute-done((bf16[256,1536]{1,0:T(8,128)(2,1)S(1)}, bf16[256,1536]{1,0:T(8,128)(2,1)S(1)}, u32[]{:S(2)}, u32[]{:S(2)}) %collective-permute-start.6) | collective-permute-done | bytes 786464 | tf_op jit(solution)/shard_map/ppermute | solution.py:309
  168.3 8.5 %meet.4 = (f32[3,256,256]{2,1,0:T(8,128)S(1)}, f32[4,16,1024]{2,1,0:T(8,128)S(1)}, f32[4,16,1024]{2,1,0:T(8,128)S(1)}) custom-call(s32[4]{0:T(128)S(1)} %pad_add_fusion.at, bf16[256,4096]{1,0:T(8,128)(2,1)} %collective-permute-done.2.far, bf16[256,4096]{1,0:T(8,128)(2,1)S(1)} %bitcast.45, bf16[256,4096]{1,0:T(8,128)(2,1)S(1)} %bitcast.41, ...), custom_call_target="tpu_custom_call" | custom-call | flops 1 | bytes 1 | tf_op jit(solution)/shard_map/meet/pallas_call | solution.py:98
  177.4 4.4 %meet.5 = (f32[3,256,256]{2,1,0:T(8,128)S(1)}, f32[4,16,1408]{2,1,0:T(8,128)S(1)}, f32[4,16,1408]{2,1,0:T(8,128)S(1)}) custom-call(s32[4]{0:T(128)S(1)} %pad_add_fusion.at, bf16[256,1536]{1,0:T(8,128)(2,1)S(1)} %collective-permute-done.6.far, bf16[256,4096]{1,0:T(8,128)(2,1)} %collective-permute-done.4.near, bf16[256,4096]{1,0:T(8,128)(2,1)S(1)} %bitcast.37, ...), custom_call_target="tpu_custom_call" | custom-call | flops 1 | bytes 1 | tf_op jit(solution)/shard_map/meet/pallas_call | solution.py:98
  183.3 5.3 %collective-permute-start.8 = (bf16[256,512]{1,0:T(8,128)(2,1)S(1)}, bf16[256,512]{1,0:T(8,128)(2,1)S(1)}, u32[]{:S(2)}, u32[]{:S(2)}) collective-permute-start(bf16[256,512]{1,0:T(8,128)(2,1)S(1)} %slice.11), channel_id=1, source_target_pairs={{0,8},{12,4},{1,9},{13,5},{2,10},{14,6},{3,11},{15,7},{16,24},{28,... | collective-permute-start | bytes 786440 | tf_op jit(solution)/shard_map/ppermute | solution.py:309
  197.1 5.2 %meet.6 = (f32[3,256,256]{2,1,0:T(8,128)S(1)}, f32[4,16,512]{2,1,0:T(8,128)S(1)}, f32[4,16,512]{2,1,0:T(8,128)S(1)}) custom-call(s32[4]{0:T(128)S(1)} %pad_add_fusion.at, bf16[256,2048]{1,0:T(8,128)(2,1)S(1)} %collective-permute-done.9.far, bf16[256,4096]{1,0:T(8,128)(2,1)} %collective-permute-done.4.near, bf16[256,4096]{1,0:T(8,128)(2,1)S(1)} %bitcast.38, ...), custom_call_target="tpu_custom_call" | custom-call | flops 1 | bytes 1 | tf_op jit(solution)/shard_map/meet/pallas_call | solution.py:98
  202.4 3.8 %collective-permute-done.15.rest_3_ = f32[16,1408]{1,0:T(8,128)S(1)} collective-permute-done((f32[16,1408]{1,0:T(8,128)S(1)}, f32[16,1408]{1,0:T(8,128)S(1)}, u32[]{:S(2)}, u32[]{:S(2)}) %collective-permute-start.15) | collective-permute-done | bytes 90144 | tf_op jit(solution)/shard_map/ppermute | solution.py:331
  213.3 4.3 %collective-permute-done.17.got = bf16[256,256]{1,0:T(8,128)(2,1)S(1)} collective-permute-done((bf16[256,256]{1,0:T(8,128)(2,1)S(1)}, bf16[256,256]{1,0:T(8,128)(2,1)S(1)}, u32[]{:S(2)}, u32[]{:S(2)}) %collective-permute-start.17) | collective-permute-done | bytes 131104 | tf_op jit(solution)/shard_map/ppermute | solution.py:384
  224.2 4.6 %collective-permute-done.21.rest_4_ = bf16[16,640]{1,0:T(8,128)(2,1)S(1)} collective-permute-done((bf16[16,640]{1,0:T(8,128)(2,1)S(1)}, bf16[16,640]{1,0:T(8,128)(2,1)S(1)}, u32[]{:S(2)}, u32[]{:S(2)}) %collective-permute-start.21) | collective-permute-done | bytes 20512 | tf_op jit(solution)/shard_map/ppermute | solution.py:328
  228.8 4.7 %collective-permute-done.23.rest_7_ = bf16[16,640]{1,0:T(8,128)(2,1)S(1)} collective-permute-done((bf16[16,640]{1,0:T(8,128)(2,1)S(1)}, bf16[16,640]{1,0:T(8,128)(2,1)S(1)}, u32[]{:S(2)}, u32[]{:S(2)}) %collective-permute-start.23) | collective-permute-done | bytes 20512 | tf_op jit(solution)/shard_map/ppermute | solution.py:331
  (78 shorter events, 52.1 us)
Async XLA Ops:
  3.7 37.8 %collective-permute-start = (bf16[256,8,512]{2,1,0:T(8,128)(2,1)}, bf16[256,8,512]{2,1,0:T(8,128)(2,1)}, u32[]{:S(2)}, u32[]{:S(2)}) collective-permute-start(bf16[256,8,512]{2,1,0:T(8,128)(2,1)} %dynamic-slice_bitcast_fusion.2), channel_id=1, source_target_pairs={{4,8},{8,4},{5,9},{9,5},{6,10},{10,6},{7,11},{11,7},{20,24},{24,20... | collective-permute-start | bytes 6291464 | tf_op jit(solution)/shard_map/ppermute | solution.py:289
  8.8 52.8 %collective-permute-start.1 = (bf16[256,8,512]{2,1,0:T(8,128)(2,1)}, bf16[256,8,512]{2,1,0:T(8,128)(2,1)}, u32[]{:S(2)}, u32[]{:S(2)}) collective-permute-start(bf16[256,8,512]{2,1,0:T(8,128)(2,1)} %dynamic-slice_bitcast_fusion.1), channel_id=1, source_target_pairs={{0,4},{12,8},{1,5},{13,9},{2,6},{14,10},{3,7},{15,11},{16,20},{28,... | collective-permute-start | bytes 6291464 | tf_op jit(solution)/shard_map/ppermute | solution.py:290
  20.6 63.0 %collective-permute-start.3 = (bf16[256,4096]{1,0:T(8,128)(2,1)}, bf16[256,4096]{1,0:T(8,128)(2,1)}, u32[]{:S(2)}, u32[]{:S(2)}) collective-permute-start(bf16[256,4096]{1,0:T(8,128)(2,1)} %bitcast.20.other), channel_id=1, source_target_pairs={{4,8},{8,4},{5,9},{9,5},{6,10},{10,6},{7,11},{11,7},{20,24},{24,20... | collective-permute-start | bytes 6291464 | tf_op jit(solution)/shard_map/ppermute | solution.py:291
  25.2 81.2 %collective-permute-start.4 = (bf16[256,4096]{1,0:T(8,128)(2,1)S(1)}, bf16[256,4096]{1,0:T(8,128)(2,1)}, u32[]{:S(2)}, u32[]{:S(2)}) collective-permute-start(bf16[256,4096]{1,0:T(8,128)(2,1)S(1)} %bitcast.35), channel_id=1, source_target_pairs={{0,4},{12,8},{1,5},{13,9},{2,6},{14,10},{3,7},{15,11},{16,20},{28,... | collective-permute-start | bytes 6291464 | tf_op jit(solution)/shard_map/ppermute | solution.py:292
  65.5 86.0 %collective-permute-start.2 = (bf16[256,4096]{1,0:T(8,128)(2,1)}, bf16[256,4096]{1,0:T(8,128)(2,1)}, u32[]{:S(2)}, u32[]{:S(2)}) collective-permute-start(bf16[256,4096]{1,0:T(8,128)(2,1)} %bitcast.25.other), channel_id=1, source_target_pairs={{0,8},{12,4},{1,9},{13,5},{2,10},{14,6},{3,11},{15,7},{16,24},{28,... | collective-permute-start | bytes 6291464 | tf_op jit(solution)/shard_map/ppermute | solution.py:309
  115.3 4.8 %collective-permute-start.5 = (f32[2,768,256]{2,1,0:T(8,128)S(1)}, f32[2,768,256]{2,1,0:T(8,128)S(1)}, u32[]{:S(2)}, u32[]{:S(2)}) collective-permute-start(f32[2,768,256]{2,1,0:T(8,128)S(1)} %get-tuple-element.110), channel_id=1, source_target_pairs={{0,1},{1,0},{2,3},{3,2},{4,5},{5,4},{6,7},{7,6},{8,9},{9,8},{10,11... | collective-permute-start | bytes 4718600 | tf_op jit(solution)/shard_map/ppermute | solution.py:349
  115.4 52.9 %collective-permute-start.6 = (bf16[256,1536]{1,0:T(8,128)(2,1)S(1)}, bf16[256,1536]{1,0:T(8,128)(2,1)S(1)}, u32[]{:S(2)}, u32[]{:S(2)}) collective-permute-start(bf16[256,1536]{1,0:T(8,128)(2,1)S(1)} %copy-done.8), channel_id=1, source_target_pairs={{0,8},{12,4},{1,9},{13,5},{2,10},{14,6},{3,11},{15,7},{16,24},{28,... | collective-permute-start | bytes 2359304 | tf_op jit(solution)/shard_map/ppermute | solution.py:309
  151.5 25.3 %collective-permute-start.7 = (f32[768,256]{1,0:T(8,128)S(1)}, f32[768,256]{1,0:T(8,128)S(1)}, u32[]{:S(2)}, u32[]{:S(2)}) collective-permute-start(f32[768,256]{1,0:T(8,128)S(1)} %get-tuple-element.116), channel_id=1, source_target_pairs={{0,2},{2,0},{1,3},{3,1},{4,6},{6,4},{5,7},{7,5},{8,10},{10,8},{9,1... | collective-permute-start | bytes 2359304 | tf_op jit(solution)/shard_map/ppermute | solution.py:355
  153.0 42.6 %collective-permute-start.9 = (bf16[256,2048]{1,0:T(8,128)(2,1)S(1)}, bf16[256,2048]{1,0:T(8,128)(2,1)S(1)}, u32[]{:S(2)}, u32[]{:S(2)}) collective-permute-start(bf16[256,2048]{1,0:T(8,128)(2,1)S(1)} %copy-done.7), channel_id=1, source_target_pairs={{0,8},{12,4},{1,9},{13,5},{2,10},{14,6},{3,11},{15,7},{16,24},{28,... | collective-permute-start | bytes 3145736 | tf_op jit(solution)/shard_map/ppermute | solution.py:309
  181.8 8.8 %collective-permute-start.10 = (f32[4,16,1408]{2,1,0:T(8,128)S(1)}, f32[4,16,1408]{2,1,0:T(8,128)S(1)}, u32[]{:S(2)}, u32[]{:S(2)}) collective-permute-start(f32[4,16,1408]{2,1,0:T(8,128)S(1)} %get-tuple-element.130), channel_id=1, source_target_pairs={{0,2},{2,0},{1,3},{3,1},{4,6},{6,4},{5,7},{7,5},{8,10},{10,8},{9,1... | collective-permute-start | bytes 1081352 | tf_op jit(solution)/shard_map/ppermute | solution.py:321
  183.3 11.6 %collective-permute-start.8 = (bf16[256,512]{1,0:T(8,128)(2,1)S(1)}, bf16[256,512]{1,0:T(8,128)(2,1)S(1)}, u32[]{:S(2)}, u32[]{:S(2)}) collective-permute-start(bf16[256,512]{1,0:T(8,128)(2,1)S(1)} %slice.11), channel_id=1, source_target_pairs={{0,8},{12,4},{1,9},{13,5},{2,10},{14,6},{3,11},{15,7},{16,24},{28,... | collective-permute-start | bytes 786440 | tf_op jit(solution)/shard_map/ppermute | solution.py:309
  188.6 13.7 %collective-permute-start.11 = (f32[256,256]{1,0:T(8,128)S(1)}, f32[256,256]{1,0:T(8,128)S(1)}, u32[]{:S(2)}, u32[]{:S(2)}) collective-permute-start(f32[256,256]{1,0:T(8,128)S(1)} %get-tuple-element.138), channel_id=1, source_target_pairs={{4,0},{8,12},{5,1},{9,13},{6,2},{10,14},{7,3},{11,15},{20,16},{24,... | collective-permute-start | bytes 786440 | tf_op jit(solution)/shard_map/ppermute | solution.py:360
  189.9 12.4 %collective-permute-start.12 = (f32[256,256]{1,0:T(8,128)S(1)}, f32[256,256]{1,0:T(8,128)S(1)}, u32[]{:S(2)}, u32[]{:S(2)}) collective-permute-start(f32[256,256]{1,0:T(8,128)S(1)} %get-tuple-element.139), channel_id=1, source_target_pairs={{4,8},{8,4},{5,9},{9,5},{6,10},{10,6},{7,11},{11,7},{20,24},{24,20... | collective-permute-start | bytes 786440 | tf_op jit(solution)/shard_map/ppermute | solution.py:361
  191.2 11.1 %collective-permute-start.13 = (f32[16,1408]{1,0:T(8,128)S(1)}, f32[16,1408]{1,0:T(8,128)S(1)}, u32[]{:S(2)}, u32[]{:S(2)}) collective-permute-start(f32[16,1408]{1,0:T(8,128)S(1)} %get-tuple-element.131), channel_id=1, source_target_pairs={{4,0},{8,12},{5,1},{9,13},{6,2},{10,14},{7,3},{11,15},{20,16},{24,... | collective-permute-start | bytes 270344 | tf_op jit(solution)/shard_map/ppermute | solution.py:328
  194.9 7.4 %collective-permute-start.14 = (f32[16,1408]{1,0:T(8,128)S(1)}, f32[16,1408]{1,0:T(8,128)S(1)}, u32[]{:S(2)}, u32[]{:S(2)}) collective-permute-start(f32[16,1408]{1,0:T(8,128)S(1)} %get-tuple-element.133), channel_id=1, source_target_pairs={{4,8},{8,4},{5,9},{9,5},{6,10},{10,6},{7,11},{11,7},{20,24},{24,20... | collective-permute-start | bytes 270344 | tf_op jit(solution)/shard_map/ppermute | solution.py:330
  195.6 10.6 %collective-permute-start.15 = (f32[16,1408]{1,0:T(8,128)S(1)}, f32[16,1408]{1,0:T(8,128)S(1)}, u32[]{:S(2)}, u32[]{:S(2)}) collective-permute-start(f32[16,1408]{1,0:T(8,128)S(1)} %get-tuple-element.134), channel_id=1, source_target_pairs={{4,12},{8,0},{5,13},{9,1},{6,14},{10,2},{7,15},{11,3},{20,28},{24,... | collective-permute-start | bytes 270344 | tf_op jit(solution)/shard_map/ppermute | solution.py:331
  208.6 2.0 collective-permute-start.16
  211.2 6.4 %collective-permute-start.17 = (bf16[256,256]{1,0:T(8,128)(2,1)S(1)}, bf16[256,256]{1,0:T(8,128)(2,1)S(1)}, u32[]{:S(2)}, u32[]{:S(2)}) collective-permute-start(bf16[256,256]{1,0:T(8,128)(2,1)S(1)} %get-tuple-element.149), channel_id=1, source_target_pairs={{0,2},{2,0},{1,3},{3,1},{4,6},{6,4},{5,7},{7,5},{8,10},{10,8},{9,1... | collective-permute-start | bytes 393224 | tf_op jit(solution)/shard_map/ppermute | solution.py:384
  212.8 7.6 %collective-permute-start.20 = (f32[4,16,640]{2,1,0:T(8,128)S(1)}, f32[4,16,640]{2,1,0:T(8,128)S(1)}, u32[]{:S(2)}, u32[]{:S(2)}) collective-permute-start(f32[4,16,640]{2,1,0:T(8,128)S(1)} %get-tuple-element.157), channel_id=1, source_target_pairs={{0,2},{2,0},{1,3},{3,1},{4,6},{6,4},{5,7},{7,5},{8,10},{10,8},{9,1... | collective-permute-start | bytes 491528 | tf_op jit(solution)/shard_map/ppermute | solution.py:321
  218.3 15.2 %collective-permute-start.18 = (bf16[256,256]{1,0:T(8,128)(2,1)S(1)}, bf16[256,256]{1,0:T(8,128)(2,1)S(1)}, u32[]{:S(2)}, u32[]{:S(2)}) collective-permute-start(bf16[256,256]{1,0:T(8,128)(2,1)S(1)} %get-tuple-element.150), channel_id=1, source_target_pairs={{4,12},{8,0},{5,13},{9,1},{6,14},{10,2},{7,15},{11,3},{20,28},{24,... | collective-permute-start | bytes 393224 | tf_op jit(solution)/shard_map/ppermute | solution.py:388
  219.6 13.9 %collective-permute-start.19 = (bf16[256,256]{1,0:T(8,128)(2,1)S(1)}, bf16[256,256]{1,0:T(8,128)(2,1)S(1)}, u32[]{:S(2)}, u32[]{:S(2)}) collective-permute-start(bf16[256,256]{1,0:T(8,128)(2,1)S(1)} %get-tuple-element.151), channel_id=1, source_target_pairs={{4,3},{5,7},{6,11},{9,4},{10,8},{11,12},{20,19},{21,23},{22,27},{2... | collective-permute-start | bytes 393224 | tf_op jit(solution)/shard_map/ppermute | solution.py:389
  220.9 7.9 %collective-permute-start.21 = (bf16[16,640]{1,0:T(8,128)(2,1)S(1)}, bf16[16,640]{1,0:T(8,128)(2,1)S(1)}, u32[]{:S(2)}, u32[]{:S(2)}) collective-permute-start(bf16[16,640]{1,0:T(8,128)(2,1)S(1)} %get-tuple-element.158), channel_id=1, source_target_pairs={{4,0},{8,12},{5,1},{9,13},{6,2},{10,14},{7,3},{11,15},{20,16},{24,... | collective-permute-start | bytes 61448 | tf_op jit(solution)/shard_map/ppermute | solution.py:328
  222.2 6.6 %collective-permute-start.22 = (bf16[16,640]{1,0:T(8,128)(2,1)S(1)}, bf16[16,640]{1,0:T(8,128)(2,1)S(1)}, u32[]{:S(2)}, u32[]{:S(2)}) collective-permute-start(bf16[16,640]{1,0:T(8,128)(2,1)S(1)} %get-tuple-element.160), channel_id=1, source_target_pairs={{4,8},{8,4},{5,9},{9,5},{6,10},{10,6},{7,11},{11,7},{20,24},{24,20... | collective-permute-start | bytes 61448 | tf_op jit(solution)/shard_map/ppermute | solution.py:330
  222.9 10.6 %collective-permute-start.23 = (bf16[16,640]{1,0:T(8,128)(2,1)S(1)}, bf16[16,640]{1,0:T(8,128)(2,1)S(1)}, u32[]{:S(2)}, u32[]{:S(2)}) collective-permute-start(bf16[16,640]{1,0:T(8,128)(2,1)S(1)} %get-tuple-element.161), channel_id=1, source_target_pairs={{4,12},{8,0},{5,13},{9,1},{6,14},{10,2},{7,15},{11,3},{20,28},{24,... | collective-permute-start | bytes 61448 | tf_op jit(solution)/shard_map/ppermute | solution.py:331
  (10 other events, 297.2 us)

commit v3 on v2

--- a/solution.py
+++ b/solution.py
@@ -121,48 +121,83 @@
     second[...] = keep[1] + got[1]
 
 
-def add_rows_kernel(at, keep, got, *outs):
-    size = keep.shape[0] // len(outs)
-    for i, out in enumerate(outs):
-        out[...] = keep[i * size : (i + 1) * size] + got[i * size : (i + 1) * size]
-
-
-def add_home_kernel(at, keep, got, *outs):
-    for k, out in enumerate(outs):
-        out[...] = (keep[k] + got[k]).astype(out.dtype)
-
-
-def add_late_kernel(at, keep, got, stay, leave):
+def wrapped(cols, lanes):
+    return [(lo, min(lo + lanes, cols)) for lo in range(0, cols, lanes)]
+
+
+def lay(out, start, value):
+    few, lanes = value.shape[0], out.shape[1]
+    for i, (lo, hi) in enumerate(wrapped(value.shape[1], lanes)):
+        row = start + i * few
+        out[row : row + few, : hi - lo] = value[:, lo:hi].astype(out.dtype)
+
+
+def pick(laid, start, few, k):
+    row, lane = divmod(k * 128, laid.shape[1])
+    row = start + row * few
+    return laid[row : row + few, lane : lane + 128].astype(F32)
+
+
+def home_kernel(at, keep, got, core_keep, core_got, gram_own, to_near, kept, to_cross, to_far):
+    rows = gram_own.shape[0]
+    to_near[:rows] = (keep[:rows] + got[:rows]).astype(to_near.dtype)
+    gram_own[...] = keep[rows : 2 * rows] + got[rows : 2 * rows]
+    to_cross[:rows] = (keep[2 * rows :] + got[2 * rows :]).astype(to_cross.dtype)
+    lay(to_near, rows, core_keep[0] + core_got[0])
+    kept[...] = core_keep[1] + core_got[1]
+    lay(to_cross, rows, core_keep[2] + core_got[2])
+    lay(to_far, 0, core_keep[3] + core_got[3])
+
+
+def pack_kernel(at, keep, got, core_give, stay, leave):
+    rows = stay.shape[0]
     stay[...] = keep[0] + got[0]
-    leave[...] = (keep[1] + got[1]).astype(leave.dtype)
-
-
-def part_kernel(at, stay, got, late, turned):
-    total = stay[...] + got[...]
-    late[...] = total.astype(late.dtype)
+    leave[:rows] = (keep[1] + got[1]).astype(leave.dtype)
+    size = (leave.shape[0] - rows) // 4
+    for k in range(4):
+        lay(leave, rows + k * size, core_give[k])
+
+
+def part_kernel(at, stay, got, core_keep, near0, cross0, far0, to_far, turned, to_near, kept, to_cross):
+    rows = turned.shape[0]
+    total = stay[...] + got[:rows].astype(F32)
+    to_far[:rows] = total.astype(to_far.dtype)
     turned[...] = total.T.astype(turned.dtype)
-
-
-def final_kernel(inverse, at, gram_own, gram_near, gram_cross, late, turned, *rest):
-    *groups, gram, core = rest
+    laid = near0.shape[0]
+    to_near[:laid] = near0[...]
+    to_cross[:laid] = cross0[...]
+    to_far[rows:laid] = far0[...]
+    few, cols = core_keep.shape[1:]
+    size, lanes = kept.shape
+    for k, (out, start) in enumerate(((to_near, laid), (kept, 0), (to_cross, laid), (to_far, laid))):
+        for i, (lo, hi) in enumerate(wrapped(cols, lanes)):
+            row = i * few
+            other = got[rows + k * size + row : rows + k * size + row + few, : hi - lo]
+            out[start + row : start + row + few, : hi - lo] = (
+                core_keep[k, :, lo:hi] + other.astype(F32)
+            ).astype(out.dtype)
+
+
+def final_kernel(inverse, at, own, kept0, far, turned, near, kept1, cross, gram, core):
+    rows = own.shape[0]
     side, inner = at[2], at[3]
     gram[...] = (
-        (gram_own[...] + gram_near[...] + gram_cross[...])
-        + (late[...].astype(F32) + turned[...].astype(F32))
+        (own[...] + near[:rows].astype(F32) + cross[:rows].astype(F32))
+        + (far[:rows].astype(F32) + turned[...].astype(F32))
     ) * inverse
-    nz = core.shape[2]
+    few, nz = core.shape[0], core.shape[2]
     half = core.shape[1] // 2
-    mid = jnp.full((core.shape[0], 128), inner, jnp.int32) == 1
-    j = 0
-    for near, kept, cross, far in (groups[:4], groups[4:]):
-        for k in range(near.shape[1] // 128):
-            span = slice(k * 128, (k + 1) * 128)
-            mine = jnp.where(mid, kept[:, span], near[:, span].astype(F32))
-            other = cross[:, span].astype(F32) + far[:, span].astype(F32)
-            c, z = divmod(j, nz)
-            core[:, half * (1 - side) + c, z, :] = mine
-            core[:, half * side + c, z, :] = other
-            j += 1
+    early = kept0.shape[1] // 128
+    laid = near.shape[0] - kept1.shape[0]
+    mid = jnp.full((few, 128), inner, jnp.int32) == 1
+    for j in range(half * nz):
+        first = j < early
+        start, k = (rows, j) if first else (laid, j - early)
+        kept = kept0[:, k * 128 : (k + 1) * 128] if first else pick(kept1, 0, few, k)
+        mine = jnp.where(mid, kept, pick(near, start, few, k))
+        c, z = divmod(j, nz)
+        core[:, half * (1 - side) + c, z, :] = mine
+        core[:, half * side + c, z, :] = pick(cross, start, few, k) + pick(far, start, few, k)
 
 
 def pairs(at, near, own, cross, other, carried, last, ny):
@@ -232,11 +267,10 @@
                     out[(l >> 1) ^ gy] = acc[k] if k < 3 else jnp.zeros_like(acc[0])
 
 
-def meet(at, far, near, own, cross, lo, basis, y_own, carried, old, last):
-    rows, width = far.shape
+def meet(at, far, skip, n, near, own, cross, lo, basis, y_own, carried, old, last):
+    rows = far.shape[0]
     ny, s_cols = y_own.shape
     rank = basis.shape[1]
-    n = width // ny
     first, joined = carried is None, old is not None
     shifted = pl.BlockSpec((rows, ny), lambda j, at: (0, lo + j))
     acc_shape = (3, rows, rows)
@@ -246,7 +280,7 @@
         functools.partial(meet_kernel, first, last, joined),
         at,
         n,
-        [pl.BlockSpec((rows, ny), lambda j, at: (0, j)), shifted, shifted, shifted]
+        [pl.BlockSpec((rows, ny), lambda j, at: (0, skip + j)), shifted, shifted, shifted]
         + [whole(basis.shape), whole(y_own.shape)]
         + ([] if first else [whole(acc_shape)])
         + ([whole(o.shape) for o in old] if joined else []),
@@ -302,36 +336,38 @@
     basis = jnp.stack([lax.dynamic_slice_in_dim(x_basis, p * rows, rows, 0).T for p in places])
     y_own = lax.dynamic_slice_in_dim(y_basis, gy * ny, ny, 0)
 
-    cuts = [(0, 0, 8), (1, 0, 3), (1, 3, 7), (1, 7, 8)]
+    cuts = [(0, 9), (9, 14), (14, 16)]
+
+    def piece(lo, hi):
+        parts = []
+        for h in range(half):
+            a, b = max(lo, h * nz), min(hi, (h + 1) * nz)
+            if a < b:
+                parts.append(oth[h] if b - a == nz else oth[h][:, (a - h * nz) * ny : (b - h * nz) * ny])
+        return parts[0] if len(parts) == 1 else jnp.concatenate(parts, 1)
 
     def send_far(i, *gate):
         data, gate = tied((sends[i], gate))
         return lax.ppermute(data, "gx", FAR), *gate
 
     def meets(i, far, carried, old, last=False):
-        h, lo, _ = cuts[i]
-        return meet(at, far, near[h], own[h], cross[h], lo, basis, y_own, carried, old, last)
-
-    def across(core, link):
-        keep, give = core
-        return once(
-            "add_home",
-            add_home_kernel,
-            at,
-            [keep, lax.ppermute(give, "gy", SWAP)],
-            [keep.shape[1:]] * 4,
-            [link, F32, link, link],
-        )
-
-    def send_home(near, kept, cross, far):
-        return (
-            lax.ppermute(near, "gx", NEAR_BACK),
-            kept,
-            lax.ppermute(cross, "gx", CROSS),
-            lax.ppermute(far, "gx", FAR_BACK),
-        )
-
-    sends = [oth[0]] + [oth[1][:, lo * ny : hi * ny] for _, lo, hi in cuts[1:]]
+        lo, hi = cuts[i]
+        for h in range(half):
+            a, b = max(lo, h * nz), min(hi, (h + 1) * nz)
+            if a < b:
+                carried, *old = meet(
+                    at, far, a - lo, b - a, near[h], own[h], cross[h], a - h * nz,
+                    basis, y_own, carried, old, False
+                ) if not last else wrap_last(meet(
+                    at, far, a - lo, b - a, near[h], own[h], cross[h], a - h * nz,
+                    basis, y_own, carried, old, True
+                ))
+        return carried, *old
+
+    def wrap_last(outs):
+        return (outs[0], outs[1]), *outs[2:]
+
+    sends = [piece(lo, hi) for lo, hi in cuts]
     sends, cross_raw, own[0] = tied((sends, cross_raw, own[0]))
     cross[0] = flat(cross_raw)
     cross[0], near_raw = tied((cross[0], near_raw))
@@ -348,51 +384,60 @@
     early, leave = once(
         "add_split", add_split_kernel, at, [keep, lax.ppermute(give, "gz", SWAP)], [keep.shape[1:]] * 2
     )
-    far2, far0, leave = send_far(2, far0, leave)
-    far0, far1 = tied((far0, far1))
+    got = lax.ppermute(leave, "gy", SWAP)
+    far2, far0 = send_far(2, far0)
+    far0, got = tied((far0, got))
     acc, *core = meets(0, far0, None, None)
-    gram_near, gram_own, gram_cross = once(
-        "add_rows", add_rows_kernel, at, [early, lax.ppermute(leave, "gy", SWAP)], [(rows, rows)] * 3
-    )
-
-    far3, far1, gram_own, acc = send_far(3, far1, gram_own, acc)
-    acc, *core = meets(1, far1, acc, core)
-    gram_near = lax.ppermute(gram_near, "gx", NEAR_BACK)
-    gram_cross = lax.ppermute(gram_cross, "gx", CROSS)
-    blocks = across(core, F32)
-    home = send_home(*blocks)
-
-    far2, blocks = tied((far2, blocks))
-    acc, *core = meets(2, far2, acc, None)
-    far3, acc, gram_near, gram_cross, home = tied(
-        (far3, acc, gram_near, gram_cross, home)
-    )
-    keep, give, *core = meets(3, far3, acc, core, True)
+    core_got = lax.ppermute(core[1], "gy", SWAP)
+    few, cols = core_got.shape[1:]
+    laid = rows + few * len(wrapped(cols, rows))
+    home = once(
+        "home",
+        home_kernel,
+        at,
+        [early, got, core[0], core_got],
+        [(rows, rows), (laid, rows), (few, cols), (laid, rows), (laid - rows, rows)],
+        [F32, BF16, F32, BF16, BF16],
+    )
+    far1, acc, home = tied((far1, acc, home))
+    acc, *core = meets(1, far1, acc, None)
+    far2, acc, home = tied((far2, acc, home))
+    gram_own, near_home, kept_home, cross_home, far_home = home
+    (keep, give), *core = meets(2, far2, acc, core, True)
+
+    few, cols = core[0].shape[1:]
+    size = few * len(wrapped(cols, rows))
     stay, leave = once(
-        "add_late",
-        add_late_kernel,
-        at,
-        [keep, lax.ppermute(give, "gz", SWAP)],
-        [(rows, rows)] * 2,
+        "pack",
+        pack_kernel,
+        at,
+        [keep, lax.ppermute(give, "gz", SWAP), core[1]],
+        [(rows, rows), (rows + 4 * size, rows)],
         [F32, BF16],
     )
-    rest = send_home(*across(core, BF16))
-    late, turned = once(
+    full = laid + size
+    to_far, turned, to_near, kept, to_cross = once(
         "part",
         part_kernel,
         at,
-        [stay, lax.ppermute(leave, "gy", SWAP)],
-        [(rows, rows)] * 2,
-        [BF16] * 2,
-    )
-    late = lax.ppermute(late, "gx", FAR_BACK)
-    turned = lax.ppermute(turned, ("gx", "gy", "gz"), TURN)
+        [stay, lax.ppermute(leave, "gy", SWAP), core[0], near_home, cross_home, far_home],
+        [(full, rows), (rows, rows), (full, rows), (size, rows), (full, rows)],
+        [BF16, BF16, BF16, F32, BF16],
+    )
     return once(
         "final",
         functools.partial(final_kernel, inverse),
         at,
-        [gram_own, gram_near, gram_cross, late, turned, *home, *rest],
-        [(rows, rows), (rank // 8, ncomp, nz, y_basis.shape[1])],
+        [
+            gram_own,
+            kept_home,
+            lax.ppermute(to_far, "gx", FAR_BACK),
+            lax.ppermute(turned, ("gx", "gy", "gz"), TURN),
+            lax.ppermute(to_near, "gx", NEAR_BACK),
+            kept,
+            lax.ppermute(to_cross, "gx", CROSS),
+        ],
+        [(rows, rows), (few, ncomp, nz, y_basis.shape[1])],
     )
 
 

time: 236 us -> 227 us (0.962)
  starting transfers between devices: 51.2 us -> 38.6 us
  local copies, waits for them, and re-layouts: 38.8 us -> 44.4 us
  waiting for transfers between devices: 102 us -> 97.5 us
  other arithmetic: 0.11 us -> 4.21 us
  Pallas kernels: 42.3 us -> 39.6 us
    ppermute x1, waiting for transfers between devices: 16.3 us -> 8.26 us  [meeting(): near_raw = lax.ppermute(own_raw, 'gx', NEAR)]
    unnamed x30, local copies, waits for them, and re-layouts: 23.8 us -> 29.5 us
    ppermute x12 -> x6, starting transfers between devices: 12.7 us -> 6.99 us  [the longest x1 1.55 us: meeting(): got = lax.ppermute(leave, 'gy', SWAP)]
    ppermute x4 -> x3, starting transfers between devices: 20.9 us -> 15.6 us  [send_far(): return (lax.ppermute(data, 'gx', FAR), *gate)]
    concatenate x0 -> x1, other arithmetic: none -> 3.16 us  [piece(): return parts[0] if len(parts) == 1 else jnp.concatenate(parts, 1)]
    pallas_call x13 -> x11, Pallas kernels: 42.3 us -> 39.6 us  [call(): pl.pallas_call(kernel, out_shape=tuple((jax.ShapeDtypeStruct(o, t) for o,...]
    ppermute x2 -> x1, waiting for transfers between devices: 4.32 us -> 6.87 us  [meeting(): lax.ppermute(leave, 'gy', SWAP)]
    ppermute x12 -> x6, waiting for transfers between devices: 13.2 us -> 14.9 us  [the longest x1 6.23 us: meeting(): lax.ppermute(to_far, 'gx', FAR_BACK)]
  transfers between devices with their start and end apart: 24 -> 16, of which waited for: 11 -> 10; matrix products, arithmetic and copies ran while one was open for 13% -> 17% of each run, Pallas kernels for 16% -> 15%
where the time goes in v3:
time: 227 us; the launch traced here: 225 us
  waiting for transfers between devices  97.5 us (43%)
  local copies, waits for them, and re-layouts  44.4 us (20%)
  Pallas kernels  39.6 us (17%)
  starting transfers between devices  38.6 us (17%)
  other arithmetic  4.21 us (2%)
    ppermute x3, waiting for transfers between devices, send_far(): return (lax.ppermute(data, 'gx', FAR), *gate)  42.4 us
    pallas_call x11, Pallas kernels, call(): pl.pallas_call(kernel, out_shape=tuple((jax.ShapeDtypeStruct(o, t) for o,...  39.6 us
    unnamed x30, local copies, waits for them, and re-layouts  29.5 us
    ppermute x1, waiting for transfers between devices, meeting(): near[1] = lax.ppermute(own[1], 'gx', NEAR)  23.1 us
    ppermute x3, starting transfers between devices, send_far(): return (lax.ppermute(data, 'gx', FAR), *gate)  15.6 us
    ppermute x1, waiting for transfers between devices, meeting(): near_raw = lax.ppermute(own_raw, 'gx', NEAR)  8.26 us
    reshape x3, local copies, waits for them, and re-layouts, take(): return lax.dynamic_slice_in_dim(source, start, 1, 1).reshape(rows, nz, ny)  7.93 us
    ppermute x1, starting transfers between devices, meeting(): near_raw = lax.ppermute(own_raw, 'gx', NEAR)  7.75 us
  transfers between devices with their start and end apart: 16, of which 10 were waited for; matrix products, arithmetic and copies ran while one was open for 17% of the time, Pallas kernels for 15%

profile of v3, /device:TPU:0, one launch (start us, length us, event | category | flops | bytes accessed | tf_op | source)
XLA Modules:
  0.0 225.2 jit_solution(10782195856726469910)
XLA Ops:
  0.7 3.1 %dynamic-slice_bitcast_fusion.2 = bf16[256,8,512]{2,1,0:T(8,128)(2,1)} fusion(bf16[256,4,8,512]{3,2,1,0:T(8,128)(2,1)} %param.3, s32[]{:T(128)S(6)} %select_n.43), kind=kLoop, calls=%fused_computation.3 | loop fusion | bytes 4194308 | tf_op jit(solution)/shard_map/reshape | solution.py:310
  8.8 7.7 %collective-permute-start.1 = (bf16[256,8,512]{2,1,0:T(8,128)(2,1)}, bf16[256,8,512]{2,1,0:T(8,128)(2,1)}, u32[]{:S(2)}, u32[]{:S(2)}) collective-permute-start(bf16[256,8,512]{2,1,0:T(8,128)(2,1)} %dynamic-slice_bitcast_fusion.1), channel_id=1, source_target_pairs={{0,4},{12,8},{1,5},{13,9},{2,6},{14,10},{3,7},{15,11},{16,20},{28,... | collective-permute-start | bytes 6291464 | tf_op jit(solution)/shard_map/ppermute | solution.py:324
  32.4 3.8 %copy.15 = bf16[32,8,8,512]{3,1,2,0:T(8,128)(2,1)} copy(bf16[32,8,8,512]{3,2,1,0:T(8,128)(2,1)} %bitcast.24) | data formatting | bytes 4194304
  36.2 3.9 %copy.16 = bf16[32,8,8,512]{3,1,2,0:T(8,128)(2,1)} copy(bf16[32,8,8,512]{3,2,1,0:T(8,128)(2,1)} %bitcast.26) | data formatting | bytes 4194304
  46.4 3.2 %pad_maximum_fusion = bf16[256,4608]{1,0:T(8,128)(2,1)} fusion(bf16[256,512]{1,0:T(8,128)(2,1)S(1)} %slice.9, bf16[256,4096]{1,0:T(8,128)(2,1)} %bitcast.46), kind=kLoop, calls=%fused_computation | loop fusion | flops 4718592 | bytes 4718592 | tf_op jit(solution)/shard_map/concatenate | solution.py:347
  49.6 3.8 %copy.17 = bf16[32,8,8,512]{3,1,2,0:T(8,128)(2,1)} copy(bf16[32,8,8,512]{3,2,1,0:T(8,128)(2,1)} %bitcast.28) | data formatting | bytes 4194304
  53.4 8.3 %collective-permute-done.1 = bf16[256,8,512]{2,1,0:T(8,128)(2,1)} collective-permute-done((bf16[256,8,512]{2,1,0:T(8,128)(2,1)}, bf16[256,8,512]{2,1,0:T(8,128)(2,1)}, u32[]{:S(2)}, u32[]{:S(2)}) %collective-permute-start.1) | collective-permute-done | bytes 2097184 | tf_op jit(solution)/shard_map/ppermute | solution.py:324
  61.7 3.8 %copy.18 = bf16[32,8,8,512]{3,1,2,0:T(8,128)(2,1)} copy(bf16[32,8,8,512]{3,2,1,0:T(8,128)(2,1)} %bitcast.30) | data formatting | bytes 4194304
  65.5 5.7 %collective-permute-start.2 = (bf16[256,4608]{1,0:T(8,128)(2,1)}, bf16[256,4608]{1,0:T(8,128)(2,1)}, u32[]{:S(2)}, u32[]{:S(2)}) collective-permute-start(bf16[256,4608]{1,0:T(8,128)(2,1)} %pad_maximum_fusion), channel_id=1, source_target_pairs={{0,8},{12,4},{1,9},{13,5},{2,10},{14,6},{3,11},{15,7},{16,24},{28,... | collective-permute-start | bytes 7077896 | tf_op jit(solution)/shard_map/ppermute | solution.py:351
  77.6 5.7 %pairs.2.rest_0_ = f32[4,256,256]{2,1,0:T(8,128)S(1)} custom-call(s32[4]{0:T(128)S(1)} %pad_add_fusion.at, bf16[256,4096]{1,0:T(8,128)(2,1)S(1)} %bitcast.44, bf16[256,4096]{1,0:T(8,128)(2,1)S(1)} %bitcast.40, bf16[256,4096]{1,0:T(8,128)(2,1)S(1)} %bitcast.42, bf16[256,4096]{1,0:T(8,128)(2,1)S(1)} %bitcast.47), custom_call_target="tpu_custom_call" | custom-call | flops 1 | bytes 1 | tf_op jit(solution)/shard_map/pairs/pallas_call | solution.py:98
  83.4 23.1 %collective-permute-done.5.near = bf16[256,4096]{1,0:T(8,128)(2,1)} collective-permute-done((bf16[256,4096]{1,0:T(8,128)(2,1)S(1)}, bf16[256,4096]{1,0:T(8,128)(2,1)}, u32[]{:S(2)}, u32[]{:S(2)}) %collective-permute-start.5) | collective-permute-done | bytes 2097184 | tf_op jit(solution)/shard_map/ppermute | solution.py:326
  106.5 8.8 %pairs.3 = (f32[2,768,256]{2,1,0:T(8,128)S(1)}, f32[2,768,256]{2,1,0:T(8,128)S(1)}) custom-call(s32[4]{0:T(128)S(1)} %pad_add_fusion.at, bf16[256,4096]{1,0:T(8,128)(2,1)} %collective-permute-done.5.near, bf16[256,4096]{1,0:T(8,128)(2,1)S(1)} %bitcast.36, bf16[256,4096]{1,0:T(8,128)(2,1)} %collective-permute-done.4.cross, bf16[256,4096]{1,0:T(8,128)(2,1)} %bitcast.20.other, ...), custom_call_target="tpu_custom_call" | custom-call | flops 1 | bytes 1 | tf_op jit(solution)/shard_map/pairs/pallas_call | solution.py:98
  115.4 4.6 %collective-permute-start.6 = (bf16[256,2560]{1,0:T(8,128)(2,1)S(1)}, bf16[256,2560]{1,0:T(8,128)(2,1)S(1)}, u32[]{:S(2)}, u32[]{:S(2)}) collective-permute-start(bf16[256,2560]{1,0:T(8,128)(2,1)S(1)} %copy-done.8), channel_id=1, source_target_pairs={{0,8},{12,4},{1,9},{13,5},{2,10},{14,6},{3,11},{15,7},{16,24},{28,... | collective-permute-start | bytes 3932168 | tf_op jit(solution)/shard_map/ppermute | solution.py:351
  122.3 34.9 %collective-permute-done.2.far = bf16[256,4608]{1,0:T(8,128)(2,1)} collective-permute-done((bf16[256,4608]{1,0:T(8,128)(2,1)}, bf16[256,4608]{1,0:T(8,128)(2,1)}, u32[]{:S(2)}, u32[]{:S(2)}) %collective-permute-start.2) | collective-permute-done | bytes 2359328 | tf_op jit(solution)/shard_map/ppermute | solution.py:351
  157.2 5.3 %collective-permute-start.3 = (bf16[256,1024]{1,0:T(8,128)(2,1)S(1)}, bf16[256,1024]{1,0:T(8,128)(2,1)S(1)}, u32[]{:S(2)}, u32[]{:S(2)}) collective-permute-start(bf16[256,1024]{1,0:T(8,128)(2,1)S(1)} %slice.11), channel_id=1, source_target_pairs={{0,8},{12,4},{1,9},{13,5},{2,10},{14,6},{3,11},{15,7},{16,24},{28,... | collective-permute-start | bytes 1572872 | tf_op jit(solution)/shard_map/ppermute | solution.py:351
  162.5 8.5 %meet.4 = (f32[3,256,256]{2,1,0:T(8,128)S(1)}, f32[4,16,1024]{2,1,0:T(8,128)S(1)}, f32[4,16,1024]{2,1,0:T(8,128)S(1)}) custom-call(s32[4]{0:T(128)S(1)} %pad_add_fusion.at, bf16[256,4608]{1,0:T(8,128)(2,1)} %collective-permute-done.2.far, bf16[256,4096]{1,0:T(8,128)(2,1)S(1)} %bitcast.45, bf16[256,4096]{1,0:T(8,128)(2,1)S(1)} %bitcast.41, ...), custom_call_target="tpu_custom_call" | custom-call | flops 1 | bytes 1 | tf_op jit(solution)/shard_map/meet/pallas_call | solution.py:98
  175.2 5.3 %collective-permute-done.9.core_got = f32[4,16,1152]{2,1,0:T(8,128)S(1)} collective-permute-done((f32[4,16,1152]{2,1,0:T(8,128)S(1)}, f32[4,16,1152]{2,1,0:T(8,128)S(1)}, u32[]{:S(2)}, u32[]{:S(2)}) %collective-permute-start.9) | collective-permute-done | bytes 294944 | tf_op jit(solution)/shard_map/ppermute | solution.py:391
  181.2 4.0 %collective-permute-done.6.far = bf16[256,2560]{1,0:T(8,128)(2,1)S(1)} collective-permute-done((bf16[256,2560]{1,0:T(8,128)(2,1)S(1)}, bf16[256,2560]{1,0:T(8,128)(2,1)S(1)}, u32[]{:S(2)}, u32[]{:S(2)}) %collective-permute-start.6) | collective-permute-done | bytes 1310752 | tf_op jit(solution)/shard_map/ppermute | solution.py:351
  185.2 6.2 %meet.6 = (f32[3,256,256]{2,1,0:T(8,128)S(1)}, f32[4,16,640]{2,1,0:T(8,128)S(1)}, f32[4,16,640]{2,1,0:T(8,128)S(1)}) custom-call(s32[4]{0:T(128)S(1)} %pad_add_fusion.at, bf16[256,2560]{1,0:T(8,128)(2,1)S(1)} %collective-permute-done.6.far, bf16[256,4096]{1,0:T(8,128)(2,1)} %collective-permute-done.5.near, bf16[256,4096]{1,0:T(8,128)(2,1)S(1)} %bitcast.38, ...), custom_call_target="tpu_custom_call" | custom-call | flops 1 | bytes 1 | tf_op jit(solution)/shard_map/meet/pallas_call | solution.py:98
  191.4 3.6 %collective-permute-done.3.far = bf16[256,1024]{1,0:T(8,128)(2,1)S(1)} collective-permute-done((bf16[256,1024]{1,0:T(8,128)(2,1)S(1)}, bf16[256,1024]{1,0:T(8,128)(2,1)S(1)}, u32[]{:S(2)}, u32[]{:S(2)}) %collective-permute-start.3) | collective-permute-done | bytes 524320 | tf_op jit(solution)/shard_map/ppermute | solution.py:351
  194.9 3.4 %meet.7 = (f32[2,256,256]{2,1,0:T(8,128)S(1)}, f32[2,256,256]{2,1,0:T(8,128)S(1)}, f32[4,16,896]{2,1,0:T(8,128)S(1)}, f32[4,16,896]{2,1,0:T(8,128)S(1)}) custom-call(s32[4]{0:T(128)S(1)} %pad_add_fusion.at, bf16[256,1024]{1,0:T(8,128)(2,1)S(1)} %collective-permute-done.3.far, bf16[256,4096]{1,0:T(8,128)(2,1)} %collective-permute-done.5.near, ...), custom_call_target="tpu_custom_call" | custom-call | flops 1 | bytes 1 | tf_op jit(solution)/shard_map/meet/pallas_call | solution.py:98
  202.5 6.9 %collective-permute-done.11.got = bf16[512,256]{1,0:T(8,128)(2,1)S(1)} collective-permute-done((bf16[512,256]{1,0:T(8,128)(2,1)S(1)}, bf16[512,256]{1,0:T(8,128)(2,1)S(1)}, u32[]{:S(2)}, u32[]{:S(2)}) %collective-permute-start.11) | collective-permute-done | bytes 262176 | tf_op jit(solution)/shard_map/ppermute | solution.py:423
  214.0 6.2 %collective-permute-done.12.far = bf16[400,256]{1,0:T(8,128)(2,1)S(1)} collective-permute-done((bf16[400,256]{1,0:T(8,128)(2,1)S(1)}, bf16[400,256]{1,0:T(8,128)(2,1)S(1)}, u32[]{:S(2)}, u32[]{:S(2)}) %collective-permute-start.12) | collective-permute-done | bytes 204832 | tf_op jit(solution)/shard_map/ppermute | solution.py:434
  220.2 3.4 %collective-permute-done.14.near = bf16[400,256]{1,0:T(8,128)(2,1)S(1)} collective-permute-done((bf16[400,256]{1,0:T(8,128)(2,1)S(1)}, bf16[400,256]{1,0:T(8,128)(2,1)S(1)}, u32[]{:S(2)}, u32[]{:S(2)}) %collective-permute-start.14) | collective-permute-done | bytes 204832 | tf_op jit(solution)/shard_map/ppermute | solution.py:436
  (61 shorter events, 51.1 us)
Async XLA Ops:
  0.6 44.8 %copy-start = (bf16[1024,128]{1,0:T(8,128)(2,1)S(1)}, bf16[1024,128]{1,0:T(8,128)(2,1)}, u32[]{:S(2)}) copy-start(bf16[1024,128]{1,0:T(8,128)(2,1)} %param.5) | copy-start | bytes 786436
  3.8 45.8 %collective-permute-start = (bf16[256,8,512]{2,1,0:T(8,128)(2,1)}, bf16[256,8,512]{2,1,0:T(8,128)(2,1)}, u32[]{:S(2)}, u32[]{:S(2)}) collective-permute-start(bf16[256,8,512]{2,1,0:T(8,128)(2,1)} %dynamic-slice_bitcast_fusion.2), channel_id=1, source_target_pairs={{4,8},{8,4},{5,9},{9,5},{6,10},{10,6},{7,11},{11,7},{20,24},{24,20... | collective-permute-start | bytes 6291464 | tf_op jit(solution)/shard_map/ppermute | solution.py:323
  8.8 52.8 %collective-permute-start.1 = (bf16[256,8,512]{2,1,0:T(8,128)(2,1)}, bf16[256,8,512]{2,1,0:T(8,128)(2,1)}, u32[]{:S(2)}, u32[]{:S(2)}) collective-permute-start(bf16[256,8,512]{2,1,0:T(8,128)(2,1)} %dynamic-slice_bitcast_fusion.1), channel_id=1, source_target_pairs={{0,4},{12,8},{1,5},{13,9},{2,6},{14,10},{3,7},{15,11},{16,20},{28,... | collective-permute-start | bytes 6291464 | tf_op jit(solution)/shard_map/ppermute | solution.py:324
  20.6 62.8 %collective-permute-start.4 = (bf16[256,4096]{1,0:T(8,128)(2,1)}, bf16[256,4096]{1,0:T(8,128)(2,1)}, u32[]{:S(2)}, u32[]{:S(2)}) collective-permute-start(bf16[256,4096]{1,0:T(8,128)(2,1)} %bitcast.20.other), channel_id=1, source_target_pairs={{4,8},{8,4},{5,9},{9,5},{6,10},{10,6},{7,11},{11,7},{20,24},{24,20... | collective-permute-start | bytes 6291464 | tf_op jit(solution)/shard_map/ppermute | solution.py:325
  25.2 81.3 %collective-permute-start.5 = (bf16[256,4096]{1,0:T(8,128)(2,1)S(1)}, bf16[256,4096]{1,0:T(8,128)(2,1)}, u32[]{:S(2)}, u32[]{:S(2)}) collective-permute-start(bf16[256,4096]{1,0:T(8,128)(2,1)S(1)} %bitcast.35), channel_id=1, source_target_pairs={{0,4},{12,8},{1,5},{13,9},{2,6},{14,10},{3,7},{15,11},{16,20},{28,... | collective-permute-start | bytes 6291464 | tf_op jit(solution)/shard_map/ppermute | solution.py:326
  36.2 3.9 %copy-start.9 = (bf16[1024,128]{1,0:T(8,128)(2,1)S(1)}, bf16[1024,128]{1,0:T(8,128)(2,1)}, u32[]{:S(2)}) copy-start(bf16[1024,128]{1,0:T(8,128)(2,1)} %param.4) | copy-start | bytes 786436
  65.5 91.7 %collective-permute-start.2 = (bf16[256,4608]{1,0:T(8,128)(2,1)}, bf16[256,4608]{1,0:T(8,128)(2,1)}, u32[]{:S(2)}, u32[]{:S(2)}) collective-permute-start(bf16[256,4608]{1,0:T(8,128)(2,1)} %pad_maximum_fusion), channel_id=1, source_target_pairs={{0,8},{12,4},{1,9},{13,5},{2,10},{14,6},{3,11},{15,7},{16,24},{28,... | collective-permute-start | bytes 7077896 | tf_op jit(solution)/shard_map/ppermute | solution.py:351
  71.2 1.6 copy-start.1
  72.8 1.6 copy-start.3
  83.3 32.0 %copy-start.8 = (bf16[256,2560]{1,0:T(8,128)(2,1)S(1)}, bf16[256,2560]{1,0:T(8,128)(2,1)}, u32[]{:S(2)}) copy-start(bf16[256,2560]{1,0:T(8,128)(2,1)} %slice.10) | copy-start | bytes 3932164
  106.5 56.0 %copy-start.4 = (bf16[32,8,8,512]{3,1,2,0:T(8,128)(2,1)S(1)}, bf16[32,8,8,512]{3,1,2,0:T(8,128)(2,1)}, u32[]{:S(2)}) copy-start(bf16[32,8,8,512]{3,1,2,0:T(8,128)(2,1)} %copy.17) | copy-start | bytes 6291460
  106.5 56.0 %copy-start.6 = (bf16[32,8,8,512]{3,1,2,0:T(8,128)(2,1)S(1)}, bf16[32,8,8,512]{3,1,2,0:T(8,128)(2,1)}, u32[]{:S(2)}) copy-start(bf16[32,8,8,512]{3,1,2,0:T(8,128)(2,1)} %copy.18) | copy-start | bytes 6291460
  115.3 47.2 %copy-start.2 = (bf16[32,8,8,512]{3,1,2,0:T(8,128)(2,1)S(1)}, bf16[32,8,8,512]{3,1,2,0:T(8,128)(2,1)}, u32[]{:S(2)}) copy-start(bf16[32,8,8,512]{3,1,2,0:T(8,128)(2,1)} %copy.16) | copy-start | bytes 6291460
  115.3 4.7 %collective-permute-start.7 = (f32[2,768,256]{2,1,0:T(8,128)S(1)}, f32[2,768,256]{2,1,0:T(8,128)S(1)}, u32[]{:S(2)}, u32[]{:S(2)}) collective-permute-start(f32[2,768,256]{2,1,0:T(8,128)S(1)} %get-tuple-element.108), channel_id=1, source_target_pairs={{0,1},{1,0},{2,3},{3,2},{4,5},{5,4},{6,7},{7,6},{8,9},{9,8},{10,11... | collective-permute-start | bytes 4718600 | tf_op jit(solution)/shard_map/ppermute | solution.py:385
  115.4 69.7 %collective-permute-start.6 = (bf16[256,2560]{1,0:T(8,128)(2,1)S(1)}, bf16[256,2560]{1,0:T(8,128)(2,1)S(1)}, u32[]{:S(2)}, u32[]{:S(2)}) collective-permute-start(bf16[256,2560]{1,0:T(8,128)(2,1)S(1)} %copy-done.8), channel_id=1, source_target_pairs={{0,8},{12,4},{1,9},{13,5},{2,10},{14,6},{3,11},{15,7},{16,24},{28,... | collective-permute-start | bytes 3932168 | tf_op jit(solution)/shard_map/ppermute | solution.py:351
  120.7 41.7 %collective-permute-start.8 = (f32[768,256]{1,0:T(8,128)S(1)}, f32[768,256]{1,0:T(8,128)S(1)}, u32[]{:S(2)}, u32[]{:S(2)}) collective-permute-start(f32[768,256]{1,0:T(8,128)S(1)} %get-tuple-element.109), channel_id=1, source_target_pairs={{0,2},{2,0},{1,3},{3,1},{4,6},{6,4},{5,7},{7,5},{8,10},{10,8},{9,1... | collective-permute-start | bytes 2359304 | tf_op jit(solution)/shard_map/ppermute | solution.py:387
  157.2 37.8 %collective-permute-start.3 = (bf16[256,1024]{1,0:T(8,128)(2,1)S(1)}, bf16[256,1024]{1,0:T(8,128)(2,1)S(1)}, u32[]{:S(2)}, u32[]{:S(2)}) collective-permute-start(bf16[256,1024]{1,0:T(8,128)(2,1)S(1)} %slice.11), channel_id=1, source_target_pairs={{0,8},{12,4},{1,9},{13,5},{2,10},{14,6},{3,11},{15,7},{16,24},{28,... | collective-permute-start | bytes 1572872 | tf_op jit(solution)/shard_map/ppermute | solution.py:351
  173.7 6.8 %collective-permute-start.9 = (f32[4,16,1152]{2,1,0:T(8,128)S(1)}, f32[4,16,1152]{2,1,0:T(8,128)S(1)}, u32[]{:S(2)}, u32[]{:S(2)}) collective-permute-start(f32[4,16,1152]{2,1,0:T(8,128)S(1)} %get-tuple-element.120), channel_id=1, source_target_pairs={{0,2},{2,0},{1,3},{3,1},{4,6},{6,4},{5,7},{7,5},{8,10},{10,8},{9,1... | collective-permute-start | bytes 884744 | tf_op jit(solution)/shard_map/ppermute | solution.py:391
  198.3 2.0 collective-permute-start.10
  200.9 8.4 %collective-permute-start.11 = (bf16[512,256]{1,0:T(8,128)(2,1)S(1)}, bf16[512,256]{1,0:T(8,128)(2,1)S(1)}, u32[]{:S(2)}, u32[]{:S(2)}) collective-permute-start(bf16[512,256]{1,0:T(8,128)(2,1)S(1)} %get-tuple-element.144), channel_id=1, source_target_pairs={{0,2},{2,0},{1,3},{3,1},{4,6},{6,4},{5,7},{7,5},{8,10},{10,8},{9,1... | collective-permute-start | bytes 786440 | tf_op jit(solution)/shard_map/ppermute | solution.py:423
  210.0 10.2 %collective-permute-start.12 = (bf16[400,256]{1,0:T(8,128)(2,1)S(1)}, bf16[400,256]{1,0:T(8,128)(2,1)S(1)}, u32[]{:S(2)}, u32[]{:S(2)}) collective-permute-start(bf16[400,256]{1,0:T(8,128)(2,1)S(1)} %get-tuple-element.149), channel_id=1, source_target_pairs={{4,12},{8,0},{5,13},{9,1},{6,14},{10,2},{7,15},{11,3},{20,28},{24,... | collective-permute-start | bytes 614408 | tf_op jit(solution)/shard_map/ppermute | solution.py:434
  211.3 12.3 %collective-permute-start.14 = (bf16[400,256]{1,0:T(8,128)(2,1)S(1)}, bf16[400,256]{1,0:T(8,128)(2,1)S(1)}, u32[]{:S(2)}, u32[]{:S(2)}) collective-permute-start(bf16[400,256]{1,0:T(8,128)(2,1)S(1)} %get-tuple-element.151), channel_id=1, source_target_pairs={{4,0},{8,12},{5,1},{9,13},{6,2},{10,14},{7,3},{11,15},{20,16},{24,... | collective-permute-start | bytes 614408 | tf_op jit(solution)/shard_map/ppermute | solution.py:436
  212.6 11.0 %collective-permute-start.15 = (bf16[400,256]{1,0:T(8,128)(2,1)S(1)}, bf16[400,256]{1,0:T(8,128)(2,1)S(1)}, u32[]{:S(2)}, u32[]{:S(2)}) collective-permute-start(bf16[400,256]{1,0:T(8,128)(2,1)S(1)} %get-tuple-element.153), channel_id=1, source_target_pairs={{4,8},{8,4},{5,9},{9,5},{6,10},{10,6},{7,11},{11,7},{20,24},{24,20... | collective-permute-start | bytes 614408 | tf_op jit(solution)/shard_map/ppermute | solution.py:438
  213.3 0.7 collective-permute-start.13
  (2 other events, 3.2 us)

commit v4 on v3

--- a/solution.py
+++ b/solution.py
@@ -149,55 +149,52 @@
     lay(to_far, 0, core_keep[3] + core_got[3])
 
 
-def pack_kernel(at, keep, got, core_give, stay, leave):
-    rows = stay.shape[0]
+def add_late_kernel(at, keep, got, stay, leave):
     stay[...] = keep[0] + got[0]
-    leave[:rows] = (keep[1] + got[1]).astype(leave.dtype)
-    size = (leave.shape[0] - rows) // 4
-    for k in range(4):
-        lay(leave, rows + k * size, core_give[k])
-
-
-def part_kernel(at, stay, got, core_keep, near0, cross0, far0, to_far, turned, to_near, kept, to_cross):
+    leave[...] = (keep[1] + got[1]).astype(leave.dtype)
+
+
+def join_kernel(at, keep, got, near0, to_near, kept, to_cross):
+    laid = near0.shape[0]
+    to_near[:laid] = near0[...]
+    lay(to_near, laid, keep[0] + got[0])
+    kept[...] = keep[1] + got[1]
+    lay(to_cross, 0, keep[2] + got[2])
+
+
+def part_kernel(at, stay, got, core_keep, core_got, far0, to_far, turned):
     rows = turned.shape[0]
-    total = stay[...] + got[:rows].astype(F32)
+    total = stay[...] + got[...].astype(F32)
     to_far[:rows] = total.astype(to_far.dtype)
     turned[...] = total.T.astype(turned.dtype)
-    laid = near0.shape[0]
-    to_near[:laid] = near0[...]
-    to_cross[:laid] = cross0[...]
+    laid = rows + far0.shape[0]
     to_far[rows:laid] = far0[...]
-    few, cols = core_keep.shape[1:]
-    size, lanes = kept.shape
-    for k, (out, start) in enumerate(((to_near, laid), (kept, 0), (to_cross, laid), (to_far, laid))):
-        for i, (lo, hi) in enumerate(wrapped(cols, lanes)):
-            row = i * few
-            other = got[rows + k * size + row : rows + k * size + row + few, : hi - lo]
-            out[start + row : start + row + few, : hi - lo] = (
-                core_keep[k, :, lo:hi] + other.astype(F32)
-            ).astype(out.dtype)
-
-
-def final_kernel(inverse, at, own, kept0, far, turned, near, kept1, cross, gram, core):
+    lay(to_far, laid, core_keep[3] + core_got[3])
+
+
+def final_kernel(inverse, at, own, kept0, far, turned, near, kept1, cross0, cross1, gram, core):
     rows = own.shape[0]
     side, inner = at[2], at[3]
     gram[...] = (
-        (own[...] + near[:rows].astype(F32) + cross[:rows].astype(F32))
+        (own[...] + near[:rows].astype(F32) + cross0[:rows].astype(F32))
         + (far[:rows].astype(F32) + turned[...].astype(F32))
     ) * inverse
     few, nz = core.shape[0], core.shape[2]
     half = core.shape[1] // 2
     early = kept0.shape[1] // 128
-    laid = near.shape[0] - kept1.shape[0]
+    few_cols = kept1.shape[1]
+    size = few * len(wrapped(few_cols, rows))
+    laid = near.shape[0] - size
     mid = jnp.full((few, 128), inner, jnp.int32) == 1
     for j in range(half * nz):
         first = j < early
         start, k = (rows, j) if first else (laid, j - early)
-        kept = kept0[:, k * 128 : (k + 1) * 128] if first else pick(kept1, 0, few, k)
+        kept = (kept0 if first else kept1)[:, k * 128 : (k + 1) * 128]
         mine = jnp.where(mid, kept, pick(near, start, few, k))
         c, z = divmod(j, nz)
         core[:, half * (1 - side) + c, z, :] = mine
-        core[:, half * side + c, z, :] = pick(cross, start, few, k) + pick(far, start, few, k)
+        cross = pick(cross0, rows, few, k) if first else pick(cross1, 0, few, k)
+        core[:, half * side + c, z, :] = cross + pick(far, start, few, k)
 
 
 def pairs(at, near, own, cross, other, carried, last, ny):
@@ -313,10 +310,8 @@
         return a.reshape(rows, width)
 
     near, cross, own, oth = ([None] * half for _ in range(4))
-    oth_raw = take(snapshot, oth_at)
-    source, oth_raw = tied((snapshot, oth_raw))
-    own_raw = take(source, own_at)
-    source, own_raw = tied((source, own_raw))
+    oth_raw, own_raw = take(snapshot, oth_at), take(snapshot, own_at)
+    source, oth_raw, own_raw = tied((snapshot, oth_raw, own_raw))
     oth_late = take(source, oth_at + 1)
     source, oth_late = tied((source, oth_late))
     oth[1], own[1] = flat(oth_late), flat(take(source, own_at + 1))
@@ -407,22 +402,36 @@
 
     few, cols = core[0].shape[1:]
     size = few * len(wrapped(cols, rows))
+    core_got = lax.ppermute(core[1], "gy", SWAP)
     stay, leave = once(
-        "pack",
-        pack_kernel,
-        at,
-        [keep, lax.ppermute(give, "gz", SWAP), core[1]],
-        [(rows, rows), (rows + 4 * size, rows)],
+        "add_late",
+        add_late_kernel,
+        at,
+        [keep, lax.ppermute(give, "gz", SWAP)],
+        [(rows, rows)] * 2,
         [F32, BF16],
     )
     full = laid + size
-    to_far, turned, to_near, kept, to_cross = once(
+    cross_home = lax.ppermute(cross_home, "gx", CROSS)
+    to_near, kept, to_cross = once(
+        "join",
+        join_kernel,
+        at,
+        [core[0], core_got, near_home],
+        [(full, rows), (few, cols), (size, rows)],
+        [BF16, F32, BF16],
+    )
+    got = lax.ppermute(leave, "gy", SWAP)
+    near_got = lax.ppermute(to_near, "gx", NEAR_BACK)
+    cross_got = lax.ppermute(to_cross, "gx", CROSS)
+    got, cross_home = tied((got, cross_home))
+    to_far, turned = once(
         "part",
         part_kernel,
         at,
-        [stay, lax.ppermute(leave, "gy", SWAP), core[0], near_home, cross_home, far_home],
-        [(full, rows), (rows, rows), (full, rows), (size, rows), (full, rows)],
-        [BF16, BF16, BF16, F32, BF16],
+        [stay, got, core[0], core_got, far_home],
+        [(full, rows), (rows, rows)],
+        [BF16, BF16],
     )
     return once(
         "final",
@@ -433,9 +442,10 @@
             kept_home,
             lax.ppermute(to_far, "gx", FAR_BACK),
             lax.ppermute(turned, ("gx", "gy", "gz"), TURN),
-            lax.ppermute(to_near, "gx", NEAR_BACK),
+            near_got,
             kept,
-            lax.ppermute(to_cross, "gx", CROSS),
+            cross_home,
+            cross_got,
         ],
         [(rows, rows), (few, ncomp, nz, y_basis.shape[1])],
     )

time: 227 us -> 222 us (0.978)
  waiting for transfers between devices: 97.5 us -> 90.7 us
  starting transfers between devices: 38.6 us -> 42 us
    ppermute x1, waiting for transfers between devices: 6.23 us -> 1.47 us  [meeting(): lax.ppermute(to_far, 'gx', FAR_BACK)]
    ppermute x1 -> x2, waiting for transfers between devices: 5.27 us -> 9.67 us  [meeting(): core_got = lax.ppermute(core[1], 'gy', SWAP)]
    ppermute x3, waiting for transfers between devices: 10.3 us -> 6.64 us  [the longest x1 6.64 us: meeting(): near_got = lax.ppermute(to_near, 'gx', NEAR_BACK)]
    reshape x3 -> x2, local copies, waits for them, and re-layouts: 7.93 us -> 6.21 us  [take(): return lax.dynamic_slice_in_dim(source, start, 1, 1).reshape(rows, nz, ny)]
    pallas_call x11 -> x12, Pallas kernels: 39.6 us -> 40.1 us  [call(): pl.pallas_call(kernel, out_shape=tuple((jax.ShapeDtypeStruct(o, t) for o,...]
  transfers between devices with their start and end apart: 16 -> 18, of which waited for: 10 -> 10; matrix products, arithmetic and copies ran while one was open for 17% -> 16% of each run, Pallas kernels for 15% -> 16%
where the time goes in v4:
time: 222 us; the launch traced here: 221 us
  waiting for transfers between devices  90.7 us (41%)
  local copies, waits for them, and re-layouts  42.6 us (19%)
  starting transfers between devices  42 us (19%)
  Pallas kernels  40.1 us (18%)
  other arithmetic  4.21 us (2%)
    ppermute x3, waiting for transfers between devices, send_far(): return (lax.ppermute(data, 'gx', FAR), *gate)  42.4 us
    pallas_call x12, Pallas kernels, call(): pl.pallas_call(kernel, out_shape=tuple((jax.ShapeDtypeStruct(o, t) for o,...  40.1 us
    unnamed x30, local copies, waits for them, and re-layouts  29.5 us
    ppermute x1, waiting for transfers between devices, meeting(): near[1] = lax.ppermute(own[1], 'gx', NEAR)  21.8 us
    ppermute x3, starting transfers between devices, send_far(): return (lax.ppermute(data, 'gx', FAR), *gate)  17 us
    ppermute x2, waiting for transfers between devices, meeting(): core_got = lax.ppermute(core[1], 'gy', SWAP)  9.67 us
    ppermute x1, waiting for transfers between devices, meeting(): near_raw = lax.ppermute(own_raw, 'gx', NEAR)  8.23 us
    ppermute x1, starting transfers between devices, meeting(): near_raw = lax.ppermute(own_raw, 'gx', NEAR)  7.8 us
  transfers between devices with their start and end apart: 18, of which 10 were waited for; matrix products, arithmetic and copies ran while one was open for 16% of the time, Pallas kernels for 16%

profile of v4, /device:TPU:0, one launch (start us, length us, event | category | flops | bytes accessed | tf_op | source)
XLA Modules:
  0.0 220.6 jit_solution(10714370562966696521)
XLA Ops:
  0.7 4.5 %dynamic-slice_bitcast_fusion.1 = (bf16[256,8,512]{2,1,0:T(8,128)(2,1)}, bf16[256,8,512]{2,1,0:T(8,128)(2,1)}) fusion(bf16[256,4,8,512]{3,2,1,0:T(8,128)(2,1)} %param.3, s32[]{:T(128)S(6)} %select_n.44, s32[]{:T(128)S(6)} %select_n.43), kind=kLoop, calls=%fused_computation.2 | loop fusion | bytes 8388616 | tf_op jit(solution)/shard_map/reshape | solution.py:307
  7.1 7.8 %collective-permute-start.1 = (bf16[256,8,512]{2,1,0:T(8,128)(2,1)}, bf16[256,8,512]{2,1,0:T(8,128)(2,1)}, u32[]{:S(2)}, u32[]{:S(2)}) collective-permute-start(bf16[256,8,512]{2,1,0:T(8,128)(2,1)} %get-tuple-element.86), channel_id=1, source_target_pairs={{0,4},{12,8},{1,5},{13,9},{2,6},{14,10},{3,7},{15,11},{16,20},{28,... | collective-permute-start | bytes 6291464 | tf_op jit(solution)/shard_map/ppermute | solution.py:319
  30.8 3.8 %copy.15 = bf16[32,8,8,512]{3,1,2,0:T(8,128)(2,1)} copy(bf16[32,8,8,512]{3,2,1,0:T(8,128)(2,1)} %bitcast.24) | data formatting | bytes 4194304
  34.6 3.9 %copy.16 = bf16[32,8,8,512]{3,1,2,0:T(8,128)(2,1)} copy(bf16[32,8,8,512]{3,2,1,0:T(8,128)(2,1)} %bitcast.26) | data formatting | bytes 4194304
  44.8 3.2 %pad_maximum_fusion = bf16[256,4608]{1,0:T(8,128)(2,1)} fusion(bf16[256,512]{1,0:T(8,128)(2,1)S(1)} %slice.9, bf16[256,4096]{1,0:T(8,128)(2,1)} %bitcast.46), kind=kLoop, calls=%fused_computation | loop fusion | flops 4718592 | bytes 4718592 | tf_op jit(solution)/shard_map/concatenate | solution.py:342
  47.9 3.8 %copy.17 = bf16[32,8,8,512]{3,1,2,0:T(8,128)(2,1)} copy(bf16[32,8,8,512]{3,2,1,0:T(8,128)(2,1)} %bitcast.28) | data formatting | bytes 4194304
  51.7 8.2 %collective-permute-done.1 = bf16[256,8,512]{2,1,0:T(8,128)(2,1)} collective-permute-done((bf16[256,8,512]{2,1,0:T(8,128)(2,1)}, bf16[256,8,512]{2,1,0:T(8,128)(2,1)}, u32[]{:S(2)}, u32[]{:S(2)}) %collective-permute-start.1) | collective-permute-done | bytes 2097184 | tf_op jit(solution)/shard_map/ppermute | solution.py:319
  60.0 3.8 %copy.18 = bf16[32,8,8,512]{3,1,2,0:T(8,128)(2,1)} copy(bf16[32,8,8,512]{3,2,1,0:T(8,128)(2,1)} %bitcast.30) | data formatting | bytes 4194304
  63.8 7.1 %collective-permute-start.2 = (bf16[256,4608]{1,0:T(8,128)(2,1)}, bf16[256,4608]{1,0:T(8,128)(2,1)}, u32[]{:S(2)}, u32[]{:S(2)}) collective-permute-start(bf16[256,4608]{1,0:T(8,128)(2,1)} %pad_maximum_fusion), channel_id=1, source_target_pairs={{0,8},{12,4},{1,9},{13,5},{2,10},{14,6},{3,11},{15,7},{16,24},{28,... | collective-permute-start | bytes 7077896 | tf_op jit(solution)/shard_map/ppermute | solution.py:346
  77.3 5.7 %pairs.2.rest_0_ = f32[4,256,256]{2,1,0:T(8,128)S(1)} custom-call(s32[4]{0:T(128)S(1)} %pad_add_fusion.at, bf16[256,4096]{1,0:T(8,128)(2,1)S(1)} %bitcast.44, bf16[256,4096]{1,0:T(8,128)(2,1)S(1)} %bitcast.40, bf16[256,4096]{1,0:T(8,128)(2,1)S(1)} %bitcast.42, bf16[256,4096]{1,0:T(8,128)(2,1)S(1)} %bitcast.47), custom_call_target="tpu_custom_call" | custom-call | flops 1 | bytes 1 | tf_op jit(solution)/shard_map/pairs/pallas_call | solution.py:98
  83.0 21.8 %collective-permute-done.5.near = bf16[256,4096]{1,0:T(8,128)(2,1)} collective-permute-done((bf16[256,4096]{1,0:T(8,128)(2,1)S(1)}, bf16[256,4096]{1,0:T(8,128)(2,1)}, u32[]{:S(2)}, u32[]{:S(2)}) %collective-permute-start.5) | collective-permute-done | bytes 2097184 | tf_op jit(solution)/shard_map/ppermute | solution.py:321
  104.8 8.8 %pairs.3 = (f32[2,768,256]{2,1,0:T(8,128)S(1)}, f32[2,768,256]{2,1,0:T(8,128)S(1)}) custom-call(s32[4]{0:T(128)S(1)} %pad_add_fusion.at, bf16[256,4096]{1,0:T(8,128)(2,1)} %collective-permute-done.5.near, bf16[256,4096]{1,0:T(8,128)(2,1)S(1)} %bitcast.36, bf16[256,4096]{1,0:T(8,128)(2,1)} %collective-permute-done.4.cross, bf16[256,4096]{1,0:T(8,128)(2,1)} %bitcast.20.other, ...), custom_call_target="tpu_custom_call" | custom-call | flops 1 | bytes 1 | tf_op jit(solution)/shard_map/pairs/pallas_call | solution.py:98
  113.7 4.6 %collective-permute-start.6 = (bf16[256,2560]{1,0:T(8,128)(2,1)S(1)}, bf16[256,2560]{1,0:T(8,128)(2,1)S(1)}, u32[]{:S(2)}, u32[]{:S(2)}) collective-permute-start(bf16[256,2560]{1,0:T(8,128)(2,1)S(1)} %copy-done.8), channel_id=1, source_target_pairs={{0,8},{12,4},{1,9},{13,5},{2,10},{14,6},{3,11},{15,7},{16,24},{28,... | collective-permute-start | bytes 3932168 | tf_op jit(solution)/shard_map/ppermute | solution.py:346
  120.6 34.9 %collective-permute-done.2.far = bf16[256,4608]{1,0:T(8,128)(2,1)} collective-permute-done((bf16[256,4608]{1,0:T(8,128)(2,1)}, bf16[256,4608]{1,0:T(8,128)(2,1)}, u32[]{:S(2)}, u32[]{:S(2)}) %collective-permute-start.2) | collective-permute-done | bytes 2359328 | tf_op jit(solution)/shard_map/ppermute | solution.py:346
  155.5 5.3 %collective-permute-start.3 = (bf16[256,1024]{1,0:T(8,128)(2,1)S(1)}, bf16[256,1024]{1,0:T(8,128)(2,1)S(1)}, u32[]{:S(2)}, u32[]{:S(2)}) collective-permute-start(bf16[256,1024]{1,0:T(8,128)(2,1)S(1)} %slice.11), channel_id=1, source_target_pairs={{0,8},{12,4},{1,9},{13,5},{2,10},{14,6},{3,11},{15,7},{16,24},{28,... | collective-permute-start | bytes 1572872 | tf_op jit(solution)/shard_map/ppermute | solution.py:346
  160.8 8.5 %meet.4 = (f32[3,256,256]{2,1,0:T(8,128)S(1)}, f32[4,16,1024]{2,1,0:T(8,128)S(1)}, f32[4,16,1024]{2,1,0:T(8,128)S(1)}) custom-call(s32[4]{0:T(128)S(1)} %pad_add_fusion.at, bf16[256,4608]{1,0:T(8,128)(2,1)} %collective-permute-done.2.far, bf16[256,4096]{1,0:T(8,128)(2,1)S(1)} %bitcast.45, bf16[256,4096]{1,0:T(8,128)(2,1)S(1)} %bitcast.41, ...), custom_call_target="tpu_custom_call" | custom-call | flops 1 | bytes 1 | tf_op jit(solution)/shard_map/meet/pallas_call | solution.py:98
  169.3 2.7 %meet.5 = (f32[3,256,256]{2,1,0:T(8,128)S(1)}, f32[4,16,1152]{2,1,0:T(8,128)S(1)}, f32[4,16,1152]{2,1,0:T(8,128)S(1)}) custom-call(s32[4]{0:T(128)S(1)} %pad_add_fusion.at, bf16[256,4608]{1,0:T(8,128)(2,1)} %collective-permute-done.2.far, bf16[256,4096]{1,0:T(8,128)(2,1)} %collective-permute-done.5.near, bf16[256,4096]{1,0:T(8,128)(2,1)S(1)} %bitcast.37, ...), custom_call_target="tpu_custom_call" | custom-call | flops 1 | bytes 1 | tf_op jit(solution)/shard_map/meet/pallas_call | solution.py:98
  173.5 5.3 %collective-permute-done.9.core_got = f32[4,16,1152]{2,1,0:T(8,128)S(1)} collective-permute-done((f32[4,16,1152]{2,1,0:T(8,128)S(1)}, f32[4,16,1152]{2,1,0:T(8,128)S(1)}, u32[]{:S(2)}, u32[]{:S(2)}) %collective-permute-start.9) | collective-permute-done | bytes 294944 | tf_op jit(solution)/shard_map/ppermute | solution.py:386
  179.4 4.0 %collective-permute-done.6.far = bf16[256,2560]{1,0:T(8,128)(2,1)S(1)} collective-permute-done((bf16[256,2560]{1,0:T(8,128)(2,1)S(1)}, bf16[256,2560]{1,0:T(8,128)(2,1)S(1)}, u32[]{:S(2)}, u32[]{:S(2)}) %collective-permute-start.6) | collective-permute-done | bytes 1310752 | tf_op jit(solution)/shard_map/ppermute | solution.py:346
  183.4 6.2 %meet.6 = (f32[3,256,256]{2,1,0:T(8,128)S(1)}, f32[4,16,640]{2,1,0:T(8,128)S(1)}, f32[4,16,640]{2,1,0:T(8,128)S(1)}) custom-call(s32[4]{0:T(128)S(1)} %pad_add_fusion.at, bf16[256,2560]{1,0:T(8,128)(2,1)S(1)} %collective-permute-done.6.far, bf16[256,4096]{1,0:T(8,128)(2,1)} %collective-permute-done.5.near, bf16[256,4096]{1,0:T(8,128)(2,1)S(1)} %bitcast.38, ...), custom_call_target="tpu_custom_call" | custom-call | flops 1 | bytes 1 | tf_op jit(solution)/shard_map/meet/pallas_call | solution.py:98
  189.6 3.6 %collective-permute-done.3.far = bf16[256,1024]{1,0:T(8,128)(2,1)S(1)} collective-permute-done((bf16[256,1024]{1,0:T(8,128)(2,1)S(1)}, bf16[256,1024]{1,0:T(8,128)(2,1)S(1)}, u32[]{:S(2)}, u32[]{:S(2)}) %collective-permute-start.3) | collective-permute-done | bytes 524320 | tf_op jit(solution)/shard_map/ppermute | solution.py:346
  193.2 3.4 %meet.7 = (f32[2,256,256]{2,1,0:T(8,128)S(1)}, f32[2,256,256]{2,1,0:T(8,128)S(1)}, f32[4,16,896]{2,1,0:T(8,128)S(1)}, f32[4,16,896]{2,1,0:T(8,128)S(1)}) custom-call(s32[4]{0:T(128)S(1)} %pad_add_fusion.at, bf16[256,1024]{1,0:T(8,128)(2,1)S(1)} %collective-permute-done.3.far, bf16[256,4096]{1,0:T(8,128)(2,1)} %collective-permute-done.5.near, ...), custom_call_target="tpu_custom_call" | custom-call | flops 1 | bytes 1 | tf_op jit(solution)/shard_map/meet/pallas_call | solution.py:98
  200.7 4.4 %collective-permute-done.13.core_got.got = f32[4,16,896]{2,1,0:T(8,128)S(1)} collective-permute-done((f32[4,16,896]{2,1,0:T(8,128)S(1)}, f32[4,16,896]{2,1,0:T(8,128)S(1)}, u32[]{:S(2)}, u32[]{:S(2)}) %collective-permute-start.13) | collective-permute-done | bytes 229408 | tf_op jit(solution)/shard_map/ppermute | solution.py:405
  210.8 6.6 %collective-permute-done.16.near = bf16[400,256]{1,0:T(8,128)(2,1)S(1)} collective-permute-done((bf16[400,256]{1,0:T(8,128)(2,1)S(1)}, bf16[400,256]{1,0:T(8,128)(2,1)S(1)}, u32[]{:S(2)}, u32[]{:S(2)}) %collective-permute-start.16) | collective-permute-done | bytes 204832 | tf_op jit(solution)/shard_map/ppermute | solution.py:425
  (65 shorter events, 47.8 us)
Async XLA Ops:
  0.6 43.1 %copy-start = (bf16[1024,128]{1,0:T(8,128)(2,1)S(1)}, bf16[1024,128]{1,0:T(8,128)(2,1)}, u32[]{:S(2)}) copy-start(bf16[1024,128]{1,0:T(8,128)(2,1)} %param.5) | copy-start | bytes 786436
  5.2 42.8 %collective-permute-start = (bf16[256,8,512]{2,1,0:T(8,128)(2,1)}, bf16[256,8,512]{2,1,0:T(8,128)(2,1)}, u32[]{:S(2)}, u32[]{:S(2)}) collective-permute-start(bf16[256,8,512]{2,1,0:T(8,128)(2,1)} %get-tuple-element.84), channel_id=1, source_target_pairs={{4,8},{8,4},{5,9},{9,5},{6,10},{10,6},{7,11},{11,7},{20,24},{24,20... | collective-permute-start | bytes 6291464 | tf_op jit(solution)/shard_map/ppermute | solution.py:318
  7.1 52.8 %collective-permute-start.1 = (bf16[256,8,512]{2,1,0:T(8,128)(2,1)}, bf16[256,8,512]{2,1,0:T(8,128)(2,1)}, u32[]{:S(2)}, u32[]{:S(2)}) collective-permute-start(bf16[256,8,512]{2,1,0:T(8,128)(2,1)} %get-tuple-element.86), channel_id=1, source_target_pairs={{0,4},{12,8},{1,5},{13,9},{2,6},{14,10},{3,7},{15,11},{16,20},{28,... | collective-permute-start | bytes 6291464 | tf_op jit(solution)/shard_map/ppermute | solution.py:319
  18.9 64.1 %collective-permute-start.4 = (bf16[256,4096]{1,0:T(8,128)(2,1)}, bf16[256,4096]{1,0:T(8,128)(2,1)}, u32[]{:S(2)}, u32[]{:S(2)}) collective-permute-start(bf16[256,4096]{1,0:T(8,128)(2,1)} %bitcast.20.other), channel_id=1, source_target_pairs={{4,8},{8,4},{5,9},{9,5},{6,10},{10,6},{7,11},{11,7},{20,24},{24,20... | collective-permute-start | bytes 6291464 | tf_op jit(solution)/shard_map/ppermute | solution.py:320
  23.6 81.2 %collective-permute-start.5 = (bf16[256,4096]{1,0:T(8,128)(2,1)S(1)}, bf16[256,4096]{1,0:T(8,128)(2,1)}, u32[]{:S(2)}, u32[]{:S(2)}) collective-permute-start(bf16[256,4096]{1,0:T(8,128)(2,1)S(1)} %bitcast.35), channel_id=1, source_target_pairs={{0,4},{12,8},{1,5},{13,9},{2,6},{14,10},{3,7},{15,11},{16,20},{28,... | collective-permute-start | bytes 6291464 | tf_op jit(solution)/shard_map/ppermute | solution.py:321
  34.6 3.9 %copy-start.9 = (bf16[1024,128]{1,0:T(8,128)(2,1)S(1)}, bf16[1024,128]{1,0:T(8,128)(2,1)}, u32[]{:S(2)}) copy-start(bf16[1024,128]{1,0:T(8,128)(2,1)} %param.4) | copy-start | bytes 786436
  63.8 91.7 %collective-permute-start.2 = (bf16[256,4608]{1,0:T(8,128)(2,1)}, bf16[256,4608]{1,0:T(8,128)(2,1)}, u32[]{:S(2)}, u32[]{:S(2)}) collective-permute-start(bf16[256,4608]{1,0:T(8,128)(2,1)} %pad_maximum_fusion), channel_id=1, source_target_pairs={{0,8},{12,4},{1,9},{13,5},{2,10},{14,6},{3,11},{15,7},{16,24},{28,... | collective-permute-start | bytes 7077896 | tf_op jit(solution)/shard_map/ppermute | solution.py:346
  83.0 30.7 %copy-start.8 = (bf16[256,2560]{1,0:T(8,128)(2,1)S(1)}, bf16[256,2560]{1,0:T(8,128)(2,1)}, u32[]{:S(2)}) copy-start(bf16[256,2560]{1,0:T(8,128)(2,1)} %slice.10) | copy-start | bytes 3932164
  104.8 56.0 %copy-start.4 = (bf16[32,8,8,512]{3,1,2,0:T(8,128)(2,1)S(1)}, bf16[32,8,8,512]{3,1,2,0:T(8,128)(2,1)}, u32[]{:S(2)}) copy-start(bf16[32,8,8,512]{3,1,2,0:T(8,128)(2,1)} %copy.17) | copy-start | bytes 6291460
  104.8 56.0 %copy-start.6 = (bf16[32,8,8,512]{3,1,2,0:T(8,128)(2,1)S(1)}, bf16[32,8,8,512]{3,1,2,0:T(8,128)(2,1)}, u32[]{:S(2)}) copy-start(bf16[32,8,8,512]{3,1,2,0:T(8,128)(2,1)} %copy.18) | copy-start | bytes 6291460
  113.6 47.2 %copy-start.2 = (bf16[32,8,8,512]{3,1,2,0:T(8,128)(2,1)S(1)}, bf16[32,8,8,512]{3,1,2,0:T(8,128)(2,1)}, u32[]{:S(2)}) copy-start(bf16[32,8,8,512]{3,1,2,0:T(8,128)(2,1)} %copy.16) | copy-start | bytes 6291460
  113.6 4.7 %collective-permute-start.7 = (f32[2,768,256]{2,1,0:T(8,128)S(1)}, f32[2,768,256]{2,1,0:T(8,128)S(1)}, u32[]{:S(2)}, u32[]{:S(2)}) collective-permute-start(f32[2,768,256]{2,1,0:T(8,128)S(1)} %get-tuple-element.108), channel_id=1, source_target_pairs={{0,1},{1,0},{2,3},{3,2},{4,5},{5,4},{6,7},{7,6},{8,9},{9,8},{10,11... | collective-permute-start | bytes 4718600 | tf_op jit(solution)/shard_map/ppermute | solution.py:380
  113.7 69.7 %collective-permute-start.6 = (bf16[256,2560]{1,0:T(8,128)(2,1)S(1)}, bf16[256,2560]{1,0:T(8,128)(2,1)S(1)}, u32[]{:S(2)}, u32[]{:S(2)}) collective-permute-start(bf16[256,2560]{1,0:T(8,128)(2,1)S(1)} %copy-done.8), channel_id=1, source_target_pairs={{0,8},{12,4},{1,9},{13,5},{2,10},{14,6},{3,11},{15,7},{16,24},{28,... | collective-permute-start | bytes 3932168 | tf_op jit(solution)/shard_map/ppermute | solution.py:346
  119.0 41.7 %collective-permute-start.8 = (f32[768,256]{1,0:T(8,128)S(1)}, f32[768,256]{1,0:T(8,128)S(1)}, u32[]{:S(2)}, u32[]{:S(2)}) collective-permute-start(f32[768,256]{1,0:T(8,128)S(1)} %get-tuple-element.109), channel_id=1, source_target_pairs={{0,2},{2,0},{1,3},{3,1},{4,6},{6,4},{5,7},{7,5},{8,10},{10,8},{9,1... | collective-permute-start | bytes 2359304 | tf_op jit(solution)/shard_map/ppermute | solution.py:382
  155.5 37.8 %collective-permute-start.3 = (bf16[256,1024]{1,0:T(8,128)(2,1)S(1)}, bf16[256,1024]{1,0:T(8,128)(2,1)S(1)}, u32[]{:S(2)}, u32[]{:S(2)}) collective-permute-start(bf16[256,1024]{1,0:T(8,128)(2,1)S(1)} %slice.11), channel_id=1, source_target_pairs={{0,8},{12,4},{1,9},{13,5},{2,10},{14,6},{3,11},{15,7},{16,24},{28,... | collective-permute-start | bytes 1572872 | tf_op jit(solution)/shard_map/ppermute | solution.py:346
  172.0 6.8 %collective-permute-start.9 = (f32[4,16,1152]{2,1,0:T(8,128)S(1)}, f32[4,16,1152]{2,1,0:T(8,128)S(1)}, u32[]{:S(2)}, u32[]{:S(2)}) collective-permute-start(f32[4,16,1152]{2,1,0:T(8,128)S(1)} %get-tuple-element.120), channel_id=1, source_target_pairs={{0,2},{2,0},{1,3},{3,1},{4,6},{6,4},{5,7},{7,5},{8,10},{10,8},{9,1... | collective-permute-start | bytes 884744 | tf_op jit(solution)/shard_map/ppermute | solution.py:386
  196.6 2.3 %collective-permute-start.10 = (f32[2,256,256]{2,1,0:T(8,128)S(1)}, f32[2,256,256]{2,1,0:T(8,128)S(1)}, u32[]{:S(2)}, u32[]{:S(2)}) collective-permute-start(f32[2,256,256]{2,1,0:T(8,128)S(1)} %get-tuple-element.141), channel_id=1, source_target_pairs={{0,1},{1,0},{2,3},{3,2},{4,5},{5,4},{6,7},{7,6},{8,9},{9,8},{10,11... | collective-permute-start | bytes 1572872 | tf_op jit(solution)/shard_map/ppermute | solution.py:410
  196.7 8.5 %collective-permute-start.13 = (f32[4,16,896]{2,1,0:T(8,128)S(1)}, f32[4,16,896]{2,1,0:T(8,128)S(1)}, u32[]{:S(2)}, u32[]{:S(2)}) collective-permute-start(f32[4,16,896]{2,1,0:T(8,128)S(1)} %get-tuple-element.147), channel_id=1, source_target_pairs={{0,2},{2,0},{1,3},{3,1},{4,6},{6,4},{5,7},{7,5},{8,10},{10,8},{9,1... | collective-permute-start | bytes 688136 | tf_op jit(solution)/shard_map/ppermute | solution.py:405
  198.2 8.8 %collective-permute-start.12 = (bf16[336,256]{1,0:T(8,128)(2,1)S(1)}, bf16[336,256]{1,0:T(8,128)(2,1)S(1)}, u32[]{:S(2)}, u32[]{:S(2)}) collective-permute-start(bf16[336,256]{1,0:T(8,128)(2,1)S(1)} %get-tuple-element.144), channel_id=1, source_target_pairs={{4,8},{8,4},{5,9},{9,5},{6,10},{10,6},{7,11},{11,7},{20,24},{24,20... | collective-permute-start | bytes 516104 | tf_op jit(solution)/shard_map/ppermute | solution.py:415
  199.5 8.0 %collective-permute-start.11 = (bf16[256,256]{1,0:T(8,128)(2,1)S(1)}, bf16[256,256]{1,0:T(8,128)(2,1)S(1)}, u32[]{:S(2)}, u32[]{:S(2)}) collective-permute-start(bf16[256,256]{1,0:T(8,128)(2,1)S(1)} %get-tuple-element.143), channel_id=1, source_target_pairs={{0,2},{2,0},{1,3},{3,1},{4,6},{6,4},{5,7},{7,5},{8,10},{10,8},{9,1... | collective-permute-start | bytes 393224 | tf_op jit(solution)/shard_map/ppermute | solution.py:424
  205.7 11.7 %collective-permute-start.16 = (bf16[400,256]{1,0:T(8,128)(2,1)S(1)}, bf16[400,256]{1,0:T(8,128)(2,1)S(1)}, u32[]{:S(2)}, u32[]{:S(2)}) collective-permute-start(bf16[400,256]{1,0:T(8,128)(2,1)S(1)} %get-tuple-element.152), channel_id=1, source_target_pairs={{4,0},{8,12},{5,1},{9,13},{6,2},{10,14},{7,3},{11,15},{20,16},{24,... | collective-permute-start | bytes 614408 | tf_op jit(solution)/shard_map/ppermute | solution.py:425
  208.2 10.8 %collective-permute-start.14 = (bf16[400,256]{1,0:T(8,128)(2,1)S(1)}, bf16[400,256]{1,0:T(8,128)(2,1)S(1)}, u32[]{:S(2)}, u32[]{:S(2)}) collective-permute-start(bf16[400,256]{1,0:T(8,128)(2,1)S(1)} %get-tuple-element.149), channel_id=1, source_target_pairs={{4,12},{8,0},{5,13},{9,1},{6,14},{10,2},{7,15},{11,3},{20,28},{24,... | collective-permute-start | bytes 614408 | tf_op jit(solution)/shard_map/ppermute | solution.py:443
  209.5 8.0 %collective-permute-start.15 = (bf16[256,256]{1,0:T(8,128)(2,1)S(1)}, bf16[256,256]{1,0:T(8,128)(2,1)S(1)}, u32[]{:S(2)}, u32[]{:S(2)}) collective-permute-start(bf16[256,256]{1,0:T(8,128)(2,1)S(1)} %get-tuple-element.150), channel_id=1, source_target_pairs={{4,3},{5,7},{6,11},{9,4},{10,8},{11,12},{20,19},{21,23},{22,27},{2... | collective-permute-start | bytes 393224 | tf_op jit(solution)/shard_map/ppermute | solution.py:444
  210.1 0.7 collective-permute-start.17
  (4 other events, 6.4 us)

commit v5 on v4

--- a/solution.py
+++ b/solution.py
@@ -303,24 +303,31 @@
 
     tied = lax.optimization_barrier
 
-    def take(source, start):
-        return lax.dynamic_slice_in_dim(source, start, 1, 1).reshape(rows, nz, ny)
-
-    def flat(a):
-        return a.reshape(rows, width)
+    def take(source, start, lo=0, count=rows):
+        return lax.dynamic_slice(source, (lo, start, 0, 0), (count, 1, nz, ny)).reshape(count, nz, ny)
+
+    def flat(*parts):
+        parts = [a.reshape(a.shape[0], width) for a in parts]
+        return parts[0] if len(parts) == 1 else jnp.concatenate(parts, 0)
 
     near, cross, own, oth = ([None] * half for _ in range(4))
-    oth_raw, own_raw = take(snapshot, oth_at), take(snapshot, own_at)
-    source, oth_raw, own_raw = tied((snapshot, oth_raw, own_raw))
+    source = snapshot
+    oth_raw, own_raw = [], []
+    for lo, count in ((0, rows // 2), (rows // 2, rows - rows // 2)):
+        o, w = take(source, oth_at, lo, count), take(source, own_at, lo, count)
+        source, o, w = tied((source, o, w))
+        oth_raw.append(o)
+        own_raw.append(w)
     oth_late = take(source, oth_at + 1)
     source, oth_late = tied((source, oth_late))
     oth[1], own[1] = flat(oth_late), flat(take(source, own_at + 1))
-    cross_raw = lax.ppermute(oth_raw, "gx", CROSS)
-    near_raw = lax.ppermute(own_raw, "gx", NEAR)
+    cross_raw = [lax.ppermute(a, "gx", CROSS) for a in oth_raw]
+    near_raw = [lax.ppermute(a, "gx", NEAR) for a in own_raw]
     cross[1] = lax.ppermute(oth[1], "gx", CROSS)
+    own[1], cross_raw[0] = tied((own[1], cross_raw[0]))
     near[1] = lax.ppermute(own[1], "gx", NEAR)
-    oth_raw, own_raw, oth[1], own[1] = tied((oth_raw, own_raw, oth[1], own[1]))
-    oth[0], own[0] = flat(oth_raw), flat(own_raw)
+    source, oth[1], own[1] = tied((source, oth[1], own[1]))
+    oth[0], own[0] = flat(take(source, oth_at)), flat(take(source, own_at))
 
     places = [
         jnp.where(side == 0, 0, 3),
@@ -331,7 +338,7 @@
     basis = jnp.stack([lax.dynamic_slice_in_dim(x_basis, p * rows, rows, 0).T for p in places])
     y_own = lax.dynamic_slice_in_dim(y_basis, gy * ny, ny, 0)
 
-    cuts = [(0, 9), (9, 14), (14, 16)]
+    cuts = [(0, 10), (10, 15), (15, 16)]
 
     def piece(lo, hi):
         parts = []
@@ -364,9 +371,13 @@
 
     sends = [piece(lo, hi) for lo, hi in cuts]
     sends, cross_raw, own[0] = tied((sends, cross_raw, own[0]))
-    cross[0] = flat(cross_raw)
-    cross[0], near_raw = tied((cross[0], near_raw))
-    near[0] = flat(near_raw)
+    top = flat(cross_raw[0])
+    top, near_raw[0] = tied((top, near_raw[0]))
+    near_top = flat(near_raw[0])
+    near_top, cross_raw[1] = tied((near_top, cross_raw[1]))
+    cross[0] = jnp.concatenate([top, flat(cross_raw[1])], 0)
+    cross[0], near_raw[1] = tied((cross[0], near_raw[1]))
+    near[0] = jnp.concatenate([near_top, flat(near_raw[1])], 0)
     far0, cross[0], near[0], own[0], basis, y_own = send_far(
         0, cross[0], near[0], own[0], basis, y_own
     )

time: 222 us -> 220 us (level)
  starting transfers between devices: 42 us -> 54.8 us
  waiting for transfers between devices: 90.7 us -> 81.2 us
  local copies, waits for them, and re-layouts: 42.6 us -> 36.5 us
    unnamed x30 -> x36, local copies, waits for them, and re-layouts: 29.5 us -> 19.9 us
    ppermute x2 -> x4, waiting for transfers between devices: 8.23 us -> 1.42 us  [the longest x2 1.41 us: meeting(): near_raw = [lax.ppermute(a, 'gx', NEAR) for a in own_raw]]
    ppermute x1, starting transfers between devices: 2.66 us -> 9.08 us  [meeting(): near[1] = lax.ppermute(own[1], 'gx', NEAR)]
    ppermute x3, waiting for transfers between devices: 42.4 us -> 48.6 us  [send_far(): return (lax.ppermute(data, 'gx', FAR), *gate)]
    ppermute x2, waiting for transfers between devices: 9.67 us -> 4.05 us  [meeting(): core_got = lax.ppermute(core[1], 'gy', SWAP)]
    ppermute x2 -> x4, starting transfers between devices: 9.78 us -> 13.3 us  [the longest x2 10 us: meeting(): near_raw = [lax.ppermute(a, 'gx', NEAR) for a in own_raw]]
    concatenate x0 -> x2, other arithmetic: none -> 3.11 us  [the longest x1 1.56 us: meeting(): near[0] = jnp.concatenate([near_top, flat(near_raw[1])], 0)]
    ppermute x3, starting transfers between devices: 17 us -> 19.9 us  [send_far(): return (lax.ppermute(data, 'gx', FAR), *gate)]
  transfers between devices with their start and end apart: 18 -> 20, of which waited for: 10 -> 8; matrix products, arithmetic and copies ran while one was open for 16% -> 15% of each run, Pallas kernels for 16% -> 16%
where the time goes in v5:
time: 220 us; the launch traced here: 219 us
  waiting for transfers between devices  81.2 us (37%)
  starting transfers between devices  54.8 us (25%)
  Pallas kernels  39.9 us (18%)
  local copies, waits for them, and re-layouts  36.5 us (17%)
  other arithmetic  5.07 us (2%)
    ppermute x3, waiting for transfers between devices, send_far(): return (lax.ppermute(data, 'gx', FAR), *gate)  48.6 us
    pallas_call x12, Pallas kernels, call(): pl.pallas_call(kernel, out_shape=tuple((jax.ShapeDtypeStruct(o, t) for o,...  39.9 us
    unnamed x36, local copies, waits for them, and re-layouts  19.9 us
    ppermute x3, starting transfers between devices, send_far(): return (lax.ppermute(data, 'gx', FAR), *gate)  19.9 us
    ppermute x1, waiting for transfers between devices, meeting(): near[1] = lax.ppermute(own[1], 'gx', NEAR)  19.7 us
    ppermute x2, starting transfers between devices, meeting(): near_raw = [lax.ppermute(a, 'gx', NEAR) for a in own_raw]  10 us
    ppermute x1, starting transfers between devices, meeting(): near[1] = lax.ppermute(own[1], 'gx', NEAR)  9.08 us
    reshape x3, local copies, waits for them, and re-layouts, take(): lax.dynamic_slice(source, (lo, start, 0, 0), (count, 1, nz, ny))  7.79 us
  transfers between devices with their start and end apart: 20, of which 8 were waited for; matrix products, arithmetic and copies ran while one was open for 15% of the time, Pallas kernels for 16%

profile of v5, /device:TPU:0, one launch (start us, length us, event | category | flops | bytes accessed | tf_op | source)
XLA Modules:
  0.0 218.5 jit_solution(16893207928686048471)
XLA Ops:
  0.7 3.1 %dynamic-slice_bitcast_fusion.3 = (bf16[128,8,512]{2,1,0:T(8,128)(2,1)}, bf16[128,8,512]{2,1,0:T(8,128)(2,1)}) fusion(bf16[256,4,8,512]{3,2,1,0:T(8,128)(2,1)} %param.3, s32[]{:T(128)S(6)} %select_n.48, s32[]{:T(128)S(6)} %select_n.47), kind=kLoop, calls=%fused_computation.6 | loop fusion | bytes 4194312 | tf_op jit(solution)/shard_map/reshape | solution.py:307
  5.4 7.7 %collective-permute-start.2 = (bf16[128,8,512]{2,1,0:T(8,128)(2,1)}, bf16[128,8,512]{2,1,0:T(8,128)(2,1)}, u32[]{:S(2)}, u32[]{:S(2)}) collective-permute-start(bf16[128,8,512]{2,1,0:T(8,128)(2,1)} %get-tuple-element.101), channel_id=1, source_target_pairs={{0,4},{12,8},{1,5},{13,9},{2,6},{14,10},{3,7},{15,11},{16,20},{28,... | collective-permute-start | bytes 3145736 | tf_op jit(solution)/shard_map/ppermute | solution.py:325
  13.1 3.0 %dynamic-slice_bitcast_fusion.1 = (bf16[128,8,512]{2,1,0:T(8,128)(2,1)}, bf16[128,8,512]{2,1,0:T(8,128)(2,1)}) fusion(bf16[256,4,8,512]{3,2,1,0:T(8,128)(2,1)} %param.3, s32[]{:T(128)S(6)} %select_n.48, s32[]{:T(128)S(6)} %select_n.47), kind=kLoop, calls=%fused_computation.4 | loop fusion | bytes 4194312 | tf_op jit(solution)/shard_map/reshape | solution.py:307
  17.8 2.3 %collective-permute-start.3 = (bf16[128,8,512]{2,1,0:T(8,128)(2,1)}, bf16[128,8,512]{2,1,0:T(8,128)(2,1)}, u32[]{:S(2)}, u32[]{:S(2)}) collective-permute-start(bf16[128,8,512]{2,1,0:T(8,128)(2,1)} %get-tuple-element.106), channel_id=1, source_target_pairs={{0,4},{12,8},{1,5},{13,9},{2,6},{14,10},{3,7},{15,11},{16,20},{28,... | collective-permute-start | bytes 3145736 | tf_op jit(solution)/shard_map/ppermute | solution.py:325
  21.8 2.2 %copy.13 = bf16[32,8,8,512]{3,1,2,0:T(8,128)(2,1)} copy(bf16[32,8,8,512]{3,2,1,0:T(8,128)(2,1)S(1)} %bitcast.56) | data formatting | bytes 4194304
  24.0 2.0 collective-permute-start.6
  31.3 2.5 %slice.10 = bf16[256,2560]{1,0:T(8,128)(2,1)} slice(bf16[256,4096]{1,0:T(8,128)(2,1)} %bitcast.22.other), slice={[0:256], [1024:3584]} | slice | bytes 2621440 | tf_op jit(solution)/shard_map/slice | solution.py:348
  33.7 9.1 %collective-permute-start.7 = (bf16[256,4096]{1,0:T(8,128)(2,1)S(1)}, bf16[256,4096]{1,0:T(8,128)(2,1)}, u32[]{:S(2)}, u32[]{:S(2)}) collective-permute-start(bf16[256,4096]{1,0:T(8,128)(2,1)S(1)} %bitcast.45), channel_id=1, source_target_pairs={{0,4},{12,8},{1,5},{13,9},{2,6},{14,10},{3,7},{15,11},{16,20},{28,... | collective-permute-start | bytes 6291464 | tf_op jit(solution)/shard_map/ppermute | solution.py:328
  42.8 2.5 %constant_dynamic-slice_fusion.5 = (bf16[256,1,8,512]{3,2,1,0:T(8,128)(2,1)S(1)}, bf16[256,1,8,512]{3,2,1,0:T(8,128)(2,1)S(1)}) fusion(bf16[256,4,8,512]{3,2,1,0:T(8,128)(2,1)} %param.3, s32[]{:T(128)S(6)} %select_n.48, s32[]{:T(128)S(6)} %select_n.47), kind=kLoop, calls=%fused_computation.14 | loop fusion | bytes 8388616 | tf_op jit(solution)/shard_map/dynamic_slice | solution.py:307
  45.3 2.3 %copy.16 = bf16[32,8,8,512]{3,1,2,0:T(8,128)(2,1)} copy(bf16[32,8,8,512]{3,2,1,0:T(8,128)(2,1)S(1)} %bitcast.55) | data formatting | bytes 4194304
  61.7 9.8 %collective-permute-start.4 = (bf16[256,5120]{1,0:T(8,128)(2,1)}, bf16[256,5120]{1,0:T(8,128)(2,1)}, u32[]{:S(2)}, u32[]{:S(2)}) collective-permute-start(bf16[256,5120]{1,0:T(8,128)(2,1)} %pad_maximum_fusion), channel_id=1, source_target_pairs={{0,8},{12,4},{1,9},{13,5},{2,10},{14,6},{3,11},{15,7},{16,24},{28,... | collective-permute-start | bytes 7864328 | tf_op jit(solution)/shard_map/ppermute | solution.py:353
  77.9 5.7 %pairs.2.rest_0_ = f32[4,256,256]{2,1,0:T(8,128)S(1)} custom-call(s32[4]{0:T(128)S(1)} %pad_add_fusion.at, bf16[256,4096]{1,0:T(8,128)(2,1)S(1)} %copy-done.8, bf16[256,4096]{1,0:T(8,128)(2,1)S(1)} %bitcast.52, bf16[256,4096]{1,0:T(8,128)(2,1)S(1)} %copy-done.6, bf16[256,4096]{1,0:T(8,128)(2,1)S(1)} %bitcast.51), custom_call_target="tpu_custom_call" | custom-call | flops 1 | bytes 1 | tf_op jit(solution)/shard_map/pairs/pallas_call | solution.py:98
  83.7 19.7 %collective-permute-done.7.near = bf16[256,4096]{1,0:T(8,128)(2,1)} collective-permute-done((bf16[256,4096]{1,0:T(8,128)(2,1)S(1)}, bf16[256,4096]{1,0:T(8,128)(2,1)}, u32[]{:S(2)}, u32[]{:S(2)}) %collective-permute-start.7) | collective-permute-done | bytes 2097184 | tf_op jit(solution)/shard_map/ppermute | solution.py:328
  103.4 8.8 %pairs.3 = (f32[2,768,256]{2,1,0:T(8,128)S(1)}, f32[2,768,256]{2,1,0:T(8,128)S(1)}) custom-call(s32[4]{0:T(128)S(1)} %pad_add_fusion.at, bf16[256,4096]{1,0:T(8,128)(2,1)} %collective-permute-done.7.near, bf16[256,4096]{1,0:T(8,128)(2,1)S(1)} %bitcast.46, bf16[256,4096]{1,0:T(8,128)(2,1)} %collective-permute-done.6.cross, bf16[256,4096]{1,0:T(8,128)(2,1)} %bitcast.22.other, ...), custom_call_target="tpu_custom_call" | custom-call | flops 1 | bytes 1 | tf_op jit(solution)/shard_map/pairs/pallas_call | solution.py:98
  112.2 4.8 %collective-permute-start.8 = (bf16[256,2560]{1,0:T(8,128)(2,1)S(1)}, bf16[256,2560]{1,0:T(8,128)(2,1)S(1)}, u32[]{:S(2)}, u32[]{:S(2)}) collective-permute-start(bf16[256,2560]{1,0:T(8,128)(2,1)S(1)} %copy-done.10), channel_id=1, source_target_pairs={{0,8},{12,4},{1,9},{13,5},{2,10},{14,6},{3,11},{15,7},{16,24},{28,... | collective-permute-start | bytes 3932168 | tf_op jit(solution)/shard_map/ppermute | solution.py:353
  119.3 40.3 %collective-permute-done.4.far = bf16[256,5120]{1,0:T(8,128)(2,1)} collective-permute-done((bf16[256,5120]{1,0:T(8,128)(2,1)}, bf16[256,5120]{1,0:T(8,128)(2,1)}, u32[]{:S(2)}, u32[]{:S(2)}) %collective-permute-start.4) | collective-permute-done | bytes 2621472 | tf_op jit(solution)/shard_map/ppermute | solution.py:353
  159.7 8.5 %meet.4 = (f32[3,256,256]{2,1,0:T(8,128)S(1)}, f32[4,16,1024]{2,1,0:T(8,128)S(1)}, f32[4,16,1024]{2,1,0:T(8,128)S(1)}) custom-call(s32[4]{0:T(128)S(1)} %pad_add_fusion.at, bf16[256,5120]{1,0:T(8,128)(2,1)} %collective-permute-done.4.far, bf16[256,4096]{1,0:T(8,128)(2,1)S(1)} %copy-done.9, bf16[256,4096]{1,0:T(8,128)(2,1)S(1)} %bitcast.53, ...), custom_call_target="tpu_custom_call" | custom-call | flops 1 | bytes 1 | tf_op jit(solution)/shard_map/meet/pallas_call | solution.py:98
  168.2 3.4 %meet.5 = (f32[3,256,256]{2,1,0:T(8,128)S(1)}, f32[4,16,1280]{2,1,0:T(8,128)S(1)}, f32[4,16,1280]{2,1,0:T(8,128)S(1)}) custom-call(s32[4]{0:T(128)S(1)} %pad_add_fusion.at, bf16[256,5120]{1,0:T(8,128)(2,1)} %collective-permute-done.4.far, bf16[256,4096]{1,0:T(8,128)(2,1)} %collective-permute-done.7.near, bf16[256,4096]{1,0:T(8,128)(2,1)S(1)} %bitcast.47, ...), custom_call_target="tpu_custom_call" | custom-call | flops 1 | bytes 1 | tf_op jit(solution)/shard_map/meet/pallas_call | solution.py:98
  173.1 5.3 %collective-permute-start.5 = (bf16[256,512]{1,0:T(8,128)(2,1)S(1)}, bf16[256,512]{1,0:T(8,128)(2,1)S(1)}, u32[]{:S(2)}, u32[]{:S(2)}) collective-permute-start(bf16[256,512]{1,0:T(8,128)(2,1)S(1)} %slice.11), channel_id=1, source_target_pairs={{0,8},{12,4},{1,9},{13,5},{2,10},{14,6},{3,11},{15,7},{16,24},{28,... | collective-permute-start | bytes 786440 | tf_op jit(solution)/shard_map/ppermute | solution.py:353
  179.4 8.3 %collective-permute-done.8.far = bf16[256,2560]{1,0:T(8,128)(2,1)S(1)} collective-permute-done((bf16[256,2560]{1,0:T(8,128)(2,1)S(1)}, bf16[256,2560]{1,0:T(8,128)(2,1)S(1)}, u32[]{:S(2)}, u32[]{:S(2)}) %collective-permute-start.8) | collective-permute-done | bytes 1310752 | tf_op jit(solution)/shard_map/ppermute | solution.py:353
  187.6 6.2 %meet.6 = (f32[3,256,256]{2,1,0:T(8,128)S(1)}, f32[4,16,640]{2,1,0:T(8,128)S(1)}, f32[4,16,640]{2,1,0:T(8,128)S(1)}) custom-call(s32[4]{0:T(128)S(1)} %pad_add_fusion.at, bf16[256,2560]{1,0:T(8,128)(2,1)S(1)} %collective-permute-done.8.far, bf16[256,4096]{1,0:T(8,128)(2,1)} %collective-permute-done.7.near, bf16[256,4096]{1,0:T(8,128)(2,1)S(1)} %bitcast.48, ...), custom_call_target="tpu_custom_call" | custom-call | flops 1 | bytes 1 | tf_op jit(solution)/shard_map/meet/pallas_call | solution.py:98
  193.9 2.5 %meet.7 = (f32[2,256,256]{2,1,0:T(8,128)S(1)}, f32[2,256,256]{2,1,0:T(8,128)S(1)}, f32[4,16,768]{2,1,0:T(8,128)S(1)}, f32[4,16,768]{2,1,0:T(8,128)S(1)}) custom-call(s32[4]{0:T(128)S(1)} %pad_add_fusion.at, bf16[256,512]{1,0:T(8,128)(2,1)S(1)} %collective-permute-done.5.far, bf16[256,4096]{1,0:T(8,128)(2,1)} %collective-permute-done.7.near, ...), custom_call_target="tpu_custom_call" | custom-call | flops 1 | bytes 1 | tf_op jit(solution)/shard_map/meet/pallas_call | solution.py:98
  200.4 3.7 %collective-permute-done.15.core_got.got = f32[4,16,768]{2,1,0:T(8,128)S(1)} collective-permute-done((f32[4,16,768]{2,1,0:T(8,128)S(1)}, f32[4,16,768]{2,1,0:T(8,128)S(1)}, u32[]{:S(2)}, u32[]{:S(2)}) %collective-permute-start.15) | collective-permute-done | bytes 196640 | tf_op jit(solution)/shard_map/ppermute | solution.py:416
  209.8 7.0 %collective-permute-done.18.near = bf16[384,256]{1,0:T(8,128)(2,1)S(1)} collective-permute-done((bf16[384,256]{1,0:T(8,128)(2,1)S(1)}, bf16[384,256]{1,0:T(8,128)(2,1)S(1)}, u32[]{:S(2)}, u32[]{:S(2)}) %collective-permute-start.18) | collective-permute-done | bytes 196640 | tf_op jit(solution)/shard_map/ppermute | solution.py:436
  (79 shorter events, 46.9 us)
Async XLA Ops:
  3.7 25.5 %collective-permute-start = (bf16[128,8,512]{2,1,0:T(8,128)(2,1)}, bf16[128,8,512]{2,1,0:T(8,128)(2,1)}, u32[]{:S(2)}, u32[]{:S(2)}) collective-permute-start(bf16[128,8,512]{2,1,0:T(8,128)(2,1)} %get-tuple-element.92), channel_id=1, source_target_pairs={{4,8},{8,4},{5,9},{9,5},{6,10},{10,6},{7,11},{11,7},{20,24},{24,20... | collective-permute-start | bytes 3145736 | tf_op jit(solution)/shard_map/ppermute | solution.py:324
  5.4 46.9 %collective-permute-start.2 = (bf16[128,8,512]{2,1,0:T(8,128)(2,1)}, bf16[128,8,512]{2,1,0:T(8,128)(2,1)}, u32[]{:S(2)}, u32[]{:S(2)}) collective-permute-start(bf16[128,8,512]{2,1,0:T(8,128)(2,1)} %get-tuple-element.101), channel_id=1, source_target_pairs={{0,4},{12,8},{1,5},{13,9},{2,6},{14,10},{3,7},{15,11},{16,20},{28,... | collective-permute-start | bytes 3145736 | tf_op jit(solution)/shard_map/ppermute | solution.py:325
  16.1 34.6 %collective-permute-start.1 = (bf16[128,8,512]{2,1,0:T(8,128)(2,1)}, bf16[128,8,512]{2,1,0:T(8,128)(2,1)}, u32[]{:S(2)}, u32[]{:S(2)}) collective-permute-start(bf16[128,8,512]{2,1,0:T(8,128)(2,1)} %get-tuple-element.97), channel_id=1, source_target_pairs={{4,8},{8,4},{5,9},{9,5},{6,10},{10,6},{7,11},{11,7},{20,24},{24,20... | collective-permute-start | bytes 3145736 | tf_op jit(solution)/shard_map/ppermute | solution.py:324
  17.8 40.7 %collective-permute-start.3 = (bf16[128,8,512]{2,1,0:T(8,128)(2,1)}, bf16[128,8,512]{2,1,0:T(8,128)(2,1)}, u32[]{:S(2)}, u32[]{:S(2)}) collective-permute-start(bf16[128,8,512]{2,1,0:T(8,128)(2,1)} %get-tuple-element.106), channel_id=1, source_target_pairs={{0,4},{12,8},{1,5},{13,9},{2,6},{14,10},{3,7},{15,11},{16,20},{28,... | collective-permute-start | bytes 3145736 | tf_op jit(solution)/shard_map/ppermute | solution.py:325
  24.0 59.7 %collective-permute-start.6 = (bf16[256,4096]{1,0:T(8,128)(2,1)}, bf16[256,4096]{1,0:T(8,128)(2,1)}, u32[]{:S(2)}, u32[]{:S(2)}) collective-permute-start(bf16[256,4096]{1,0:T(8,128)(2,1)} %bitcast.22.other), channel_id=1, source_target_pairs={{4,8},{8,4},{5,9},{9,5},{6,10},{10,6},{7,11},{11,7},{20,24},{24,20... | collective-permute-start | bytes 6291464 | tf_op jit(solution)/shard_map/ppermute | solution.py:326
  33.7 69.6 %collective-permute-start.7 = (bf16[256,4096]{1,0:T(8,128)(2,1)S(1)}, bf16[256,4096]{1,0:T(8,128)(2,1)}, u32[]{:S(2)}, u32[]{:S(2)}) collective-permute-start(bf16[256,4096]{1,0:T(8,128)(2,1)S(1)} %bitcast.45), channel_id=1, source_target_pairs={{0,4},{12,8},{1,5},{13,9},{2,6},{14,10},{3,7},{15,11},{16,20},{28,... | collective-permute-start | bytes 6291464 | tf_op jit(solution)/shard_map/ppermute | solution.py:328
  61.7 97.9 %collective-permute-start.4 = (bf16[256,5120]{1,0:T(8,128)(2,1)}, bf16[256,5120]{1,0:T(8,128)(2,1)}, u32[]{:S(2)}, u32[]{:S(2)}) collective-permute-start(bf16[256,5120]{1,0:T(8,128)(2,1)} %pad_maximum_fusion), channel_id=1, source_target_pairs={{0,8},{12,4},{1,9},{13,5},{2,10},{14,6},{3,11},{15,7},{16,24},{28,... | collective-permute-start | bytes 7864328 | tf_op jit(solution)/shard_map/ppermute | solution.py:353
  83.7 28.5 %copy-start.10 = (bf16[256,2560]{1,0:T(8,128)(2,1)S(1)}, bf16[256,2560]{1,0:T(8,128)(2,1)}, u32[]{:S(2)}) copy-start(bf16[256,2560]{1,0:T(8,128)(2,1)} %slice.10) | copy-start | bytes 3932164
  103.4 56.3 %copy-start.7 = (bf16[256,4096]{1,0:T(8,128)(2,1)S(1)}, bf16[256,4096]{1,0:T(8,128)(2,1)}, u32[]{:S(2)}) copy-start(bf16[256,4096]{1,0:T(8,128)(2,1)} %pad_maximum_fusion.1.cross) | copy-start | bytes 6291460
  103.4 56.3 %copy-start.9 = (bf16[256,4096]{1,0:T(8,128)(2,1)S(1)}, bf16[256,4096]{1,0:T(8,128)(2,1)}, u32[]{:S(2)}) copy-start(bf16[256,4096]{1,0:T(8,128)(2,1)} %pad_maximum_fusion.2.near) | copy-start | bytes 6291460
  112.1 47.5 %copy-start.5 = (bf16[32,8,8,512]{3,1,2,0:T(8,128)(2,1)S(1)}, bf16[32,8,8,512]{3,1,2,0:T(8,128)(2,1)}, u32[]{:S(2)}) copy-start(bf16[32,8,8,512]{3,1,2,0:T(8,128)(2,1)} %copy.16) | copy-start | bytes 6291460
  112.2 4.9 %collective-permute-start.9 = (f32[2,768,256]{2,1,0:T(8,128)S(1)}, f32[2,768,256]{2,1,0:T(8,128)S(1)}, u32[]{:S(2)}, u32[]{:S(2)}) collective-permute-start(f32[2,768,256]{2,1,0:T(8,128)S(1)} %get-tuple-element.126), channel_id=1, source_target_pairs={{0,1},{1,0},{2,3},{3,2},{4,5},{5,4},{6,7},{7,6},{8,9},{9,8},{10,11... | collective-permute-start | bytes 4718600 | tf_op jit(solution)/shard_map/ppermute | solution.py:391
  112.2 75.4 %collective-permute-start.8 = (bf16[256,2560]{1,0:T(8,128)(2,1)S(1)}, bf16[256,2560]{1,0:T(8,128)(2,1)S(1)}, u32[]{:S(2)}, u32[]{:S(2)}) collective-permute-start(bf16[256,2560]{1,0:T(8,128)(2,1)S(1)} %copy-done.10), channel_id=1, source_target_pairs={{0,8},{12,4},{1,9},{13,5},{2,10},{14,6},{3,11},{15,7},{16,24},{28,... | collective-permute-start | bytes 3932168 | tf_op jit(solution)/shard_map/ppermute | solution.py:353
  117.8 41.9 %collective-permute-start.10 = (f32[768,256]{1,0:T(8,128)S(1)}, f32[768,256]{1,0:T(8,128)S(1)}, u32[]{:S(2)}, u32[]{:S(2)}) collective-permute-start(f32[768,256]{1,0:T(8,128)S(1)} %get-tuple-element.127), channel_id=1, source_target_pairs={{0,2},{2,0},{1,3},{3,1},{4,6},{6,4},{5,7},{7,5},{8,10},{10,8},{9,1... | collective-permute-start | bytes 2359304 | tf_op jit(solution)/shard_map/ppermute | solution.py:393
  171.6 7.1 %collective-permute-start.11 = (f32[4,16,1280]{2,1,0:T(8,128)S(1)}, f32[4,16,1280]{2,1,0:T(8,128)S(1)}, u32[]{:S(2)}, u32[]{:S(2)}) collective-permute-start(f32[4,16,1280]{2,1,0:T(8,128)S(1)} %get-tuple-element.138), channel_id=1, source_target_pairs={{0,2},{2,0},{1,3},{3,1},{4,6},{6,4},{5,7},{7,5},{8,10},{10,8},{9,1... | collective-permute-start | bytes 983048 | tf_op jit(solution)/shard_map/ppermute | solution.py:397
  173.1 20.7 %collective-permute-start.5 = (bf16[256,512]{1,0:T(8,128)(2,1)S(1)}, bf16[256,512]{1,0:T(8,128)(2,1)S(1)}, u32[]{:S(2)}, u32[]{:S(2)}) collective-permute-start(bf16[256,512]{1,0:T(8,128)(2,1)S(1)} %slice.11), channel_id=1, source_target_pairs={{0,8},{12,4},{1,9},{13,5},{2,10},{14,6},{3,11},{15,7},{16,24},{28,... | collective-permute-start | bytes 786440 | tf_op jit(solution)/shard_map/ppermute | solution.py:353
  196.3 2.3 %collective-permute-start.12 = (f32[2,256,256]{2,1,0:T(8,128)S(1)}, f32[2,256,256]{2,1,0:T(8,128)S(1)}, u32[]{:S(2)}, u32[]{:S(2)}) collective-permute-start(f32[2,256,256]{2,1,0:T(8,128)S(1)} %get-tuple-element.159), channel_id=1, source_target_pairs={{0,1},{1,0},{2,3},{3,2},{4,5},{5,4},{6,7},{7,6},{8,9},{9,8},{10,11... | collective-permute-start | bytes 1572872 | tf_op jit(solution)/shard_map/ppermute | solution.py:421
  196.4 7.8 %collective-permute-start.15 = (f32[4,16,768]{2,1,0:T(8,128)S(1)}, f32[4,16,768]{2,1,0:T(8,128)S(1)}, u32[]{:S(2)}, u32[]{:S(2)}) collective-permute-start(f32[4,16,768]{2,1,0:T(8,128)S(1)} %get-tuple-element.165), channel_id=1, source_target_pairs={{0,2},{2,0},{1,3},{3,1},{4,6},{6,4},{5,7},{7,5},{8,10},{10,8},{9,1... | collective-permute-start | bytes 589832 | tf_op jit(solution)/shard_map/ppermute | solution.py:416
  197.9 8.1 %collective-permute-start.14 = (bf16[336,256]{1,0:T(8,128)(2,1)S(1)}, bf16[336,256]{1,0:T(8,128)(2,1)S(1)}, u32[]{:S(2)}, u32[]{:S(2)}) collective-permute-start(bf16[336,256]{1,0:T(8,128)(2,1)S(1)} %get-tuple-element.162), channel_id=1, source_target_pairs={{4,8},{8,4},{5,9},{9,5},{6,10},{10,6},{7,11},{11,7},{20,24},{24,20... | collective-permute-start | bytes 516104 | tf_op jit(solution)/shard_map/ppermute | solution.py:426
  199.2 7.3 %collective-permute-start.13 = (bf16[256,256]{1,0:T(8,128)(2,1)S(1)}, bf16[256,256]{1,0:T(8,128)(2,1)S(1)}, u32[]{:S(2)}, u32[]{:S(2)}) collective-permute-start(bf16[256,256]{1,0:T(8,128)(2,1)S(1)} %get-tuple-element.161), channel_id=1, source_target_pairs={{0,2},{2,0},{1,3},{3,1},{4,6},{6,4},{5,7},{7,5},{8,10},{10,8},{9,1... | collective-permute-start | bytes 393224 | tf_op jit(solution)/shard_map/ppermute | solution.py:435
  204.8 12.1 %collective-permute-start.18 = (bf16[384,256]{1,0:T(8,128)(2,1)S(1)}, bf16[384,256]{1,0:T(8,128)(2,1)S(1)}, u32[]{:S(2)}, u32[]{:S(2)}) collective-permute-start(bf16[384,256]{1,0:T(8,128)(2,1)S(1)} %get-tuple-element.170), channel_id=1, source_target_pairs={{4,0},{8,12},{5,1},{9,13},{6,2},{10,14},{7,3},{11,15},{20,16},{24,... | collective-permute-start | bytes 589832 | tf_op jit(solution)/shard_map/ppermute | solution.py:436
  207.2 9.7 %collective-permute-start.16 = (bf16[384,256]{1,0:T(8,128)(2,1)S(1)}, bf16[384,256]{1,0:T(8,128)(2,1)S(1)}, u32[]{:S(2)}, u32[]{:S(2)}) collective-permute-start(bf16[384,256]{1,0:T(8,128)(2,1)S(1)} %get-tuple-element.167), channel_id=1, source_target_pairs={{4,12},{8,0},{5,13},{9,1},{6,14},{10,2},{7,15},{11,3},{20,28},{24,... | collective-permute-start | bytes 589832 | tf_op jit(solution)/shard_map/ppermute | solution.py:454
  208.5 8.4 %collective-permute-start.17 = (bf16[256,256]{1,0:T(8,128)(2,1)S(1)}, bf16[256,256]{1,0:T(8,128)(2,1)S(1)}, u32[]{:S(2)}, u32[]{:S(2)}) collective-permute-start(bf16[256,256]{1,0:T(8,128)(2,1)S(1)} %get-tuple-element.168), channel_id=1, source_target_pairs={{4,3},{5,7},{6,11},{9,4},{10,8},{11,12},{20,19},{21,23},{22,27},{2... | collective-permute-start | bytes 393224 | tf_op jit(solution)/shard_map/ppermute | solution.py:455
  209.2 0.7 collective-permute-start.19
  (8 other events, 65.9 us)

commit v6 on v5

--- a/solution.py
+++ b/solution.py
@@ -338,7 +338,7 @@
     basis = jnp.stack([lax.dynamic_slice_in_dim(x_basis, p * rows, rows, 0).T for p in places])
     y_own = lax.dynamic_slice_in_dim(y_basis, gy * ny, ny, 0)
 
-    cuts = [(0, 10), (10, 15), (15, 16)]
+    cuts = [(0, 10), (10, 14), (14, 16)]
 
     def piece(lo, hi):
         parts = []

time: 220 us -> 219 us (level)
    ppermute x3, waiting for transfers between devices: 48.6 us -> 38.9 us  [send_far(): return (lax.ppermute(data, 'gx', FAR), *gate)]
    ppermute x2, waiting for transfers between devices: 4.05 us -> 9.34 us  [meeting(): core_got = lax.ppermute(core[1], 'gy', SWAP)]
    ppermute x2, waiting for transfers between devices: 0.01 us -> 3.4 us  [meeting(): lax.ppermute(give, 'gz', SWAP)]
    slice x3 -> x2, local copies, waits for them, and re-layouts: 4.53 us -> 3.59 us  [piece(): oth[h][:, (a - h * nz) * ny:(b - h * nz) * ny]]
  transfers between devices with their start and end apart: 20 -> 20, of which waited for: 8 -> 9; matrix products, arithmetic and copies ran while one was open for 15% -> 14% of each run, Pallas kernels for 16% -> 16%
where the time goes in v6:
time: 219 us; the launch traced here: 217 us
  waiting for transfers between devices  81.2 us (37%)
  starting transfers between devices  54.7 us (25%)
  Pallas kernels  39.8 us (18%)
  local copies, waits for them, and re-layouts  35.6 us (16%)
  other arithmetic  5.06 us (2%)
    pallas_call x12, Pallas kernels, call(): pl.pallas_call(kernel, out_shape=tuple((jax.ShapeDtypeStruct(o, t) for o,...  39.8 us
    ppermute x3, waiting for transfers between devices, send_far(): return (lax.ppermute(data, 'gx', FAR), *gate)  38.9 us
    unnamed x36, local copies, waits for them, and re-layouts  19.9 us
    ppermute x3, starting transfers between devices, send_far(): return (lax.ppermute(data, 'gx', FAR), *gate)  19.7 us
    ppermute x1, waiting for transfers between devices, meeting(): near[1] = lax.ppermute(own[1], 'gx', NEAR)  19.7 us
    ppermute x2, starting transfers between devices, meeting(): near_raw = [lax.ppermute(a, 'gx', NEAR) for a in own_raw]  10 us
    ppermute x2, waiting for transfers between devices, meeting(): core_got = lax.ppermute(core[1], 'gy', SWAP)  9.34 us
    ppermute x1, starting transfers between devices, meeting(): near[1] = lax.ppermute(own[1], 'gx', NEAR)  9.03 us
  transfers between devices with their start and end apart: 20, of which 9 were waited for; matrix products, arithmetic and copies ran while one was open for 14% of the time, Pallas kernels for 16%

profile of v6, /device:TPU:0, one launch (start us, length us, event | category | flops | bytes accessed | tf_op | source)
XLA Modules:
  0.0 217.4 jit_solution(14652971786659641874)
XLA Ops:
  0.7 3.1 %dynamic-slice_bitcast_fusion.3 = (bf16[128,8,512]{2,1,0:T(8,128)(2,1)}, bf16[128,8,512]{2,1,0:T(8,128)(2,1)}) fusion(bf16[256,4,8,512]{3,2,1,0:T(8,128)(2,1)} %param.3, s32[]{:T(128)S(6)} %select_n.48, s32[]{:T(128)S(6)} %select_n.47), kind=kLoop, calls=%fused_computation.6 | loop fusion | bytes 4194312 | tf_op jit(solution)/shard_map/reshape | solution.py:307
  5.4 7.8 %collective-permute-start.2 = (bf16[128,8,512]{2,1,0:T(8,128)(2,1)}, bf16[128,8,512]{2,1,0:T(8,128)(2,1)}, u32[]{:S(2)}, u32[]{:S(2)}) collective-permute-start(bf16[128,8,512]{2,1,0:T(8,128)(2,1)} %get-tuple-element.101), channel_id=1, source_target_pairs={{0,4},{12,8},{1,5},{13,9},{2,6},{14,10},{3,7},{15,11},{16,20},{28,... | collective-permute-start | bytes 3145736 | tf_op jit(solution)/shard_map/ppermute | solution.py:325
  13.1 3.1 %dynamic-slice_bitcast_fusion.1 = (bf16[128,8,512]{2,1,0:T(8,128)(2,1)}, bf16[128,8,512]{2,1,0:T(8,128)(2,1)}) fusion(bf16[256,4,8,512]{3,2,1,0:T(8,128)(2,1)} %param.3, s32[]{:T(128)S(6)} %select_n.48, s32[]{:T(128)S(6)} %select_n.47), kind=kLoop, calls=%fused_computation.4 | loop fusion | bytes 4194312 | tf_op jit(solution)/shard_map/reshape | solution.py:307
  17.8 2.3 %collective-permute-start.3 = (bf16[128,8,512]{2,1,0:T(8,128)(2,1)}, bf16[128,8,512]{2,1,0:T(8,128)(2,1)}, u32[]{:S(2)}, u32[]{:S(2)}) collective-permute-start(bf16[128,8,512]{2,1,0:T(8,128)(2,1)} %get-tuple-element.106), channel_id=1, source_target_pairs={{0,4},{12,8},{1,5},{13,9},{2,6},{14,10},{3,7},{15,11},{16,20},{28,... | collective-permute-start | bytes 3145736 | tf_op jit(solution)/shard_map/ppermute | solution.py:325
  29.3 9.0 %collective-permute-start.7 = (bf16[256,4096]{1,0:T(8,128)(2,1)S(1)}, bf16[256,4096]{1,0:T(8,128)(2,1)}, u32[]{:S(2)}, u32[]{:S(2)}) collective-permute-start(bf16[256,4096]{1,0:T(8,128)(2,1)S(1)} %bitcast.45), channel_id=1, source_target_pairs={{0,4},{12,8},{1,5},{13,9},{2,6},{14,10},{3,7},{15,11},{16,20},{28,... | collective-permute-start | bytes 6291464 | tf_op jit(solution)/shard_map/ppermute | solution.py:328
  39.6 2.5 %constant_dynamic-slice_fusion.5 = (bf16[256,1,8,512]{3,2,1,0:T(8,128)(2,1)S(1)}, bf16[256,1,8,512]{3,2,1,0:T(8,128)(2,1)S(1)}) fusion(bf16[256,4,8,512]{3,2,1,0:T(8,128)(2,1)} %param.3, s32[]{:T(128)S(6)} %select_n.48, s32[]{:T(128)S(6)} %select_n.47), kind=kLoop, calls=%fused_computation.14 | loop fusion | bytes 8388616 | tf_op jit(solution)/shard_map/dynamic_slice | solution.py:307
  42.1 2.3 %slice.10 = bf16[256,2048]{1,0:T(8,128)(2,1)} slice(bf16[256,4096]{1,0:T(8,128)(2,1)} %bitcast.22.other), slice={[0:256], [1024:3072]} | slice | bytes 2097152 | tf_op jit(solution)/shard_map/slice | solution.py:348
  44.4 2.3 %copy.16 = bf16[32,8,8,512]{3,1,2,0:T(8,128)(2,1)} copy(bf16[32,8,8,512]{3,2,1,0:T(8,128)(2,1)S(1)} %bitcast.55) | data formatting | bytes 4194304
  56.2 2.4 %collective-permute-done.3 = bf16[128,8,512]{2,1,0:T(8,128)(2,1)} collective-permute-done((bf16[128,8,512]{2,1,0:T(8,128)(2,1)}, bf16[128,8,512]{2,1,0:T(8,128)(2,1)}, u32[]{:S(2)}, u32[]{:S(2)}) %collective-permute-start.3) | collective-permute-done | bytes 1048608 | tf_op jit(solution)/shard_map/ppermute | solution.py:325
  61.7 9.8 %collective-permute-start.4 = (bf16[256,5120]{1,0:T(8,128)(2,1)}, bf16[256,5120]{1,0:T(8,128)(2,1)}, u32[]{:S(2)}, u32[]{:S(2)}) collective-permute-start(bf16[256,5120]{1,0:T(8,128)(2,1)} %pad_maximum_fusion), channel_id=1, source_target_pairs={{0,8},{12,4},{1,9},{13,5},{2,10},{14,6},{3,11},{15,7},{16,24},{28,... | collective-permute-start | bytes 7864328 | tf_op jit(solution)/shard_map/ppermute | solution.py:353
  78.0 5.7 %pairs.2.rest_0_ = f32[4,256,256]{2,1,0:T(8,128)S(1)} custom-call(s32[4]{0:T(128)S(1)} %pad_add_fusion.at, bf16[256,4096]{1,0:T(8,128)(2,1)S(1)} %copy-done.8, bf16[256,4096]{1,0:T(8,128)(2,1)S(1)} %bitcast.52, bf16[256,4096]{1,0:T(8,128)(2,1)S(1)} %copy-done.6, bf16[256,4096]{1,0:T(8,128)(2,1)S(1)} %bitcast.51), custom_call_target="tpu_custom_call" | custom-call | flops 1 | bytes 1 | tf_op jit(solution)/shard_map/pairs/pallas_call | solution.py:98
  83.7 19.7 %collective-permute-done.7.near = bf16[256,4096]{1,0:T(8,128)(2,1)} collective-permute-done((bf16[256,4096]{1,0:T(8,128)(2,1)S(1)}, bf16[256,4096]{1,0:T(8,128)(2,1)}, u32[]{:S(2)}, u32[]{:S(2)}) %collective-permute-start.7) | collective-permute-done | bytes 2097184 | tf_op jit(solution)/shard_map/ppermute | solution.py:328
  103.4 8.8 %pairs.3 = (f32[2,768,256]{2,1,0:T(8,128)S(1)}, f32[2,768,256]{2,1,0:T(8,128)S(1)}) custom-call(s32[4]{0:T(128)S(1)} %pad_add_fusion.at, bf16[256,4096]{1,0:T(8,128)(2,1)} %collective-permute-done.7.near, bf16[256,4096]{1,0:T(8,128)(2,1)S(1)} %bitcast.46, bf16[256,4096]{1,0:T(8,128)(2,1)} %collective-permute-done.6.cross, bf16[256,4096]{1,0:T(8,128)(2,1)} %bitcast.22.other, ...), custom_call_target="tpu_custom_call" | custom-call | flops 1 | bytes 1 | tf_op jit(solution)/shard_map/pairs/pallas_call | solution.py:98
  112.3 3.4 %collective-permute-done.9.got = f32[2,768,256]{2,1,0:T(8,128)S(1)} collective-permute-done((f32[2,768,256]{2,1,0:T(8,128)S(1)}, f32[2,768,256]{2,1,0:T(8,128)S(1)}, u32[]{:S(2)}, u32[]{:S(2)}) %collective-permute-start.9) | collective-permute-done | bytes 1572896 | tf_op jit(solution)/shard_map/ppermute | solution.py:391
  118.0 4.4 %collective-permute-start.8 = (bf16[256,2048]{1,0:T(8,128)(2,1)S(1)}, bf16[256,2048]{1,0:T(8,128)(2,1)S(1)}, u32[]{:S(2)}, u32[]{:S(2)}) collective-permute-start(bf16[256,2048]{1,0:T(8,128)(2,1)S(1)} %copy-done.10), channel_id=1, source_target_pairs={{0,8},{12,4},{1,9},{13,5},{2,10},{14,6},{3,11},{15,7},{16,24},{28,... | collective-permute-start | bytes 3145736 | tf_op jit(solution)/shard_map/ppermute | solution.py:353
  122.4 37.2 %collective-permute-done.4.far = bf16[256,5120]{1,0:T(8,128)(2,1)} collective-permute-done((bf16[256,5120]{1,0:T(8,128)(2,1)}, bf16[256,5120]{1,0:T(8,128)(2,1)}, u32[]{:S(2)}, u32[]{:S(2)}) %collective-permute-start.4) | collective-permute-done | bytes 2621472 | tf_op jit(solution)/shard_map/ppermute | solution.py:353
  159.6 5.5 %collective-permute-start.5 = (bf16[256,1024]{1,0:T(8,128)(2,1)S(1)}, bf16[256,1024]{1,0:T(8,128)(2,1)S(1)}, u32[]{:S(2)}, u32[]{:S(2)}) collective-permute-start(bf16[256,1024]{1,0:T(8,128)(2,1)S(1)} %get-tuple-element.112), channel_id=1, source_target_pairs={{0,8},{12,4},{1,9},{13,5},{2,10},{14,6},{3,11},{15,7},{16,24},{28,... | collective-permute-start | bytes 1572872 | tf_op jit(solution)/shard_map/ppermute | solution.py:353
  165.2 8.5 %meet.4 = (f32[3,256,256]{2,1,0:T(8,128)S(1)}, f32[4,16,1024]{2,1,0:T(8,128)S(1)}, f32[4,16,1024]{2,1,0:T(8,128)S(1)}) custom-call(s32[4]{0:T(128)S(1)} %pad_add_fusion.at, bf16[256,5120]{1,0:T(8,128)(2,1)} %collective-permute-done.4.far, bf16[256,4096]{1,0:T(8,128)(2,1)S(1)} %copy-done.9, bf16[256,4096]{1,0:T(8,128)(2,1)S(1)} %bitcast.53, ...), custom_call_target="tpu_custom_call" | custom-call | flops 1 | bytes 1 | tf_op jit(solution)/shard_map/meet/pallas_call | solution.py:98
  173.7 3.4 %meet.5 = (f32[3,256,256]{2,1,0:T(8,128)S(1)}, f32[4,16,1280]{2,1,0:T(8,128)S(1)}, f32[4,16,1280]{2,1,0:T(8,128)S(1)}) custom-call(s32[4]{0:T(128)S(1)} %pad_add_fusion.at, bf16[256,5120]{1,0:T(8,128)(2,1)} %collective-permute-done.4.far, bf16[256,4096]{1,0:T(8,128)(2,1)} %collective-permute-done.7.near, bf16[256,4096]{1,0:T(8,128)(2,1)S(1)} %bitcast.47, ...), custom_call_target="tpu_custom_call" | custom-call | flops 1 | bytes 1 | tf_op jit(solution)/shard_map/meet/pallas_call | solution.py:98
  178.6 5.6 %collective-permute-done.11.core_got = f32[4,16,1280]{2,1,0:T(8,128)S(1)} collective-permute-done((f32[4,16,1280]{2,1,0:T(8,128)S(1)}, f32[4,16,1280]{2,1,0:T(8,128)S(1)}, u32[]{:S(2)}, u32[]{:S(2)}) %collective-permute-start.11) | collective-permute-done | bytes 327712 | tf_op jit(solution)/shard_map/ppermute | solution.py:397
  184.9 5.2 %meet.6 = (f32[3,256,256]{2,1,0:T(8,128)S(1)}, f32[4,16,512]{2,1,0:T(8,128)S(1)}, f32[4,16,512]{2,1,0:T(8,128)S(1)}) custom-call(s32[4]{0:T(128)S(1)} %pad_add_fusion.at, bf16[256,2048]{1,0:T(8,128)(2,1)S(1)} %collective-permute-done.8.far, bf16[256,4096]{1,0:T(8,128)(2,1)} %collective-permute-done.7.near, bf16[256,4096]{1,0:T(8,128)(2,1)S(1)} %bitcast.48, ...), custom_call_target="tpu_custom_call" | custom-call | flops 1 | bytes 1 | tf_op jit(solution)/shard_map/meet/pallas_call | solution.py:98
  191.8 3.4 %meet.7 = (f32[2,256,256]{2,1,0:T(8,128)S(1)}, f32[2,256,256]{2,1,0:T(8,128)S(1)}, f32[4,16,768]{2,1,0:T(8,128)S(1)}, f32[4,16,768]{2,1,0:T(8,128)S(1)}) custom-call(s32[4]{0:T(128)S(1)} %pad_add_fusion.at, bf16[256,1024]{1,0:T(8,128)(2,1)S(1)} %collective-permute-done.5.far, bf16[256,4096]{1,0:T(8,128)(2,1)} %collective-permute-done.7.near, ...), custom_call_target="tpu_custom_call" | custom-call | flops 1 | bytes 1 | tf_op jit(solution)/shard_map/meet/pallas_call | solution.py:98
  199.3 3.7 %collective-permute-done.15.core_got.got = f32[4,16,768]{2,1,0:T(8,128)S(1)} collective-permute-done((f32[4,16,768]{2,1,0:T(8,128)S(1)}, f32[4,16,768]{2,1,0:T(8,128)S(1)}, u32[]{:S(2)}, u32[]{:S(2)}) %collective-permute-start.15) | collective-permute-done | bytes 196640 | tf_op jit(solution)/shard_map/ppermute | solution.py:416
  208.7 7.0 %collective-permute-done.18.near = bf16[384,256]{1,0:T(8,128)(2,1)S(1)} collective-permute-done((bf16[384,256]{1,0:T(8,128)(2,1)S(1)}, bf16[384,256]{1,0:T(8,128)(2,1)S(1)}, u32[]{:S(2)}, u32[]{:S(2)}) %collective-permute-start.18) | collective-permute-done | bytes 196640 | tf_op jit(solution)/shard_map/ppermute | solution.py:436
  (78 shorter events, 50.2 us)
Async XLA Ops:
  0.6 28.5 %copy-start = (bf16[1024,128]{1,0:T(8,128)(2,1)S(1)}, bf16[1024,128]{1,0:T(8,128)(2,1)}, u32[]{:S(2)}) copy-start(bf16[1024,128]{1,0:T(8,128)(2,1)} %param.5) | copy-start | bytes 786436
  3.7 25.5 %collective-permute-start = (bf16[128,8,512]{2,1,0:T(8,128)(2,1)}, bf16[128,8,512]{2,1,0:T(8,128)(2,1)}, u32[]{:S(2)}, u32[]{:S(2)}) collective-permute-start(bf16[128,8,512]{2,1,0:T(8,128)(2,1)} %get-tuple-element.92), channel_id=1, source_target_pairs={{4,8},{8,4},{5,9},{9,5},{6,10},{10,6},{7,11},{11,7},{20,24},{24,20... | collective-permute-start | bytes 3145736 | tf_op jit(solution)/shard_map/ppermute | solution.py:324
  5.4 46.0 %collective-permute-start.2 = (bf16[128,8,512]{2,1,0:T(8,128)(2,1)}, bf16[128,8,512]{2,1,0:T(8,128)(2,1)}, u32[]{:S(2)}, u32[]{:S(2)}) collective-permute-start(bf16[128,8,512]{2,1,0:T(8,128)(2,1)} %get-tuple-element.101), channel_id=1, source_target_pairs={{0,4},{12,8},{1,5},{13,9},{2,6},{14,10},{3,7},{15,11},{16,20},{28,... | collective-permute-start | bytes 3145736 | tf_op jit(solution)/shard_map/ppermute | solution.py:325
  16.2 33.6 %collective-permute-start.1 = (bf16[128,8,512]{2,1,0:T(8,128)(2,1)}, bf16[128,8,512]{2,1,0:T(8,128)(2,1)}, u32[]{:S(2)}, u32[]{:S(2)}) collective-permute-start(bf16[128,8,512]{2,1,0:T(8,128)(2,1)} %get-tuple-element.97), channel_id=1, source_target_pairs={{4,8},{8,4},{5,9},{9,5},{6,10},{10,6},{7,11},{11,7},{20,24},{24,20... | collective-permute-start | bytes 3145736 | tf_op jit(solution)/shard_map/ppermute | solution.py:324
  17.8 40.7 %collective-permute-start.3 = (bf16[128,8,512]{2,1,0:T(8,128)(2,1)}, bf16[128,8,512]{2,1,0:T(8,128)(2,1)}, u32[]{:S(2)}, u32[]{:S(2)}) collective-permute-start(bf16[128,8,512]{2,1,0:T(8,128)(2,1)} %get-tuple-element.106), channel_id=1, source_target_pairs={{0,4},{12,8},{1,5},{13,9},{2,6},{14,10},{3,7},{15,11},{16,20},{28,... | collective-permute-start | bytes 3145736 | tf_op jit(solution)/shard_map/ppermute | solution.py:325
  24.1 59.6 %collective-permute-start.6 = (bf16[256,4096]{1,0:T(8,128)(2,1)}, bf16[256,4096]{1,0:T(8,128)(2,1)}, u32[]{:S(2)}, u32[]{:S(2)}) collective-permute-start(bf16[256,4096]{1,0:T(8,128)(2,1)} %bitcast.22.other), channel_id=1, source_target_pairs={{4,8},{8,4},{5,9},{9,5},{6,10},{10,6},{7,11},{11,7},{20,24},{24,20... | collective-permute-start | bytes 6291464 | tf_op jit(solution)/shard_map/ppermute | solution.py:326
  29.3 74.1 %collective-permute-start.7 = (bf16[256,4096]{1,0:T(8,128)(2,1)S(1)}, bf16[256,4096]{1,0:T(8,128)(2,1)}, u32[]{:S(2)}, u32[]{:S(2)}) collective-permute-start(bf16[256,4096]{1,0:T(8,128)(2,1)S(1)} %bitcast.45), channel_id=1, source_target_pairs={{0,4},{12,8},{1,5},{13,9},{2,6},{14,10},{3,7},{15,11},{16,20},{28,... | collective-permute-start | bytes 6291464 | tf_op jit(solution)/shard_map/ppermute | solution.py:328
  61.7 97.9 %collective-permute-start.4 = (bf16[256,5120]{1,0:T(8,128)(2,1)}, bf16[256,5120]{1,0:T(8,128)(2,1)}, u32[]{:S(2)}, u32[]{:S(2)}) collective-permute-start(bf16[256,5120]{1,0:T(8,128)(2,1)} %pad_maximum_fusion), channel_id=1, source_target_pairs={{0,8},{12,4},{1,9},{13,5},{2,10},{14,6},{3,11},{15,7},{16,24},{28,... | collective-permute-start | bytes 7864328 | tf_op jit(solution)/shard_map/ppermute | solution.py:353
  103.4 61.8 %copy-start.7 = (bf16[256,4096]{1,0:T(8,128)(2,1)S(1)}, bf16[256,4096]{1,0:T(8,128)(2,1)}, u32[]{:S(2)}) copy-start(bf16[256,4096]{1,0:T(8,128)(2,1)} %pad_maximum_fusion.1.cross) | copy-start | bytes 6291460
  103.4 61.8 %copy-start.9 = (bf16[256,4096]{1,0:T(8,128)(2,1)S(1)}, bf16[256,4096]{1,0:T(8,128)(2,1)}, u32[]{:S(2)}) copy-start(bf16[256,4096]{1,0:T(8,128)(2,1)} %pad_maximum_fusion.2.near) | copy-start | bytes 6291460
  112.2 53.0 %copy-start.5 = (bf16[32,8,8,512]{3,1,2,0:T(8,128)(2,1)S(1)}, bf16[32,8,8,512]{3,1,2,0:T(8,128)(2,1)}, u32[]{:S(2)}) copy-start(bf16[32,8,8,512]{3,1,2,0:T(8,128)(2,1)} %copy.16) | copy-start | bytes 6291460
  112.2 3.5 %collective-permute-start.9 = (f32[2,768,256]{2,1,0:T(8,128)S(1)}, f32[2,768,256]{2,1,0:T(8,128)S(1)}, u32[]{:S(2)}, u32[]{:S(2)}) collective-permute-start(f32[2,768,256]{2,1,0:T(8,128)S(1)} %get-tuple-element.126), channel_id=1, source_target_pairs={{0,1},{1,0},{2,3},{3,2},{4,5},{5,4},{6,7},{7,6},{8,9},{9,8},{10,11... | collective-permute-start | bytes 4718600 | tf_op jit(solution)/shard_map/ppermute | solution.py:391
  116.4 48.7 %collective-permute-start.10 = (f32[768,256]{1,0:T(8,128)S(1)}, f32[768,256]{1,0:T(8,128)S(1)}, u32[]{:S(2)}, u32[]{:S(2)}) collective-permute-start(f32[768,256]{1,0:T(8,128)S(1)} %get-tuple-element.127), channel_id=1, source_target_pairs={{0,2},{2,0},{1,3},{3,1},{4,6},{6,4},{5,7},{7,5},{8,10},{10,8},{9,1... | collective-permute-start | bytes 2359304 | tf_op jit(solution)/shard_map/ppermute | solution.py:393
  118.0 66.9 %collective-permute-start.8 = (bf16[256,2048]{1,0:T(8,128)(2,1)S(1)}, bf16[256,2048]{1,0:T(8,128)(2,1)S(1)}, u32[]{:S(2)}, u32[]{:S(2)}) collective-permute-start(bf16[256,2048]{1,0:T(8,128)(2,1)S(1)} %copy-done.10), channel_id=1, source_target_pairs={{0,8},{12,4},{1,9},{13,5},{2,10},{14,6},{3,11},{15,7},{16,24},{28,... | collective-permute-start | bytes 3145736 | tf_op jit(solution)/shard_map/ppermute | solution.py:353
  159.6 32.1 %collective-permute-start.5 = (bf16[256,1024]{1,0:T(8,128)(2,1)S(1)}, bf16[256,1024]{1,0:T(8,128)(2,1)S(1)}, u32[]{:S(2)}, u32[]{:S(2)}) collective-permute-start(bf16[256,1024]{1,0:T(8,128)(2,1)S(1)} %get-tuple-element.112), channel_id=1, source_target_pairs={{0,8},{12,4},{1,9},{13,5},{2,10},{14,6},{3,11},{15,7},{16,24},{28,... | collective-permute-start | bytes 1572872 | tf_op jit(solution)/shard_map/ppermute | solution.py:353
  177.1 7.1 %collective-permute-start.11 = (f32[4,16,1280]{2,1,0:T(8,128)S(1)}, f32[4,16,1280]{2,1,0:T(8,128)S(1)}, u32[]{:S(2)}, u32[]{:S(2)}) collective-permute-start(f32[4,16,1280]{2,1,0:T(8,128)S(1)} %get-tuple-element.138), channel_id=1, source_target_pairs={{0,2},{2,0},{1,3},{3,1},{4,6},{6,4},{5,7},{7,5},{8,10},{10,8},{9,1... | collective-permute-start | bytes 983048 | tf_op jit(solution)/shard_map/ppermute | solution.py:397
  195.2 2.3 %collective-permute-start.12 = (f32[2,256,256]{2,1,0:T(8,128)S(1)}, f32[2,256,256]{2,1,0:T(8,128)S(1)}, u32[]{:S(2)}, u32[]{:S(2)}) collective-permute-start(f32[2,256,256]{2,1,0:T(8,128)S(1)} %get-tuple-element.159), channel_id=1, source_target_pairs={{0,1},{1,0},{2,3},{3,2},{4,5},{5,4},{6,7},{7,6},{8,9},{9,8},{10,11... | collective-permute-start | bytes 1572872 | tf_op jit(solution)/shard_map/ppermute | solution.py:421
  195.2 7.8 %collective-permute-start.15 = (f32[4,16,768]{2,1,0:T(8,128)S(1)}, f32[4,16,768]{2,1,0:T(8,128)S(1)}, u32[]{:S(2)}, u32[]{:S(2)}) collective-permute-start(f32[4,16,768]{2,1,0:T(8,128)S(1)} %get-tuple-element.165), channel_id=1, source_target_pairs={{0,2},{2,0},{1,3},{3,1},{4,6},{6,4},{5,7},{7,5},{8,10},{10,8},{9,1... | collective-permute-start | bytes 589832 | tf_op jit(solution)/shard_map/ppermute | solution.py:416
  196.8 8.1 %collective-permute-start.14 = (bf16[336,256]{1,0:T(8,128)(2,1)S(1)}, bf16[336,256]{1,0:T(8,128)(2,1)S(1)}, u32[]{:S(2)}, u32[]{:S(2)}) collective-permute-start(bf16[336,256]{1,0:T(8,128)(2,1)S(1)} %get-tuple-element.162), channel_id=1, source_target_pairs={{4,8},{8,4},{5,9},{9,5},{6,10},{10,6},{7,11},{11,7},{20,24},{24,20... | collective-permute-start | bytes 516104 | tf_op jit(solution)/shard_map/ppermute | solution.py:426
  198.1 7.3 %collective-permute-start.13 = (bf16[256,256]{1,0:T(8,128)(2,1)S(1)}, bf16[256,256]{1,0:T(8,128)(2,1)S(1)}, u32[]{:S(2)}, u32[]{:S(2)}) collective-permute-start(bf16[256,256]{1,0:T(8,128)(2,1)S(1)} %get-tuple-element.161), channel_id=1, source_target_pairs={{0,2},{2,0},{1,3},{3,1},{4,6},{6,4},{5,7},{7,5},{8,10},{10,8},{9,1... | collective-permute-start | bytes 393224 | tf_op jit(solution)/shard_map/ppermute | solution.py:435
  203.6 12.1 %collective-permute-start.18 = (bf16[384,256]{1,0:T(8,128)(2,1)S(1)}, bf16[384,256]{1,0:T(8,128)(2,1)S(1)}, u32[]{:S(2)}, u32[]{:S(2)}) collective-permute-start(bf16[384,256]{1,0:T(8,128)(2,1)S(1)} %get-tuple-element.170), channel_id=1, source_target_pairs={{4,0},{8,12},{5,1},{9,13},{6,2},{10,14},{7,3},{11,15},{20,16},{24,... | collective-permute-start | bytes 589832 | tf_op jit(solution)/shard_map/ppermute | solution.py:436
  206.0 9.7 %collective-permute-start.16 = (bf16[384,256]{1,0:T(8,128)(2,1)S(1)}, bf16[384,256]{1,0:T(8,128)(2,1)S(1)}, u32[]{:S(2)}, u32[]{:S(2)}) collective-permute-start(bf16[384,256]{1,0:T(8,128)(2,1)S(1)} %get-tuple-element.167), channel_id=1, source_target_pairs={{4,12},{8,0},{5,13},{9,1},{6,14},{10,2},{7,15},{11,3},{20,28},{24,... | collective-permute-start | bytes 589832 | tf_op jit(solution)/shard_map/ppermute | solution.py:454
  207.3 8.4 %collective-permute-start.17 = (bf16[256,256]{1,0:T(8,128)(2,1)S(1)}, bf16[256,256]{1,0:T(8,128)(2,1)S(1)}, u32[]{:S(2)}, u32[]{:S(2)}) collective-permute-start(bf16[256,256]{1,0:T(8,128)(2,1)S(1)} %get-tuple-element.168), channel_id=1, source_target_pairs={{4,3},{5,7},{6,11},{9,4},{10,8},{11,12},{20,19},{21,23},{22,27},{2... | collective-permute-start | bytes 393224 | tf_op jit(solution)/shard_map/ppermute | solution.py:455
  208.0 0.7 collective-permute-start.19
  (8 other events, 44.1 us)

commit v7 on v6

--- a/solution.py
+++ b/solution.py
@@ -106,7 +106,7 @@
             scratch_shapes=scratch,
         ),
         cost_estimate=pl.CostEstimate(flops=1, transcendentals=0, bytes_accessed=1),
-        compiler_params=pltpu.CompilerParams(vmem_limit_bytes=40 << 20),
+        compiler_params=pltpu.CompilerParams(vmem_limit_bytes=16 << 20),
         name=name,
     )(at, *operands)
 

time: 219 us -> 219 us (level)
  no operation moved by 1% of the time
where the time goes in v7:
time: 219 us; the launch traced here: 217 us
  waiting for transfers between devices  81.2 us (37%)
  starting transfers between devices  54.7 us (25%)
  Pallas kernels  39.8 us (18%)
  local copies, waits for them, and re-layouts  35.6 us (16%)
  other arithmetic  5.06 us (2%)
    pallas_call x12, Pallas kernels, call(): pl.pallas_call(kernel, out_shape=tuple((jax.ShapeDtypeStruct(o, t) for o,...  39.8 us
    ppermute x3, waiting for transfers between devices, send_far(): return (lax.ppermute(data, 'gx', FAR), *gate)  38.9 us
    unnamed x36, local copies, waits for them, and re-layouts  19.9 us
    ppermute x3, starting transfers between devices, send_far(): return (lax.ppermute(data, 'gx', FAR), *gate)  19.7 us
    ppermute x1, waiting for transfers between devices, meeting(): near[1] = lax.ppermute(own[1], 'gx', NEAR)  19.7 us
    ppermute x2, starting transfers between devices, meeting(): near_raw = [lax.ppermute(a, 'gx', NEAR) for a in own_raw]  10 us
    ppermute x2, waiting for transfers between devices, meeting(): core_got = lax.ppermute(core[1], 'gy', SWAP)  9.34 us
    ppermute x1, starting transfers between devices, meeting(): near[1] = lax.ppermute(own[1], 'gx', NEAR)  9.03 us
  transfers between devices with their start and end apart: 20, of which 9 were waited for; matrix products, arithmetic and copies ran while one was open for 14% of the time, Pallas kernels for 16%

profile of v7, /device:TPU:0, one launch (start us, length us, event | category | flops | bytes accessed | tf_op | source)
XLA Modules:
  0.0 217.4 jit_solution(6085928963611245504)
XLA Ops:
  0.7 3.1 %dynamic-slice_bitcast_fusion.3 = (bf16[128,8,512]{2,1,0:T(8,128)(2,1)}, bf16[128,8,512]{2,1,0:T(8,128)(2,1)}) fusion(bf16[256,4,8,512]{3,2,1,0:T(8,128)(2,1)} %param.3, s32[]{:T(128)S(6)} %select_n.48, s32[]{:T(128)S(6)} %select_n.47), kind=kLoop, calls=%fused_computation.6 | loop fusion | bytes 4194312 | tf_op jit(solution)/shard_map/reshape | solution.py:307
  5.4 7.8 %collective-permute-start.2 = (bf16[128,8,512]{2,1,0:T(8,128)(2,1)}, bf16[128,8,512]{2,1,0:T(8,128)(2,1)}, u32[]{:S(2)}, u32[]{:S(2)}) collective-permute-start(bf16[128,8,512]{2,1,0:T(8,128)(2,1)} %get-tuple-element.101), channel_id=1, source_target_pairs={{0,4},{12,8},{1,5},{13,9},{2,6},{14,10},{3,7},{15,11},{16,20},{28,... | collective-permute-start | bytes 3145736 | tf_op jit(solution)/shard_map/ppermute | solution.py:325
  13.1 3.1 %dynamic-slice_bitcast_fusion.1 = (bf16[128,8,512]{2,1,0:T(8,128)(2,1)}, bf16[128,8,512]{2,1,0:T(8,128)(2,1)}) fusion(bf16[256,4,8,512]{3,2,1,0:T(8,128)(2,1)} %param.3, s32[]{:T(128)S(6)} %select_n.48, s32[]{:T(128)S(6)} %select_n.47), kind=kLoop, calls=%fused_computation.4 | loop fusion | bytes 4194312 | tf_op jit(solution)/shard_map/reshape | solution.py:307
  17.8 2.3 %collective-permute-start.3 = (bf16[128,8,512]{2,1,0:T(8,128)(2,1)}, bf16[128,8,512]{2,1,0:T(8,128)(2,1)}, u32[]{:S(2)}, u32[]{:S(2)}) collective-permute-start(bf16[128,8,512]{2,1,0:T(8,128)(2,1)} %get-tuple-element.106), channel_id=1, source_target_pairs={{0,4},{12,8},{1,5},{13,9},{2,6},{14,10},{3,7},{15,11},{16,20},{28,... | collective-permute-start | bytes 3145736 | tf_op jit(solution)/shard_map/ppermute | solution.py:325
  29.3 9.0 %collective-permute-start.7 = (bf16[256,4096]{1,0:T(8,128)(2,1)S(1)}, bf16[256,4096]{1,0:T(8,128)(2,1)}, u32[]{:S(2)}, u32[]{:S(2)}) collective-permute-start(bf16[256,4096]{1,0:T(8,128)(2,1)S(1)} %bitcast.45), channel_id=1, source_target_pairs={{0,4},{12,8},{1,5},{13,9},{2,6},{14,10},{3,7},{15,11},{16,20},{28,... | collective-permute-start | bytes 6291464 | tf_op jit(solution)/shard_map/ppermute | solution.py:328
  39.6 2.5 %constant_dynamic-slice_fusion.5 = (bf16[256,1,8,512]{3,2,1,0:T(8,128)(2,1)S(1)}, bf16[256,1,8,512]{3,2,1,0:T(8,128)(2,1)S(1)}) fusion(bf16[256,4,8,512]{3,2,1,0:T(8,128)(2,1)} %param.3, s32[]{:T(128)S(6)} %select_n.48, s32[]{:T(128)S(6)} %select_n.47), kind=kLoop, calls=%fused_computation.14 | loop fusion | bytes 8388616 | tf_op jit(solution)/shard_map/dynamic_slice | solution.py:307
  42.1 2.3 %slice.10 = bf16[256,2048]{1,0:T(8,128)(2,1)} slice(bf16[256,4096]{1,0:T(8,128)(2,1)} %bitcast.22.other), slice={[0:256], [1024:3072]} | slice | bytes 2097152 | tf_op jit(solution)/shard_map/slice | solution.py:348
  44.4 2.3 %copy.16 = bf16[32,8,8,512]{3,1,2,0:T(8,128)(2,1)} copy(bf16[32,8,8,512]{3,2,1,0:T(8,128)(2,1)S(1)} %bitcast.55) | data formatting | bytes 4194304
  56.2 2.4 %collective-permute-done.3 = bf16[128,8,512]{2,1,0:T(8,128)(2,1)} collective-permute-done((bf16[128,8,512]{2,1,0:T(8,128)(2,1)}, bf16[128,8,512]{2,1,0:T(8,128)(2,1)}, u32[]{:S(2)}, u32[]{:S(2)}) %collective-permute-start.3) | collective-permute-done | bytes 1048608 | tf_op jit(solution)/shard_map/ppermute | solution.py:325
  61.7 9.8 %collective-permute-start.4 = (bf16[256,5120]{1,0:T(8,128)(2,1)}, bf16[256,5120]{1,0:T(8,128)(2,1)}, u32[]{:S(2)}, u32[]{:S(2)}) collective-permute-start(bf16[256,5120]{1,0:T(8,128)(2,1)} %pad_maximum_fusion), channel_id=1, source_target_pairs={{0,8},{12,4},{1,9},{13,5},{2,10},{14,6},{3,11},{15,7},{16,24},{28,... | collective-permute-start | bytes 7864328 | tf_op jit(solution)/shard_map/ppermute | solution.py:353
  78.0 5.7 %pairs.2.rest_0_ = f32[4,256,256]{2,1,0:T(8,128)S(1)} custom-call(s32[4]{0:T(128)S(1)} %pad_add_fusion.at, bf16[256,4096]{1,0:T(8,128)(2,1)S(1)} %copy-done.8, bf16[256,4096]{1,0:T(8,128)(2,1)S(1)} %bitcast.52, bf16[256,4096]{1,0:T(8,128)(2,1)S(1)} %copy-done.6, bf16[256,4096]{1,0:T(8,128)(2,1)S(1)} %bitcast.51), custom_call_target="tpu_custom_call" | custom-call | flops 1 | bytes 1 | tf_op jit(solution)/shard_map/pairs/pallas_call | solution.py:98
  83.7 19.7 %collective-permute-done.7.near = bf16[256,4096]{1,0:T(8,128)(2,1)} collective-permute-done((bf16[256,4096]{1,0:T(8,128)(2,1)S(1)}, bf16[256,4096]{1,0:T(8,128)(2,1)}, u32[]{:S(2)}, u32[]{:S(2)}) %collective-permute-start.7) | collective-permute-done | bytes 2097184 | tf_op jit(solution)/shard_map/ppermute | solution.py:328
  103.4 8.8 %pairs.3 = (f32[2,768,256]{2,1,0:T(8,128)S(1)}, f32[2,768,256]{2,1,0:T(8,128)S(1)}) custom-call(s32[4]{0:T(128)S(1)} %pad_add_fusion.at, bf16[256,4096]{1,0:T(8,128)(2,1)} %collective-permute-done.7.near, bf16[256,4096]{1,0:T(8,128)(2,1)S(1)} %bitcast.46, bf16[256,4096]{1,0:T(8,128)(2,1)} %collective-permute-done.6.cross, bf16[256,4096]{1,0:T(8,128)(2,1)} %bitcast.22.other, ...), custom_call_target="tpu_custom_call" | custom-call | flops 1 | bytes 1 | tf_op jit(solution)/shard_map/pairs/pallas_call | solution.py:98
  112.3 3.4 %collective-permute-done.9.got = f32[2,768,256]{2,1,0:T(8,128)S(1)} collective-permute-done((f32[2,768,256]{2,1,0:T(8,128)S(1)}, f32[2,768,256]{2,1,0:T(8,128)S(1)}, u32[]{:S(2)}, u32[]{:S(2)}) %collective-permute-start.9) | collective-permute-done | bytes 1572896 | tf_op jit(solution)/shard_map/ppermute | solution.py:391
  118.0 4.4 %collective-permute-start.8 = (bf16[256,2048]{1,0:T(8,128)(2,1)S(1)}, bf16[256,2048]{1,0:T(8,128)(2,1)S(1)}, u32[]{:S(2)}, u32[]{:S(2)}) collective-permute-start(bf16[256,2048]{1,0:T(8,128)(2,1)S(1)} %copy-done.10), channel_id=1, source_target_pairs={{0,8},{12,4},{1,9},{13,5},{2,10},{14,6},{3,11},{15,7},{16,24},{28,... | collective-permute-start | bytes 3145736 | tf_op jit(solution)/shard_map/ppermute | solution.py:353
  122.4 37.2 %collective-permute-done.4.far = bf16[256,5120]{1,0:T(8,128)(2,1)} collective-permute-done((bf16[256,5120]{1,0:T(8,128)(2,1)}, bf16[256,5120]{1,0:T(8,128)(2,1)}, u32[]{:S(2)}, u32[]{:S(2)}) %collective-permute-start.4) | collective-permute-done | bytes 2621472 | tf_op jit(solution)/shard_map/ppermute | solution.py:353
  159.6 5.5 %collective-permute-start.5 = (bf16[256,1024]{1,0:T(8,128)(2,1)S(1)}, bf16[256,1024]{1,0:T(8,128)(2,1)S(1)}, u32[]{:S(2)}, u32[]{:S(2)}) collective-permute-start(bf16[256,1024]{1,0:T(8,128)(2,1)S(1)} %get-tuple-element.112), channel_id=1, source_target_pairs={{0,8},{12,4},{1,9},{13,5},{2,10},{14,6},{3,11},{15,7},{16,24},{28,... | collective-permute-start | bytes 1572872 | tf_op jit(solution)/shard_map/ppermute | solution.py:353
  165.2 8.5 %meet.4 = (f32[3,256,256]{2,1,0:T(8,128)S(1)}, f32[4,16,1024]{2,1,0:T(8,128)S(1)}, f32[4,16,1024]{2,1,0:T(8,128)S(1)}) custom-call(s32[4]{0:T(128)S(1)} %pad_add_fusion.at, bf16[256,5120]{1,0:T(8,128)(2,1)} %collective-permute-done.4.far, bf16[256,4096]{1,0:T(8,128)(2,1)S(1)} %copy-done.9, bf16[256,4096]{1,0:T(8,128)(2,1)S(1)} %bitcast.53, ...), custom_call_target="tpu_custom_call" | custom-call | flops 1 | bytes 1 | tf_op jit(solution)/shard_map/meet/pallas_call | solution.py:98
  173.7 3.4 %meet.5 = (f32[3,256,256]{2,1,0:T(8,128)S(1)}, f32[4,16,1280]{2,1,0:T(8,128)S(1)}, f32[4,16,1280]{2,1,0:T(8,128)S(1)}) custom-call(s32[4]{0:T(128)S(1)} %pad_add_fusion.at, bf16[256,5120]{1,0:T(8,128)(2,1)} %collective-permute-done.4.far, bf16[256,4096]{1,0:T(8,128)(2,1)} %collective-permute-done.7.near, bf16[256,4096]{1,0:T(8,128)(2,1)S(1)} %bitcast.47, ...), custom_call_target="tpu_custom_call" | custom-call | flops 1 | bytes 1 | tf_op jit(solution)/shard_map/meet/pallas_call | solution.py:98
  178.6 5.6 %collective-permute-done.11.core_got = f32[4,16,1280]{2,1,0:T(8,128)S(1)} collective-permute-done((f32[4,16,1280]{2,1,0:T(8,128)S(1)}, f32[4,16,1280]{2,1,0:T(8,128)S(1)}, u32[]{:S(2)}, u32[]{:S(2)}) %collective-permute-start.11) | collective-permute-done | bytes 327712 | tf_op jit(solution)/shard_map/ppermute | solution.py:397
  184.9 5.2 %meet.6 = (f32[3,256,256]{2,1,0:T(8,128)S(1)}, f32[4,16,512]{2,1,0:T(8,128)S(1)}, f32[4,16,512]{2,1,0:T(8,128)S(1)}) custom-call(s32[4]{0:T(128)S(1)} %pad_add_fusion.at, bf16[256,2048]{1,0:T(8,128)(2,1)S(1)} %collective-permute-done.8.far, bf16[256,4096]{1,0:T(8,128)(2,1)} %collective-permute-done.7.near, bf16[256,4096]{1,0:T(8,128)(2,1)S(1)} %bitcast.48, ...), custom_call_target="tpu_custom_call" | custom-call | flops 1 | bytes 1 | tf_op jit(solution)/shard_map/meet/pallas_call | solution.py:98
  191.8 3.4 %meet.7 = (f32[2,256,256]{2,1,0:T(8,128)S(1)}, f32[2,256,256]{2,1,0:T(8,128)S(1)}, f32[4,16,768]{2,1,0:T(8,128)S(1)}, f32[4,16,768]{2,1,0:T(8,128)S(1)}) custom-call(s32[4]{0:T(128)S(1)} %pad_add_fusion.at, bf16[256,1024]{1,0:T(8,128)(2,1)S(1)} %collective-permute-done.5.far, bf16[256,4096]{1,0:T(8,128)(2,1)} %collective-permute-done.7.near, ...), custom_call_target="tpu_custom_call" | custom-call | flops 1 | bytes 1 | tf_op jit(solution)/shard_map/meet/pallas_call | solution.py:98
  199.3 3.7 %collective-permute-done.15.core_got.got = f32[4,16,768]{2,1,0:T(8,128)S(1)} collective-permute-done((f32[4,16,768]{2,1,0:T(8,128)S(1)}, f32[4,16,768]{2,1,0:T(8,128)S(1)}, u32[]{:S(2)}, u32[]{:S(2)}) %collective-permute-start.15) | collective-permute-done | bytes 196640 | tf_op jit(solution)/shard_map/ppermute | solution.py:416
  208.7 7.0 %collective-permute-done.18.near = bf16[384,256]{1,0:T(8,128)(2,1)S(1)} collective-permute-done((bf16[384,256]{1,0:T(8,128)(2,1)S(1)}, bf16[384,256]{1,0:T(8,128)(2,1)S(1)}, u32[]{:S(2)}, u32[]{:S(2)}) %collective-permute-start.18) | collective-permute-done | bytes 196640 | tf_op jit(solution)/shard_map/ppermute | solution.py:436
  (78 shorter events, 50.2 us)
Async XLA Ops:
  0.6 28.5 %copy-start = (bf16[1024,128]{1,0:T(8,128)(2,1)S(1)}, bf16[1024,128]{1,0:T(8,128)(2,1)}, u32[]{:S(2)}) copy-start(bf16[1024,128]{1,0:T(8,128)(2,1)} %param.5) | copy-start | bytes 786436
  3.7 25.5 %collective-permute-start = (bf16[128,8,512]{2,1,0:T(8,128)(2,1)}, bf16[128,8,512]{2,1,0:T(8,128)(2,1)}, u32[]{:S(2)}, u32[]{:S(2)}) collective-permute-start(bf16[128,8,512]{2,1,0:T(8,128)(2,1)} %get-tuple-element.92), channel_id=1, source_target_pairs={{4,8},{8,4},{5,9},{9,5},{6,10},{10,6},{7,11},{11,7},{20,24},{24,20... | collective-permute-start | bytes 3145736 | tf_op jit(solution)/shard_map/ppermute | solution.py:324
  5.4 46.0 %collective-permute-start.2 = (bf16[128,8,512]{2,1,0:T(8,128)(2,1)}, bf16[128,8,512]{2,1,0:T(8,128)(2,1)}, u32[]{:S(2)}, u32[]{:S(2)}) collective-permute-start(bf16[128,8,512]{2,1,0:T(8,128)(2,1)} %get-tuple-element.101), channel_id=1, source_target_pairs={{0,4},{12,8},{1,5},{13,9},{2,6},{14,10},{3,7},{15,11},{16,20},{28,... | collective-permute-start | bytes 3145736 | tf_op jit(solution)/shard_map/ppermute | solution.py:325
  16.2 33.6 %collective-permute-start.1 = (bf16[128,8,512]{2,1,0:T(8,128)(2,1)}, bf16[128,8,512]{2,1,0:T(8,128)(2,1)}, u32[]{:S(2)}, u32[]{:S(2)}) collective-permute-start(bf16[128,8,512]{2,1,0:T(8,128)(2,1)} %get-tuple-element.97), channel_id=1, source_target_pairs={{4,8},{8,4},{5,9},{9,5},{6,10},{10,6},{7,11},{11,7},{20,24},{24,20... | collective-permute-start | bytes 3145736 | tf_op jit(solution)/shard_map/ppermute | solution.py:324
  17.8 40.7 %collective-permute-start.3 = (bf16[128,8,512]{2,1,0:T(8,128)(2,1)}, bf16[128,8,512]{2,1,0:T(8,128)(2,1)}, u32[]{:S(2)}, u32[]{:S(2)}) collective-permute-start(bf16[128,8,512]{2,1,0:T(8,128)(2,1)} %get-tuple-element.106), channel_id=1, source_target_pairs={{0,4},{12,8},{1,5},{13,9},{2,6},{14,10},{3,7},{15,11},{16,20},{28,... | collective-permute-start | bytes 3145736 | tf_op jit(solution)/shard_map/ppermute | solution.py:325
  24.1 59.6 %collective-permute-start.6 = (bf16[256,4096]{1,0:T(8,128)(2,1)}, bf16[256,4096]{1,0:T(8,128)(2,1)}, u32[]{:S(2)}, u32[]{:S(2)}) collective-permute-start(bf16[256,4096]{1,0:T(8,128)(2,1)} %bitcast.22.other), channel_id=1, source_target_pairs={{4,8},{8,4},{5,9},{9,5},{6,10},{10,6},{7,11},{11,7},{20,24},{24,20... | collective-permute-start | bytes 6291464 | tf_op jit(solution)/shard_map/ppermute | solution.py:326
  29.3 74.1 %collective-permute-start.7 = (bf16[256,4096]{1,0:T(8,128)(2,1)S(1)}, bf16[256,4096]{1,0:T(8,128)(2,1)}, u32[]{:S(2)}, u32[]{:S(2)}) collective-permute-start(bf16[256,4096]{1,0:T(8,128)(2,1)S(1)} %bitcast.45), channel_id=1, source_target_pairs={{0,4},{12,8},{1,5},{13,9},{2,6},{14,10},{3,7},{15,11},{16,20},{28,... | collective-permute-start | bytes 6291464 | tf_op jit(solution)/shard_map/ppermute | solution.py:328
  61.7 97.9 %collective-permute-start.4 = (bf16[256,5120]{1,0:T(8,128)(2,1)}, bf16[256,5120]{1,0:T(8,128)(2,1)}, u32[]{:S(2)}, u32[]{:S(2)}) collective-permute-start(bf16[256,5120]{1,0:T(8,128)(2,1)} %pad_maximum_fusion), channel_id=1, source_target_pairs={{0,8},{12,4},{1,9},{13,5},{2,10},{14,6},{3,11},{15,7},{16,24},{28,... | collective-permute-start | bytes 7864328 | tf_op jit(solution)/shard_map/ppermute | solution.py:353
  103.4 61.8 %copy-start.7 = (bf16[256,4096]{1,0:T(8,128)(2,1)S(1)}, bf16[256,4096]{1,0:T(8,128)(2,1)}, u32[]{:S(2)}) copy-start(bf16[256,4096]{1,0:T(8,128)(2,1)} %pad_maximum_fusion.1.cross) | copy-start | bytes 6291460
  103.4 61.8 %copy-start.9 = (bf16[256,4096]{1,0:T(8,128)(2,1)S(1)}, bf16[256,4096]{1,0:T(8,128)(2,1)}, u32[]{:S(2)}) copy-start(bf16[256,4096]{1,0:T(8,128)(2,1)} %pad_maximum_fusion.2.near) | copy-start | bytes 6291460
  112.2 53.0 %copy-start.5 = (bf16[32,8,8,512]{3,1,2,0:T(8,128)(2,1)S(1)}, bf16[32,8,8,512]{3,1,2,0:T(8,128)(2,1)}, u32[]{:S(2)}) copy-start(bf16[32,8,8,512]{3,1,2,0:T(8,128)(2,1)} %copy.16) | copy-start | bytes 6291460
  112.2 3.5 %collective-permute-start.9 = (f32[2,768,256]{2,1,0:T(8,128)S(1)}, f32[2,768,256]{2,1,0:T(8,128)S(1)}, u32[]{:S(2)}, u32[]{:S(2)}) collective-permute-start(f32[2,768,256]{2,1,0:T(8,128)S(1)} %get-tuple-element.126), channel_id=1, source_target_pairs={{0,1},{1,0},{2,3},{3,2},{4,5},{5,4},{6,7},{7,6},{8,9},{9,8},{10,11... | collective-permute-start | bytes 4718600 | tf_op jit(solution)/shard_map/ppermute | solution.py:391
  116.4 48.7 %collective-permute-start.10 = (f32[768,256]{1,0:T(8,128)S(1)}, f32[768,256]{1,0:T(8,128)S(1)}, u32[]{:S(2)}, u32[]{:S(2)}) collective-permute-start(f32[768,256]{1,0:T(8,128)S(1)} %get-tuple-element.127), channel_id=1, source_target_pairs={{0,2},{2,0},{1,3},{3,1},{4,6},{6,4},{5,7},{7,5},{8,10},{10,8},{9,1... | collective-permute-start | bytes 2359304 | tf_op jit(solution)/shard_map/ppermute | solution.py:393
  118.0 66.9 %collective-permute-start.8 = (bf16[256,2048]{1,0:T(8,128)(2,1)S(1)}, bf16[256,2048]{1,0:T(8,128)(2,1)S(1)}, u32[]{:S(2)}, u32[]{:S(2)}) collective-permute-start(bf16[256,2048]{1,0:T(8,128)(2,1)S(1)} %copy-done.10), channel_id=1, source_target_pairs={{0,8},{12,4},{1,9},{13,5},{2,10},{14,6},{3,11},{15,7},{16,24},{28,... | collective-permute-start | bytes 3145736 | tf_op jit(solution)/shard_map/ppermute | solution.py:353
  159.6 32.1 %collective-permute-start.5 = (bf16[256,1024]{1,0:T(8,128)(2,1)S(1)}, bf16[256,1024]{1,0:T(8,128)(2,1)S(1)}, u32[]{:S(2)}, u32[]{:S(2)}) collective-permute-start(bf16[256,1024]{1,0:T(8,128)(2,1)S(1)} %get-tuple-element.112), channel_id=1, source_target_pairs={{0,8},{12,4},{1,9},{13,5},{2,10},{14,6},{3,11},{15,7},{16,24},{28,... | collective-permute-start | bytes 1572872 | tf_op jit(solution)/shard_map/ppermute | solution.py:353
  177.1 7.1 %collective-permute-start.11 = (f32[4,16,1280]{2,1,0:T(8,128)S(1)}, f32[4,16,1280]{2,1,0:T(8,128)S(1)}, u32[]{:S(2)}, u32[]{:S(2)}) collective-permute-start(f32[4,16,1280]{2,1,0:T(8,128)S(1)} %get-tuple-element.138), channel_id=1, source_target_pairs={{0,2},{2,0},{1,3},{3,1},{4,6},{6,4},{5,7},{7,5},{8,10},{10,8},{9,1... | collective-permute-start | bytes 983048 | tf_op jit(solution)/shard_map/ppermute | solution.py:397
  195.2 2.3 %collective-permute-start.12 = (f32[2,256,256]{2,1,0:T(8,128)S(1)}, f32[2,256,256]{2,1,0:T(8,128)S(1)}, u32[]{:S(2)}, u32[]{:S(2)}) collective-permute-start(f32[2,256,256]{2,1,0:T(8,128)S(1)} %get-tuple-element.159), channel_id=1, source_target_pairs={{0,1},{1,0},{2,3},{3,2},{4,5},{5,4},{6,7},{7,6},{8,9},{9,8},{10,11... | collective-permute-start | bytes 1572872 | tf_op jit(solution)/shard_map/ppermute | solution.py:421
  195.2 7.8 %collective-permute-start.15 = (f32[4,16,768]{2,1,0:T(8,128)S(1)}, f32[4,16,768]{2,1,0:T(8,128)S(1)}, u32[]{:S(2)}, u32[]{:S(2)}) collective-permute-start(f32[4,16,768]{2,1,0:T(8,128)S(1)} %get-tuple-element.165), channel_id=1, source_target_pairs={{0,2},{2,0},{1,3},{3,1},{4,6},{6,4},{5,7},{7,5},{8,10},{10,8},{9,1... | collective-permute-start | bytes 589832 | tf_op jit(solution)/shard_map/ppermute | solution.py:416
  196.8 8.1 %collective-permute-start.14 = (bf16[336,256]{1,0:T(8,128)(2,1)S(1)}, bf16[336,256]{1,0:T(8,128)(2,1)S(1)}, u32[]{:S(2)}, u32[]{:S(2)}) collective-permute-start(bf16[336,256]{1,0:T(8,128)(2,1)S(1)} %get-tuple-element.162), channel_id=1, source_target_pairs={{4,8},{8,4},{5,9},{9,5},{6,10},{10,6},{7,11},{11,7},{20,24},{24,20... | collective-permute-start | bytes 516104 | tf_op jit(solution)/shard_map/ppermute | solution.py:426
  198.1 7.3 %collective-permute-start.13 = (bf16[256,256]{1,0:T(8,128)(2,1)S(1)}, bf16[256,256]{1,0:T(8,128)(2,1)S(1)}, u32[]{:S(2)}, u32[]{:S(2)}) collective-permute-start(bf16[256,256]{1,0:T(8,128)(2,1)S(1)} %get-tuple-element.161), channel_id=1, source_target_pairs={{0,2},{2,0},{1,3},{3,1},{4,6},{6,4},{5,7},{7,5},{8,10},{10,8},{9,1... | collective-permute-start | bytes 393224 | tf_op jit(solution)/shard_map/ppermute | solution.py:435
  203.6 12.1 %collective-permute-start.18 = (bf16[384,256]{1,0:T(8,128)(2,1)S(1)}, bf16[384,256]{1,0:T(8,128)(2,1)S(1)}, u32[]{:S(2)}, u32[]{:S(2)}) collective-permute-start(bf16[384,256]{1,0:T(8,128)(2,1)S(1)} %get-tuple-element.170), channel_id=1, source_target_pairs={{4,0},{8,12},{5,1},{9,13},{6,2},{10,14},{7,3},{11,15},{20,16},{24,... | collective-permute-start | bytes 589832 | tf_op jit(solution)/shard_map/ppermute | solution.py:436
  206.0 9.7 %collective-permute-start.16 = (bf16[384,256]{1,0:T(8,128)(2,1)S(1)}, bf16[384,256]{1,0:T(8,128)(2,1)S(1)}, u32[]{:S(2)}, u32[]{:S(2)}) collective-permute-start(bf16[384,256]{1,0:T(8,128)(2,1)S(1)} %get-tuple-element.167), channel_id=1, source_target_pairs={{4,12},{8,0},{5,13},{9,1},{6,14},{10,2},{7,15},{11,3},{20,28},{24,... | collective-permute-start | bytes 589832 | tf_op jit(solution)/shard_map/ppermute | solution.py:454
  207.3 8.4 %collective-permute-start.17 = (bf16[256,256]{1,0:T(8,128)(2,1)S(1)}, bf16[256,256]{1,0:T(8,128)(2,1)S(1)}, u32[]{:S(2)}, u32[]{:S(2)}) collective-permute-start(bf16[256,256]{1,0:T(8,128)(2,1)S(1)} %get-tuple-element.168), channel_id=1, source_target_pairs={{4,3},{5,7},{6,11},{9,4},{10,8},{11,12},{20,19},{21,23},{22,27},{2... | collective-permute-start | bytes 393224 | tf_op jit(solution)/shard_map/ppermute | solution.py:455
  208.0 0.7 collective-permute-start.19
  (8 other events, 44.1 us)
